TPU v7x, 32 devices: a whole 2x2x4 slice. The times are simulated.
32 devices in a mesh: groups: 2 (over y), tensor: 4 (over z), seq: 2 (over core), dp: 2 (over x).
Axes of the slice: x: 2, y: 2, z: 4, core: 2. Of those that a mesh axis runs over, the one named last changes fastest.
Arguments:
- queries: bfloat16 [4, 512, 8192], P(('groups', 'dp'), 'seq', 'tensor'), parts along dimension 0, may hold values from -120 to 120
- stretch_keys: bfloat16 [4, 512, 4096], P(('groups', 'dp'), 'seq', 'tensor'), parts along dimension 0, may hold values from -5 to 5
- stretch_values: bfloat16 [4, 512, 4096], P(('groups', 'dp'), 'seq', 'tensor'), parts along dimension 0, may hold values from -96 to 96
- cache_keys: bfloat16 [4, 3584, 4096], P(('groups', 'dp'), 'seq', 'tensor'), parts along dimension 0, may hold values from -5 to 5
- cache_values: bfloat16 [4, 3584, 4096], P(('groups', 'dp'), 'seq', 'tensor'), parts along dimension 0, may hold values from -96 to 96
- blocks: bfloat16 [64, 32, 128, 128], P('tensor', 'dp'), may hold values from -0.09375 to 0.09375
- block_columns: int32 [64, 32], P('tensor', 'dp'), may hold values from 0 to 63, as said below
Outputs:
- projected: bfloat16 [4, 512, 8192], P(('groups', 'dp'), 'seq', 'tensor'), parts along dimension 0
There are 2 independent parts, one for each index of `groups`. A program takes and returns all parts, laid end to end along the dimension named above; an argument that names none is the same for every part. Nothing has to cross between parts.
Inputs may be any that keep to these rules, and one draw needn't show every extreme that they name: `block_columns`: each row of blocks lists 32 different column blocks.
All inputs are finite; a program needn't handle non-finite values.
Results may differ from a plain program's by a relative error of at most 0.02.
Values may be sent and summed in bfloat16 or wider, within the bound.
No kernel may reach another device: no remote copies, remote signals or barrier semaphores. Data moves between devices by JAX's collectives and lax.ppermute only.
A program may use at most 256 MiB of HBM per device.

v0:
```python
import jax
import jax.numpy as jnp
from jax import lax
from jax.sharding import PartitionSpec as P

D = 8192
HD = 128


floor_score = -1e30


def shards(queries, stretch_keys, stretch_values, cache_keys, cache_values, blocks, block_columns):
    seqs_dev, tok_rows, width_dev = queries.shape
    cache_rows = cache_keys.shape[1]
    key_heads = stretch_keys.shape[2] // HD
    context_span = cache_rows + tok_rows
    scale_factor = HD ** (-0.5)
    context_keys = jnp.concatenate([cache_keys, stretch_keys], axis=1)
    context_values = jnp.concatenate([cache_values, stretch_values], axis=1)
    my_seq = lax.axis_index("seq")
    query_heads = queries.reshape(seqs_dev, tok_rows, key_heads, 2, HD)
    query_pos = my_seq * tok_rows + jnp.arange(tok_rows)
    run_max = jnp.full((seqs_dev, tok_rows, key_heads, 2), floor_score, jnp.float32)
    key_piece = lax.all_gather(context_keys, "seq", axis=1, tiled=True)
    value_piece = lax.all_gather(context_values, "seq", axis=1, tiled=True)
    piece_len = key_piece.shape[1]
    key_index = jnp.arange(piece_len)
    owner_shard = key_index // context_span
    inside = key_index % context_span
    stretch_pos = owner_shard * tok_rows + inside - cache_rows
    visible = (inside[None, :] < cache_rows) | (stretch_pos[None, :] <= query_pos[:, None])
    keep_mask = visible[None, :, None, None, :]
    key_tiles = key_piece.reshape(seqs_dev, piece_len, key_heads, HD)
    scores = (
        jnp.einsum("stpgd,smpd->stpgm", query_heads, key_tiles, preferred_element_type=jnp.float32)
        * scale_factor
    )
    scores = jnp.where(keep_mask, scores, floor_score)
    new_max = jnp.maximum(run_max, jnp.max(scores, axis=-1))
    exp_terms = jnp.where(keep_mask, jnp.exp(scores - new_max[..., None]), 0.0)
    value_tiles = value_piece.reshape(seqs_dev, piece_len, key_heads, HD)
    added = jnp.einsum(
        "stpgm,smpd->stpgd",
        exp_terms.astype(jnp.bfloat16),
        value_tiles,
        preferred_element_type=jnp.float32,
    )
    run_total = jnp.sum(exp_terms, axis=-1)
    attended = added / run_total[..., None]
    attended = attended.reshape(seqs_dev * tok_rows, width_dev).astype(jnp.bfloat16)
    row_blocks = blocks.shape[0]
    block_size = blocks.shape[2]
    col_blocks = D // block_size
    empty_panel = jnp.zeros((row_blocks, block_size, col_blocks, block_size), jnp.bfloat16)
    block_piece = lax.all_gather(blocks, "dp", axis=1, tiled=True)
    column_piece = lax.all_gather(block_columns, "dp", axis=1, tiled=True)
    row_index = jnp.broadcast_to(jnp.arange(row_blocks)[:, None], column_piece.shape)
    dense_panel = empty_panel.at[row_index, :, column_piece, :].set(block_piece)
    partial_value = jnp.dot(
        attended,
        dense_panel.reshape(row_blocks * block_size, D),
        preferred_element_type=jnp.float32,
    )
    owned = lax.psum_scatter(
        partial_value.astype(jnp.bfloat16), "tensor", scatter_dimension=1, tiled=True
    )
    return owned.reshape(seqs_dev, tok_rows, width_dev)


def solution(mesh):
    placed = (
        P(("groups", "dp"), "seq", "tensor"),
        P(("groups", "dp"), "seq", "tensor"),
        P(("groups", "dp"), "seq", "tensor"),
        P(("groups", "dp"), "seq", "tensor"),
        P(("groups", "dp"), "seq", "tensor"),
        P("tensor", "dp", None, None),
        P("tensor", "dp"),
    )
    return jax.shard_map(
        shards,
        mesh=mesh,
        in_specs=placed,
        out_specs=P(("groups", "dp"), "seq", "tensor"),
        check_vma=False,
    )
```

profile of v0, /device:TPU:0, one launch (start us, length us, event | category | flops | bytes accessed | tf_op | source)
XLA Modules:
  0.0 490.6 jit_solution(9540752144256479252)
XLA Ops:
  6.5 0.0 all-gather.4.cloned.1.call-start
  6.5 4.6 pad_maximum_fusion
  11.2 0.0 all-gather.4.cloned.1.call-update
  11.2 0.0 copy-start.2
  11.2 0.0 all-gather.6.cloned.1.call-start
  11.3 6.0 %copy.27 = bf16[1,1792,1024]{1,2,0:T(8,128)(2,1)} copy(bf16[1,1792,1024]{2,1,0:T(8,128)(2,1)} %param.10) | data formatting | bytes 7340032 | tf_op args[3]
  17.3 0.0 copy-done.1
  17.3 0.2 copy.28
  17.5 4.8 pad_maximum_fusion.1
  22.3 0.0 all-gather.6.cloned.1.call-update
  22.3 0.0 all-gather.8.cloned.1.call-start
  22.3 0.7 all-gather.8.cloned.1.call-update
  23.0 0.0 reduce-scatter.2.cloned.1.call-start
  23.1 0.8 reshape.133
  23.9 0.1 copy.32
  23.9 5.8 %all_gather.14 = s32[16,32]{0,1:T(8,128)S(1)} all-gather(s32[16,16]{0,1:T(8,128)S(1)} %copy.32), channel_id=1, replica_groups=mesh['groups'=2,'tensor'=4,'seq'=2,'dp'=2] {'dp'}, dimensions={1}, use_global_device_ids=true | all-gather | bytes 3072 | tf_op jit(solution)/shard_map/all_gather | solution.py:57
  29.7 0.1 copy.33
  29.8 0.1 reshape.137
  29.9 3.0 compare_or_fusion
  32.9 1.0 all-gather.4.cloned.1.call-done
  33.9 11.7 %copy.26 = bf16[1,4096,1024]{1,2,0:T(8,128)(2,1)} copy(bf16[1,4096,1024]{2,1,0:T(8,128)(2,1)} %all-gather.4.cloned.1.call-done) | data formatting | bytes 16777216 | tf_op jit(solution)/shard_map/all_gather | solution.py:26
  45.6 10.9 %all-gather.6.cloned.1.call-done = bf16[1,4096,1024]{1,2,0:T(8,128)(2,1)} async-done(((bf16[1,2048,1024]{1,2,0:T(8,128)(2,1)}), bf16[1,4096,1024]{1,2,0:T(8,128)(2,1)}) %all-gather.6.cloned.1.call-update) | async-done | bytes 8388624 | tf_op jit(solution)/shard_map/all_gather | solution.py:25
  56.5 36.0 %fusion = (f32[256,8,2]{0,2,1:T(2,128)S(1)}, f32[8,4096,256,2]{2,1,3,0:T(8,128)}) fusion(pred[256,4096]{0,1:T(8,128)(4,1)S(1)} %compare_or_fusion, bf16[4096,8,128,1]{0,2,3,1:T(8,128)(2,1)} %bitcast.59, bf16[256,8,2,128]{3,2,1,0:T(2,128)(2,1)S(1)} %reshape.133), kind=kOutput, calls=%fused_computation.3 | convolution fusion | flops 4345294848 | bytes 77611008 | tf_op jit(solution)/shard_map/stpgd,smpd->stpgm/dot_general | solution.py:36
  92.5 21.7 %fusion.1 = f32[256,8,2]{0,2,1:T(2,128)S(1)} fusion(f32[8,4096,256,2]{2,1,3,0:T(8,128)} %get-tuple-element.6, f32[256,8,2]{0,2,1:T(2,128)S(1)} %broadcast_maximum_fusion, pred[256,4096]{0,1:T(8,128)(4,1)S(1)} %compare_or_fusion), kind=kLoop, calls=%fused_computation.4 | loop fusion | flops 83881984 | bytes 68190208 | tf_op jit(solution)/shard_map/reduce_sum | solution.py:49
  114.2 27.3 %fusion.13 = bf16[1,256,8,2,128]{1,4,3,2,0:T(8,128)(2,1)S(1)} fusion(bf16[4096,8,128,1]{0,2,3,1:T(8,128)(2,1)} %bitcast.60, f32[8,4096,256,2]{2,1,3,0:T(8,128)} %get-tuple-element.6, f32[256,8,2]{0,2,1:T(2,128)S(1)} %broadcast_maximum_fusion, pred[256,4096]{0,1:T(8,128)(4,1)S(1)} %compare_or_fusion, f32[256,8,2]{0,2,1:T(2,128)S(1)} %fusion.1), kind=kOutput, calls=%fused_computation.17 | convolution fusion | flops 4379901952 | bytes 77627392 | tf_op jit(solution)/shard_map/stpgm,smpd->stpgd/dot_general | solution.py:43
  141.5 116.7 %all-gather.8.cloned.1.call-done = bf16[16,32,128,128]{3,2,1,0:T(8,128)(2,1)} async-done(((bf16[16,16,128,128]{3,2,1,0:T(8,128)(2,1)}), bf16[16,32,128,128]{3,2,1,0:T(8,128)(2,1)}) %all-gather.8.cloned.1.call-update) | async-done | bytes 16777232 | tf_op jit(solution)/shard_map/all_gather | solution.py:56
  258.2 11.2 %broadcast_in_dim.44 = bf16[16,128,64,128]{3,1,2,0:T(8,128)(2,1)} broadcast(bf16[]{:T(256)} %constant.57.clone.1), dimensions={} | broadcast | bytes 33554432 | tf_op jit(solution)/shard_map/broadcast_in_dim | solution.py:55
  269.4 79.4 %scatter_fusion = bf16[16,128,64,128]{3,1,2,0:T(8,128)(2,1)} fusion(bf16[16,128,64,128]{3,1,2,0:T(8,128)(2,1)} %broadcast_in_dim.44, s32[512]{0:T(512)S(1)} %reshape.137, bf16[512,128,128]{2,1,0:T(8,128)(2,1)} %bitcast.58), kind=kCustom, calls=%fused_computation | custom fusion | bytes 50335744 | tf_op jit(solution)/shard_map/scatter | solution.py:59
  348.8 29.2 %copy.34 = bf16[16,128,64,128]{3,2,1,0:T(8,128)(2,1)} copy(bf16[16,128,64,128]{3,1,2,0:T(8,128)(2,1)} %scatter_fusion) | data formatting | bytes 67108864 | tf_op jit(solution)/shard_map/scatter | solution.py:59
  378.0 29.0 %fusion.10 = bf16[256,8192]{1,0:T(8,128)(2,1)} fusion(bf16[256,2048]{0,1:T(8,128)(2,1)S(1)} %bitcast.61, bf16[256,8,64,128]{3,2,1,0:T(8,128)(2,1)} %bitcast.57), kind=kOutput, calls=%fused_computation.12 | convolution fusion | flops 8592031744 | bytes 38797312 | tf_op jit(solution)/shard_map/dot_general | solution.py:60
  407.0 0.0 reduce-scatter.2.cloned.1.call-update
  407.1 77.0 %reduce-scatter.2.cloned.1.call-done = bf16[256,2048]{1,0:T(8,128)(2,1)} async-done(((bf16[256,8192]{1,0:T(8,128)(2,1)}), bf16[256,2048]{1,0:T(8,128)(2,1)}) %reduce-scatter.2.cloned.1.call-update) | async-done | bytes 1048592 | tf_op jit(solution)/shard_map/reduce_scatter | solution.py:65
  (9 shorter events, 0.0 us)
Async XLA Ops:
  6.5 10.8 %copy-start.1 = (bf16[1,256,1024]{2,1,0:T(8,128)(2,1)S(1)}, bf16[1,256,1024]{2,1,0:T(8,128)(2,1)}, u32[]{:S(2)}) copy-start(bf16[1,256,1024]{2,1,0:T(8,128)(2,1)} %param.8) | copy-start | bytes 1572868
  6.5 27.4 %all-gather.4.cloned.1.call-start = ((), (), s32[]{:S(2)}) async-start(), calls=%async_computation.1 | async-start | bytes 12582912 | tf_op jit(solution)/shard_map/all_gather | solution.py:26
  11.2 11.9 %copy-start = (bf16[1,256,2048]{2,1,0:T(8,128)(2,1)S(1)}, bf16[1,256,2048]{2,1,0:T(8,128)(2,1)}, u32[]{:S(2)}) copy-start(bf16[1,256,2048]{2,1,0:T(8,128)(2,1)} %param.7) | copy-start | bytes 3145732
  11.2 12.7 %copy-start.2 = (s32[16,16]{1,0:T(8,128)S(1)}, s32[16,16]{1,0:T(8,128)}, u32[]{:S(2)}) copy-start(s32[16,16]{1,0:T(8,128)} %param.13) | copy-start | bytes 3076
  11.2 45.3 %all-gather.6.cloned.1.call-start = ((), (), s32[]{:S(2)}) async-start(), calls=%async_computation.2 | async-start | bytes 12582912 | tf_op jit(solution)/shard_map/all_gather | solution.py:25
  22.3 235.9 %all-gather.8.cloned.1.call-start = ((), (), s32[]{:S(2)}) async-start(), calls=%async_computation.3 | async-start | bytes 25165824 | tf_op jit(solution)/shard_map/all_gather | solution.py:56
  23.0 461.0 %reduce-scatter.2.cloned.1.call-start = ((), (), s32[]{:S(2)}) async-start(), calls=%async_computation.4 | async-start | bytes 5242880 | tf_op jit(solution)/shard_map/reduce_scatter | solution.py:65
Sparse Core Ops, SparseCore 0:
  11.3 22.5 all-gather.3
  35.5 21.0 all-gather.5
  58.1 200.0 all-gather.7
  407.2 76.8 reduce-scatter.1
where the time goes:
time: 492 us; the launch traced here: 491 us
  waiting for transfers between devices  206 us (42%)
  local copies, waits for them, and re-layouts  139 us (28%)
  matrix products  92.2 us (19%)
  other arithmetic  34.1 us (7%)
  between operations  13.2 us (3%)
  blocking collectives  5.77 us (1%)
    all_gather x1, waiting for transfers between devices, shards(): block_piece = lax.all_gather(blocks, 'dp', axis=1, tiled=True)  117 us
    scatter x2, local copies, waits for them, and re-layouts, shards(): dense_panel = empty_panel.at[row_index, :, column_piece, :].set(block_piece)  109 us
    reduce_scatter x1, waiting for transfers between devices, shards(): lax.psum_scatter(partial_value.astype(jnp.bfloat16), 'tensor', scatter_di...  77 us
    dot_general x1, matrix products, shards(): jnp.einsum('stpgd,smpd->stpgm', query_heads, key_tiles, preferred_element...  36 us
    dot_general x1, matrix products, shards(): jnp.dot(attended, dense_panel.reshape(row_blocks * block_size, D), prefer...  29 us
    dot_general x1, matrix products, shards(): jnp.einsum('stpgm,smpd->stpgd', exp_terms.astype(jnp.bfloat16), value_til...  27.3 us
    reduce_sum x1, other arithmetic, shards(): run_total = jnp.sum(exp_terms, axis=-1)  21.7 us
    all_gather x1, local copies, waits for them, and re-layouts, shards(): value_piece = lax.all_gather(context_values, 'seq', axis=1, tiled=True)  11.7 us
  transfers between devices with their start and end apart: 4, of which 4 were waited for; matrix products, arithmetic and copies ran while one was open for 23% of the time, Pallas kernels for 0%

commit v1 on v0

v1 whole, which is shorter than its diff:
```python
import functools
import math

import jax
import jax.numpy as jnp
from jax import lax
from jax.experimental import pallas as pl
from jax.experimental.pallas import tpu as pltpu
from jax.sharding import PartitionSpec as P

HD = 128
FLOOR = -1e30
TILE = 1024


def attention_body(seq_ref, q_ref, cka_ref, ska_ref, ckb_ref, skb_ref, cva_ref, sva_ref, cvb_ref, svb_ref, out_ref):
    rows = q_ref.shape[0]
    scale = HD ** (-0.5) * math.log2(math.e)
    q = q_ref[...].astype(jnp.float32) * scale
    q_hi = q.astype(jnp.bfloat16)
    q_lo = (q - q_hi.astype(jnp.float32)).astype(jnp.bfloat16)
    q_two = jnp.concatenate(
        [jnp.concatenate([q_hi[:, h * HD : (h + 1) * HD], q_lo[:, h * HD : (h + 1) * HD]], axis=1) for h in range(2)],
        axis=0,
    )
    tiles = []
    for side, (ck, sk, cv, sv) in enumerate(
        ((cka_ref, ska_ref, cva_ref, sva_ref), (ckb_ref, skb_ref, cvb_ref, svb_ref))
    ):
        cache_rows = ck.shape[0]
        whole = cache_rows // TILE
        for t in range(whole):
            tiles.append((ck[t * TILE : (t + 1) * TILE, :], cv[t * TILE : (t + 1) * TILE, :], None))
        tiles.append(
            (
                jnp.concatenate([ck[whole * TILE :, :], sk[...]], axis=0),
                jnp.concatenate([cv[whole * TILE :, :], sv[...]], axis=0),
                side,
            )
        )
    peak = None
    acc = None
    for keys, values, side in tiles:
        scores = lax.dot_general(
            q_two,
            jnp.concatenate([keys, keys], axis=1),
            (((1,), (1,)), ((), ())),
            preferred_element_type=jnp.float32,
        )
        if side is not None:
            plain = scores.shape[1] - rows
            tail = scores[:, plain:]
            if side == 0:
                token = lax.broadcasted_iota(jnp.int32, (rows, rows), 0)
                position = lax.broadcasted_iota(jnp.int32, (rows, rows), 1)
                seen = position <= token
                seen = jnp.concatenate([seen, seen], axis=0)
                tail = jnp.where(seen, tail, FLOOR)
            else:
                tail = jnp.where(seq_ref[0] > 0, tail, FLOOR)
            scores = jnp.concatenate([scores[:, :plain], tail], axis=1)
        tile_peak = jnp.max(scores, axis=1, keepdims=True)
        new_peak = tile_peak if peak is None else jnp.maximum(peak, tile_peak)
        expo = jnp.exp2(scores - new_peak).astype(jnp.bfloat16)
        added = jnp.dot(
            expo,
            jnp.concatenate([values, jnp.ones_like(values)], axis=1),
            preferred_element_type=jnp.float32,
        )
        acc = added if acc is None else acc * jnp.exp2(peak - new_peak) + added
        peak = new_peak
    result = acc[:, :HD] / acc[:, HD:]
    out_ref[:, :HD] = result[:rows].astype(out_ref.dtype)
    out_ref[:, HD:] = result[rows:].astype(out_ref.dtype)


def attention(my_seq, q, own, peer):
    rows, width = q.shape
    cache_rows = own[0].shape[0]
    heads = width // (2 * HD)
    qspec = pl.BlockSpec((rows, 2 * HD), lambda g, s: (0, g))
    cspec = pl.BlockSpec((cache_rows, HD), lambda g, s: (0, g))
    nspec = pl.BlockSpec((rows, HD), lambda g, s: (0, g))
    total = 2 * (cache_rows + rows)
    return pl.pallas_call(
        attention_body,
        out_shape=jax.ShapeDtypeStruct((rows, width), jnp.bfloat16),
        grid_spec=pltpu.PrefetchScalarGridSpec(
            num_scalar_prefetch=1,
            grid=(heads,),
            in_specs=[qspec, cspec, nspec, cspec, nspec, cspec, nspec, cspec, nspec],
            out_specs=qspec,
        ),
        compiler_params=pltpu.CompilerParams(
            dimension_semantics=("arbitrary",), vmem_limit_bytes=56 << 20
        ),
        cost_estimate=pl.CostEstimate(
            flops=8 * heads * rows * total * HD,
            transcendentals=2 * heads * rows * total,
            bytes_accessed=4 * (total * heads * HD + rows * width),
        ),
        name="attention",
    )(my_seq, q, own[0], own[1], peer[0], peer[1], own[2], own[3], peer[2], peer[3])


def projection_body(n_pieces, step_cols, table_ref, start_ref, x_ref, *refs):
    pieces = refs[:n_pieces]
    out_ref, held, sems = refs[n_pieces:]
    rows = x_ref.shape[1] // HD
    offset = 0
    copies = []
    for i, piece in enumerate(pieces):
        count = piece.shape[0]
        copies.append(
            pltpu.make_async_copy(piece, held.at[pl.ds(start_ref[i], count)], sems.at[i])
        )
        offset += count

    @pl.when(pl.program_id(0) == 0)
    def _():
        for copy in copies:
            copy.start()
        held[offset] = jnp.zeros(held.shape[1:], held.dtype)
        for copy in copies:
            copy.wait()

    base = pl.program_id(0) * step_cols
    x = x_ref[...]
    for pair in range(step_cols // 2):
        sides = []
        for side in range(2):
            col = base + 2 * pair + side
            sides.append(jnp.concatenate([held[table_ref[r, col]] for r in range(rows)], axis=0))
        panel = jnp.concatenate(sides, axis=1)
        value = jnp.dot(x, panel, preferred_element_type=jnp.float32)
        out_ref[:, 2 * pair * HD : 2 * (pair + 1) * HD] = value.astype(out_ref.dtype)


def projection(x, table, starts, pieces, col_blocks):
    tokens, width = x.shape
    step_cols = 8
    total = sum(p.shape[0] for p in pieces)
    return pl.pallas_call(
        functools.partial(projection_body, len(pieces), step_cols),
        out_shape=jax.ShapeDtypeStruct((tokens, col_blocks * HD), jnp.bfloat16),
        grid_spec=pltpu.PrefetchScalarGridSpec(
            num_scalar_prefetch=2,
            grid=(col_blocks // step_cols,),
            in_specs=[pl.BlockSpec((tokens, width), lambda n, t, s: (0, 0))]
            + [pl.BlockSpec(memory_space=pl.ANY)] * len(pieces),
            out_specs=pl.BlockSpec((tokens, step_cols * HD), lambda n, t, s: (0, n)),
            scratch_shapes=[
                pltpu.VMEM((total + 1, HD, HD), jnp.bfloat16),
                pltpu.SemaphoreType.DMA((len(pieces),)),
            ],
        ),
        compiler_params=pltpu.CompilerParams(
            dimension_semantics=("arbitrary",), vmem_limit_bytes=56 << 20
        ),
        cost_estimate=pl.CostEstimate(
            flops=2 * tokens * width * col_blocks * HD,
            transcendentals=0,
            bytes_accessed=2 * (total * HD * HD + tokens * width + tokens * col_blocks * HD),
        ),
        name="projection",
    )(table, starts, x, *pieces)


def swap(value, axis):
    return lax.ppermute(value, axis, [(0, 1), (1, 0)])


def shards(mesh, queries, stretch_keys, stretch_values, cache_keys, cache_values, blocks, block_columns):
    tok_rows, width_dev = queries.shape[1:]
    row_blocks, kept, block_size = blocks.shape[:3]
    col_blocks = mesh.shape["tensor"] * width_dev // block_size
    my_seq = lax.axis_index("seq")

    if mesh.shape["dp"] == 2 and mesh.shape["groups"] == 2 and row_blocks % 4 == 0:
        quarter_rows = row_blocks // 4
        groups = lax.axis_index("groups")
        quarter = 2 * my_seq + groups
        quarter_of = lambda s, g: (2 * s + g) * quarter_rows * kept
        mine = lax.dynamic_slice_in_dim(blocks, quarter * quarter_rows, quarter_rows, 0)
        mine = mine.reshape(quarter_rows * kept, block_size, block_size)
        step = quarter_rows * kept // 4
        from_x = [swap(mine[i * step : (i + 1) * step], "dp") for i in range(4)]
        from_y = [swap(part, "groups") for part in from_x]
        from_core = [swap(part, "seq") for part in from_x + from_y]
        pieces = [blocks.reshape(row_blocks * kept, block_size, block_size)] + from_x + from_y + from_core
        first = row_blocks * kept
        starts = [0]
        for s, g in ((my_seq, groups), (my_seq, 1 - groups), (1 - my_seq, groups), (1 - my_seq, 1 - groups)):
            starts += [first + quarter_of(s, g) + i * step for i in range(4)]
        all_columns = jnp.stack([block_columns, swap(block_columns, "dp")])
    else:
        gathered = lax.all_gather(blocks, "dp", axis=0)
        pieces = [gathered.reshape(-1, block_size, block_size)]
        starts = [0]
        all_columns = lax.all_gather(block_columns, "dp", axis=0)
    starts = jnp.stack([jnp.int32(s) for s in starts])
    held = all_columns.size
    place = jnp.arange(held, dtype=jnp.int32).reshape(all_columns.shape)
    match = all_columns[..., None] == jnp.arange(col_blocks, dtype=jnp.int32)
    table = jnp.min(jnp.where(match, place[..., None], held), axis=(0, 2))

    own = [a[0] for a in (cache_keys, stretch_keys, cache_values, stretch_values)]
    peer = [swap(a, "seq") for a in own]
    attended = attention(my_seq.reshape(1), queries[0], own, peer)
    partial_value = projection(attended, table, starts, pieces, col_blocks)
    owned = lax.psum_scatter(partial_value, "tensor", scatter_dimension=1, tiled=True)
    return owned[None]


def solution(mesh):
    token = P(("groups", "dp"), "seq", "tensor")
    placed = (token, token, token, token, token, P("tensor", "dp", None, None), P("tensor", "dp"))
    return jax.shard_map(
        functools.partial(shards, mesh),
        mesh=mesh,
        in_specs=placed,
        out_specs=token,
        check_vma=False,
    )
```

time: 492 us -> 219 us (0.45)
  local copies, waits for them, and re-layouts: 139 us -> 4.59 us
  matrix products: 92.2 us -> 0 us
  waiting for transfers between devices: 206 us -> 135 us
  Pallas kernels: 0 us -> 45.8 us
  other arithmetic: 34.1 us -> 0.82 us
  starting transfers between devices: 0.12 us -> 19.6 us
  blocking collectives: 5.77 us -> 0 us
    all_gather x3 -> x0, waiting for transfers between devices: 129 us -> none  [the longest x1 117 us: shards(): block_piece = lax.all_gather(blocks, 'dp', axis=1, tiled=True)]
    scatter x2 -> x0, local copies, waits for them, and re-layouts: 109 us -> none  [shards(): dense_panel = empty_panel.at[row_index, :, column_piece, :].set(block_piece)]
    dot_general x3 -> x0, matrix products: 92.2 us -> none  [the longest x1 36 us: shards(): jnp.einsum('stpgd,smpd->stpgm', query_heads, key_tiles, preferred_element...]
    ppermute x0 -> x21, waiting for transfers between devices: none -> 58.1 us  [swap(): return lax.ppermute(value, axis, [(0, 1), (1, 0)])]
    pallas_call x0 -> x2, Pallas kernels: none -> 45.8 us  [the longest x1 26.9 us: attention(): pl.pallas_call(attention_body, out_shape=jax.ShapeDtypeStruct((rows, widt...]
    reduce_sum x1 -> x0, other arithmetic: 21.7 us -> none  [shards(): run_total = jnp.sum(exp_terms, axis=-1)]
    ppermute x0 -> x21, starting transfers between devices: none -> 19.6 us  [swap(): return lax.ppermute(value, axis, [(0, 1), (1, 0)])]
    all_gather x1 -> x0, local copies, waits for them, and re-layouts: 11.7 us -> none  [shards(): value_piece = lax.all_gather(context_values, 'seq', axis=1, tiled=True)]
  transfers between devices with their start and end apart: 4 -> 22, of which waited for: 4 -> 8; matrix products, arithmetic and copies ran while one was open for 23% -> 1% of each run, Pallas kernels for 0% -> 12%
where the time goes in v1:
time: 219 us
  waiting for transfers between devices  135 us (62%)
  Pallas kernels  45.8 us (21%)
  starting transfers between devices  19.6 us (9%)
  between operations  13.6 us (6%)
  local copies, waits for them, and re-layouts  4.59 us (2%)
    reduce_scatter x1, waiting for transfers between devices, shards(): lax.psum_scatter(partial_value, 'tensor', scatter_dimension=1, tiled=True)  76.8 us
    ppermute x21, waiting for transfers between devices, swap(): return lax.ppermute(value, axis, [(0, 1), (1, 0)])  58.1 us
    pallas_call x1, Pallas kernels, attention(): pl.pallas_call(attention_body, out_shape=jax.ShapeDtypeStruct((rows, widt...  26.9 us
    ppermute x21, starting transfers between devices, swap(): return lax.ppermute(value, axis, [(0, 1), (1, 0)])  19.6 us
    pallas_call x1, Pallas kernels, projection(): pl.pallas_call(functools.partial(projection_body, len(pieces), step_cols)...  18.9 us
  transfers between devices with their start and end apart: 22, of which 8 were waited for; matrix products, arithmetic and copies ran while one was open for 1% of the time, Pallas kernels for 12%

profile of v1, /device:TPU:0, one launch (start us, length us, event | category | flops | bytes accessed | tf_op | source)
XLA Modules:
  0.0 219.2 jit_solution(5172207819921903642)
XLA Ops:
  6.5 0.5 collective-permute-start.1
  7.1 0.5 collective-permute-start.2
  7.5 2.5 %collective-permute-start = (s32[16,16]{1,0:T(8,128)}, s32[16,16]{1,0:T(8,128)S(1)}, u32[]{:S(2)}, u32[]{:S(2)}) collective-permute-start(s32[16,16]{1,0:T(8,128)} %param.13), channel_id=1, source_target_pairs={{0,1},{1,0},{2,3},{3,2},{4,5},{5,4},{6,7},{7,6},{8,9},{9,8},{10,11... | collective-permute-start | bytes 3080 | tf_op jit(solution)/shard_map/ppermute | solution.py:170
  10.0 0.2 collective-permute-start.4
  10.2 1.7 dynamic-slice_bitcast_fusion
  11.9 2.0 collective-permute-start.5
  13.9 0.7 collective-permute-done.2.skb_ref
  14.6 2.9 %collective-permute-start.6 = (bf16[16,128,128]{2,1,0:T(8,128)(2,1)S(1)}, bf16[16,128,128]{2,1,0:T(8,128)(2,1)S(1)}, u32[]{:S(2)}, u32[]{:S(2)}) collective-permute-start(bf16[16,128,128]{2,1,0:T(8,128)(2,1)S(1)} %get-tuple-element.7), channel_id=1, source_target_pairs={{0,1},{1,0},{2,3},{3,2},{4,5},{5,4},{6,7},{7,6},{8,9},{9,8},{10,11... | collective-permute-start | bytes 1572872 | tf_op jit(solution)/shard_map/ppermute | solution.py:170
  17.5 1.5 collective-permute-start.7
  19.0 7.7 %collective-permute-done.5.refs_1_ = bf16[16,128,128]{2,1,0:T(8,128)(2,1)S(1)} collective-permute-done((bf16[16,128,128]{2,1,0:T(8,128)(2,1)S(1)}, bf16[16,128,128]{2,1,0:T(8,128)(2,1)S(1)}, u32[]{:S(2)}, u32[]{:S(2)}) %collective-permute-start.5) | collective-permute-done | bytes 524320 | tf_op jit(solution)/shard_map/ppermute | solution.py:170
  26.7 2.0 collective-permute-start.8
  28.7 9.2 %collective-permute-done.6.refs_2_ = bf16[16,128,128]{2,1,0:T(8,128)(2,1)S(1)} collective-permute-done((bf16[16,128,128]{2,1,0:T(8,128)(2,1)S(1)}, bf16[16,128,128]{2,1,0:T(8,128)(2,1)S(1)}, u32[]{:S(2)}, u32[]{:S(2)}) %collective-permute-start.6) | collective-permute-done | bytes 524320 | tf_op jit(solution)/shard_map/ppermute | solution.py:170
  37.9 2.0 collective-permute-start.9
  39.9 9.2 %collective-permute-done.7.refs_3_ = bf16[16,128,128]{2,1,0:T(8,128)(2,1)S(1)} collective-permute-done((bf16[16,128,128]{2,1,0:T(8,128)(2,1)S(1)}, bf16[16,128,128]{2,1,0:T(8,128)(2,1)S(1)}, u32[]{:S(2)}, u32[]{:S(2)}) %collective-permute-start.7) | collective-permute-done | bytes 524320 | tf_op jit(solution)/shard_map/ppermute | solution.py:170
  49.2 2.0 collective-permute-start.10
  51.2 8.6 %collective-permute-done.8.refs_4_ = bf16[16,128,128]{2,1,0:T(8,128)(2,1)S(1)} collective-permute-done((bf16[16,128,128]{2,1,0:T(8,128)(2,1)S(1)}, bf16[16,128,128]{2,1,0:T(8,128)(2,1)S(1)}, u32[]{:S(2)}, u32[]{:S(2)}) %collective-permute-start.8) | collective-permute-done | bytes 524320 | tf_op jit(solution)/shard_map/ppermute | solution.py:170
  59.8 1.5 collective-permute-start.11
  61.3 0.5 collective-permute-start.12
  61.8 12.8 %collective-permute-done.11.refs_7_ = bf16[16,128,128]{2,1,0:T(8,128)(2,1)S(1)} collective-permute-done((bf16[16,128,128]{2,1,0:T(8,128)(2,1)S(1)}, bf16[16,128,128]{2,1,0:T(8,128)(2,1)S(1)}, u32[]{:S(2)}, u32[]{:S(2)}) %collective-permute-start.11) | collective-permute-done | bytes 524320 | tf_op jit(solution)/shard_map/ppermute | solution.py:170
  74.6 9.7 %collective-permute-done.12.refs_8_ = bf16[16,128,128]{2,1,0:T(8,128)(2,1)S(1)} collective-permute-done((bf16[16,128,128]{2,1,0:T(8,128)(2,1)S(1)}, bf16[16,128,128]{2,1,0:T(8,128)(2,1)S(1)}, u32[]{:S(2)}, u32[]{:S(2)}) %collective-permute-start.12) | collective-permute-done | bytes 524320 | tf_op jit(solution)/shard_map/ppermute | solution.py:170
  84.3 0.8 copy-done.10
  85.1 0.7 stack.79.start_ref
  85.8 0.8 select_reduce_fusion.table_ref
  86.6 0.5 collective-permute-start.16
  87.2 0.4 collective-permute-start.18
  87.7 0.4 collective-permute-start.20
  88.2 26.9 %attention.1.x_ref = bf16[256,2048]{1,0:T(8,128)(2,1)} custom-call(s32[1]{0:T(128)} %bitcast.18.seq_ref, bf16[256,2048]{1,0:T(8,128)(2,1)} %bitcast.41, bf16[1792,1024]{1,0:T(8,128)(2,1)} %bitcast.38, bf16[256,1024]{1,0:T(8,128)(2,1)} %bitcast.43, bf16[1792,1024]{1,0:T(8,128)(2,1)} %collective-permute-done.1.ckb_ref, bf16[256,1024]{1,0:T(8,128)(2,1)} %copy-done.1, ...), custom_call_target="tpu_custom_call" | custom-call | flops 8589934592 | bytes 18874368 | tf_op jit(solution)/shard_map/attention/pallas_call | solution.py:85
  115.2 0.7 copy-done.11
  115.9 0.2 copy-done.12
  116.3 0.2 copy-done.14
  116.6 18.9 %projection.1 = bf16[256,8192]{1,0:T(8,128)(2,1)} custom-call(s32[16,64]{1,0:T(8,128)} %select_reduce_fusion.table_ref, s32[17]{0:T(128)} %stack.79.start_ref, bf16[256,2048]{1,0:T(8,128)(2,1)} %attention.1.x_ref, bf16[256,128,128]{2,1,0:T(8,128)(2,1)} %bitcast.34, bf16[16,128,128]{2,1,0:T(8,128)(2,1)} %copy-done.3, bf16[16,128,128]{2,1,0:T(8,128)(2,1)} %copy-done.4, ...), custom_call_target="tpu_custom_call" | custom-call | flops 8589934592 | bytes 22020096 | tf_op jit(solution)/shard_map/projection/pallas_call | solution.py:143
  135.6 76.8 %reduce-scatter.2.cloned.1.call-done = bf16[256,2048]{1,0:T(8,128)(2,1)} async-done(((bf16[256,8192]{1,0:T(8,128)(2,1)}), bf16[256,2048]{1,0:T(8,128)(2,1)}) %reduce-scatter.2.cloned.1.call-update) | async-done | bytes 1048592 | tf_op jit(solution)/shard_map/reduce_scatter | solution.py:211
  (52 shorter events, 0.6 us)
Async XLA Ops:
  6.5 79.3 %copy-start = (s32[16,16]{1,0:T(8,128)S(1)}, s32[16,16]{1,0:T(8,128)}, u32[]{:S(2)}) copy-start(s32[16,16]{1,0:T(8,128)} %param.13) | copy-start | bytes 3076
  6.5 205.8 %reduce-scatter.2.cloned.1.call-start = ((), (), s32[]{:S(2)}) async-start(), calls=%async_computation.1 | async-start | bytes 5242880 | tf_op jit(solution)/shard_map/reduce_scatter | solution.py:211
  6.5 81.1 %collective-permute-start.1 = (bf16[1792,1024]{1,0:T(8,128)(2,1)}, bf16[1792,1024]{1,0:T(8,128)(2,1)}, u32[]{:S(2)}, u32[]{:S(2)}) collective-permute-start(bf16[1792,1024]{1,0:T(8,128)(2,1)} %bitcast.37), channel_id=1, source_target_pairs={{0,2},{2,0},{1,3},{3,1},{4,6},{6,4},{5,7},{7,5},{8,10},{10,8},{9,1... | collective-permute-start | bytes 11010056 | tf_op jit(solution)/shard_map/ppermute | solution.py:170
  7.0 80.7 %collective-permute-start.3 = (bf16[1792,1024]{1,0:T(8,128)(2,1)}, bf16[1792,1024]{1,0:T(8,128)(2,1)}, u32[]{:S(2)}, u32[]{:S(2)}) collective-permute-start(bf16[1792,1024]{1,0:T(8,128)(2,1)} %bitcast.39), channel_id=1, source_target_pairs={{0,2},{2,0},{1,3},{3,1},{4,6},{6,4},{5,7},{7,5},{8,10},{10,8},{9,1... | collective-permute-start | bytes 11010056 | tf_op jit(solution)/shard_map/ppermute | solution.py:170
  7.1 7.5 %collective-permute-start.2 = (bf16[256,1024]{1,0:T(8,128)(2,1)}, bf16[256,1024]{1,0:T(8,128)(2,1)S(1)}, u32[]{:S(2)}, u32[]{:S(2)}) collective-permute-start(bf16[256,1024]{1,0:T(8,128)(2,1)} %bitcast.42), channel_id=1, source_target_pairs={{0,2},{2,0},{1,3},{3,1},{4,6},{6,4},{5,7},{7,5},{8,10},{10,8},{9,1... | collective-permute-start | bytes 1572872 | tf_op jit(solution)/shard_map/ppermute | solution.py:170
  7.5 4.4 %collective-permute-start = (s32[16,16]{1,0:T(8,128)}, s32[16,16]{1,0:T(8,128)S(1)}, u32[]{:S(2)}, u32[]{:S(2)}) collective-permute-start(s32[16,16]{1,0:T(8,128)} %param.13), channel_id=1, source_target_pairs={{0,1},{1,0},{2,3},{3,2},{4,5},{5,4},{6,7},{7,6},{8,9},{9,8},{10,11... | collective-permute-start | bytes 3080 | tf_op jit(solution)/shard_map/ppermute | solution.py:170
  10.0 7.5 %collective-permute-start.4 = (bf16[256,1024]{1,0:T(8,128)(2,1)}, bf16[256,1024]{1,0:T(8,128)(2,1)S(1)}, u32[]{:S(2)}, u32[]{:S(2)}) collective-permute-start(bf16[256,1024]{1,0:T(8,128)(2,1)} %bitcast.44), channel_id=1, source_target_pairs={{0,2},{2,0},{1,3},{3,1},{4,6},{6,4},{5,7},{7,5},{8,10},{10,8},{9,1... | collective-permute-start | bytes 1572872 | tf_op jit(solution)/shard_map/ppermute | solution.py:170
  11.9 14.8 %collective-permute-start.5 = (bf16[16,128,128]{2,1,0:T(8,128)(2,1)S(1)}, bf16[16,128,128]{2,1,0:T(8,128)(2,1)S(1)}, u32[]{:S(2)}, u32[]{:S(2)}) collective-permute-start(bf16[16,128,128]{2,1,0:T(8,128)(2,1)S(1)} %get-tuple-element.8), channel_id=1, source_target_pairs={{0,1},{1,0},{2,3},{3,2},{4,5},{5,4},{6,7},{7,6},{8,9},{9,8},{10,11... | collective-permute-start | bytes 1572872 | tf_op jit(solution)/shard_map/ppermute | solution.py:170
  14.6 73.6 %copy-start.1 = (bf16[256,1024]{1,0:T(8,128)(2,1)}, bf16[256,1024]{1,0:T(8,128)(2,1)S(1)}, u32[]{:S(2)}) copy-start(bf16[256,1024]{1,0:T(8,128)(2,1)S(1)} %collective-permute-done.2.skb_ref) | copy-start | bytes 1572868
  14.6 23.3 %collective-permute-start.6 = (bf16[16,128,128]{2,1,0:T(8,128)(2,1)S(1)}, bf16[16,128,128]{2,1,0:T(8,128)(2,1)S(1)}, u32[]{:S(2)}, u32[]{:S(2)}) collective-permute-start(bf16[16,128,128]{2,1,0:T(8,128)(2,1)S(1)} %get-tuple-element.7), channel_id=1, source_target_pairs={{0,1},{1,0},{2,3},{3,2},{4,5},{5,4},{6,7},{7,6},{8,9},{9,8},{10,11... | collective-permute-start | bytes 1572872 | tf_op jit(solution)/shard_map/ppermute | solution.py:170
  17.5 70.7 %copy-start.2 = (bf16[256,1024]{1,0:T(8,128)(2,1)}, bf16[256,1024]{1,0:T(8,128)(2,1)S(1)}, u32[]{:S(2)}) copy-start(bf16[256,1024]{1,0:T(8,128)(2,1)S(1)} %collective-permute-done.4.svb_ref) | copy-start | bytes 1572868
  17.5 31.7 %collective-permute-start.7 = (bf16[16,128,128]{2,1,0:T(8,128)(2,1)S(1)}, bf16[16,128,128]{2,1,0:T(8,128)(2,1)S(1)}, u32[]{:S(2)}, u32[]{:S(2)}) collective-permute-start(bf16[16,128,128]{2,1,0:T(8,128)(2,1)S(1)} %get-tuple-element.6), channel_id=1, source_target_pairs={{0,1},{1,0},{2,3},{3,2},{4,5},{5,4},{6,7},{7,6},{8,9},{9,8},{10,11... | collective-permute-start | bytes 1572872 | tf_op jit(solution)/shard_map/ppermute | solution.py:170
  26.7 88.4 %copy-start.3 = (bf16[16,128,128]{2,1,0:T(8,128)(2,1)}, bf16[16,128,128]{2,1,0:T(8,128)(2,1)S(1)}, u32[]{:S(2)}) copy-start(bf16[16,128,128]{2,1,0:T(8,128)(2,1)S(1)} %collective-permute-done.5.refs_1_) | copy-start | bytes 1572868
  26.7 33.1 %collective-permute-start.8 = (bf16[16,128,128]{2,1,0:T(8,128)(2,1)S(1)}, bf16[16,128,128]{2,1,0:T(8,128)(2,1)S(1)}, u32[]{:S(2)}, u32[]{:S(2)}) collective-permute-start(bf16[16,128,128]{2,1,0:T(8,128)(2,1)S(1)} %get-tuple-element.5), channel_id=1, source_target_pairs={{0,1},{1,0},{2,3},{3,2},{4,5},{5,4},{6,7},{7,6},{8,9},{9,8},{10,11... | collective-permute-start | bytes 1572872 | tf_op jit(solution)/shard_map/ppermute | solution.py:170
  37.9 77.1 %copy-start.4 = (bf16[16,128,128]{2,1,0:T(8,128)(2,1)}, bf16[16,128,128]{2,1,0:T(8,128)(2,1)S(1)}, u32[]{:S(2)}) copy-start(bf16[16,128,128]{2,1,0:T(8,128)(2,1)S(1)} %collective-permute-done.6.refs_2_) | copy-start | bytes 1572868
  37.9 23.4 %collective-permute-start.9 = (bf16[16,128,128]{2,1,0:T(8,128)(2,1)S(1)}, bf16[16,128,128]{2,1,0:T(8,128)(2,1)S(1)}, u32[]{:S(2)}, u32[]{:S(2)}) collective-permute-start(bf16[16,128,128]{2,1,0:T(8,128)(2,1)S(1)} %collective-permute-done.5.refs_1_), channel_id=1, source_target_pairs={{0,16},{16,0},{1,17},{17,1},{2,18},{18,2},{3,19},{19,3},{4,20},{20... | collective-permute-start | bytes 1572872 | tf_op jit(solution)/shard_map/ppermute | solution.py:170
  49.2 65.9 %copy-start.5 = (bf16[16,128,128]{2,1,0:T(8,128)(2,1)}, bf16[16,128,128]{2,1,0:T(8,128)(2,1)S(1)}, u32[]{:S(2)}) copy-start(bf16[16,128,128]{2,1,0:T(8,128)(2,1)S(1)} %collective-permute-done.7.refs_3_) | copy-start | bytes 1572868
  49.2 12.7 %collective-permute-start.10 = (bf16[16,128,128]{2,1,0:T(8,128)(2,1)S(1)}, bf16[16,128,128]{2,1,0:T(8,128)(2,1)S(1)}, u32[]{:S(2)}, u32[]{:S(2)}) collective-permute-start(bf16[16,128,128]{2,1,0:T(8,128)(2,1)S(1)} %collective-permute-done.6.refs_2_), channel_id=1, source_target_pairs={{0,16},{16,0},{1,17},{17,1},{2,18},{18,2},{3,19},{19,3},{4,20},{20... | collective-permute-start | bytes 1572872 | tf_op jit(solution)/shard_map/ppermute | solution.py:170
  59.8 55.3 %copy-start.6 = (bf16[16,128,128]{2,1,0:T(8,128)(2,1)}, bf16[16,128,128]{2,1,0:T(8,128)(2,1)S(1)}, u32[]{:S(2)}) copy-start(bf16[16,128,128]{2,1,0:T(8,128)(2,1)S(1)} %collective-permute-done.8.refs_4_) | copy-start | bytes 1572868
  59.8 14.9 %collective-permute-start.11 = (bf16[16,128,128]{2,1,0:T(8,128)(2,1)S(1)}, bf16[16,128,128]{2,1,0:T(8,128)(2,1)S(1)}, u32[]{:S(2)}, u32[]{:S(2)}) collective-permute-start(bf16[16,128,128]{2,1,0:T(8,128)(2,1)S(1)} %collective-permute-done.7.refs_3_), channel_id=1, source_target_pairs={{0,16},{16,0},{1,17},{17,1},{2,18},{18,2},{3,19},{19,3},{4,20},{20... | collective-permute-start | bytes 1572872 | tf_op jit(solution)/shard_map/ppermute | solution.py:170
  61.3 23.0 %copy-start.7 = (bf16[16,128,128]{2,1,0:T(8,128)(2,1)}, bf16[16,128,128]{2,1,0:T(8,128)(2,1)S(1)}, u32[]{:S(2)}) copy-start(bf16[16,128,128]{2,1,0:T(8,128)(2,1)S(1)} %collective-permute-done.9.refs_5_) | copy-start | bytes 1572868
  61.3 23.0 %collective-permute-start.12 = (bf16[16,128,128]{2,1,0:T(8,128)(2,1)S(1)}, bf16[16,128,128]{2,1,0:T(8,128)(2,1)S(1)}, u32[]{:S(2)}, u32[]{:S(2)}) collective-permute-start(bf16[16,128,128]{2,1,0:T(8,128)(2,1)S(1)} %collective-permute-done.8.refs_4_), channel_id=1, source_target_pairs={{0,16},{16,0},{1,17},{17,1},{2,18},{18,2},{3,19},{19,3},{4,20},{20... | collective-permute-start | bytes 1572872 | tf_op jit(solution)/shard_map/ppermute | solution.py:170
  61.8 22.5 %copy-start.8 = (bf16[16,128,128]{2,1,0:T(8,128)(2,1)}, bf16[16,128,128]{2,1,0:T(8,128)(2,1)S(1)}, u32[]{:S(2)}) copy-start(bf16[16,128,128]{2,1,0:T(8,128)(2,1)S(1)} %collective-permute-done.10.refs_6_) | copy-start | bytes 1572868
  61.8 24.8 %collective-permute-start.13 = (bf16[16,128,128]{2,1,0:T(8,128)(2,1)S(1)}, bf16[16,128,128]{2,1,0:T(8,128)(2,1)}, u32[]{:S(2)}, u32[]{:S(2)}) collective-permute-start(bf16[16,128,128]{2,1,0:T(8,128)(2,1)S(1)} %collective-permute-done.5.refs_1_), channel_id=1, source_target_pairs={{0,2},{2,0},{1,3},{3,1},{4,6},{6,4},{5,7},{7,5},{8,10},{10,8},{9,1... | collective-permute-start | bytes 1572872 | tf_op jit(solution)/shard_map/ppermute | solution.py:170
  74.6 9.7 %copy-start.9 = (bf16[16,128,128]{2,1,0:T(8,128)(2,1)}, bf16[16,128,128]{2,1,0:T(8,128)(2,1)S(1)}, u32[]{:S(2)}) copy-start(bf16[16,128,128]{2,1,0:T(8,128)(2,1)S(1)} %collective-permute-done.11.refs_7_) | copy-start | bytes 1572868
  74.6 12.5 %collective-permute-start.14 = (bf16[16,128,128]{2,1,0:T(8,128)(2,1)S(1)}, bf16[16,128,128]{2,1,0:T(8,128)(2,1)}, u32[]{:S(2)}, u32[]{:S(2)}) collective-permute-start(bf16[16,128,128]{2,1,0:T(8,128)(2,1)S(1)} %collective-permute-done.6.refs_2_), channel_id=1, source_target_pairs={{0,2},{2,0},{1,3},{3,1},{4,6},{6,4},{5,7},{7,5},{8,10},{10,8},{9,1... | collective-permute-start | bytes 1572872 | tf_op jit(solution)/shard_map/ppermute | solution.py:170
  85.1 2.1 collective-permute-start.15
  86.6 28.5 %collective-permute-start.16 = (bf16[16,128,128]{2,1,0:T(8,128)(2,1)S(1)}, bf16[16,128,128]{2,1,0:T(8,128)(2,1)S(1)}, u32[]{:S(2)}, u32[]{:S(2)}) collective-permute-start(bf16[16,128,128]{2,1,0:T(8,128)(2,1)S(1)} %collective-permute-done.8.refs_4_), channel_id=1, source_target_pairs={{0,2},{2,0},{1,3},{3,1},{4,6},{6,4},{5,7},{7,5},{8,10},{10,8},{9,1... | collective-permute-start | bytes 1572872 | tf_op jit(solution)/shard_map/ppermute | solution.py:170
  87.1 28.0 %collective-permute-start.17 = (bf16[16,128,128]{2,1,0:T(8,128)(2,1)}, bf16[16,128,128]{2,1,0:T(8,128)(2,1)S(1)}, u32[]{:S(2)}, u32[]{:S(2)}) collective-permute-start(bf16[16,128,128]{2,1,0:T(8,128)(2,1)} %copy-done.7), channel_id=1, source_target_pairs={{0,2},{2,0},{1,3},{3,1},{4,6},{6,4},{5,7},{7,5},{8,10},{10,8},{9,1... | collective-permute-start | bytes 1572872 | tf_op jit(solution)/shard_map/ppermute | solution.py:170
  87.2 27.9 %collective-permute-start.18 = (bf16[16,128,128]{2,1,0:T(8,128)(2,1)}, bf16[16,128,128]{2,1,0:T(8,128)(2,1)S(1)}, u32[]{:S(2)}, u32[]{:S(2)}) collective-permute-start(bf16[16,128,128]{2,1,0:T(8,128)(2,1)} %copy-done.8), channel_id=1, source_target_pairs={{0,2},{2,0},{1,3},{3,1},{4,6},{6,4},{5,7},{7,5},{8,10},{10,8},{9,1... | collective-permute-start | bytes 1572872 | tf_op jit(solution)/shard_map/ppermute | solution.py:170
  87.6 27.5 %collective-permute-start.19 = (bf16[16,128,128]{2,1,0:T(8,128)(2,1)}, bf16[16,128,128]{2,1,0:T(8,128)(2,1)S(1)}, u32[]{:S(2)}, u32[]{:S(2)}) collective-permute-start(bf16[16,128,128]{2,1,0:T(8,128)(2,1)} %copy-done.9), channel_id=1, source_target_pairs={{0,2},{2,0},{1,3},{3,1},{4,6},{6,4},{5,7},{7,5},{8,10},{10,8},{9,1... | collective-permute-start | bytes 1572872 | tf_op jit(solution)/shard_map/ppermute | solution.py:170
  87.7 27.5 %collective-permute-start.20 = (bf16[16,128,128]{2,1,0:T(8,128)(2,1)}, bf16[16,128,128]{2,1,0:T(8,128)(2,1)S(1)}, u32[]{:S(2)}, u32[]{:S(2)}) collective-permute-start(bf16[16,128,128]{2,1,0:T(8,128)(2,1)} %copy-done.10), channel_id=1, source_target_pairs={{0,2},{2,0},{1,3},{3,1},{4,6},{6,4},{5,7},{7,5},{8,10},{10,8},{9,1... | collective-permute-start | bytes 1572872 | tf_op jit(solution)/shard_map/ppermute | solution.py:170
  (6 other events, 6.5 us)
Sparse Core Ops, SparseCore 0:
  135.7 76.6 reduce-scatter.1

commit v2 on v0

v2 whole, which is shorter than its diff:
```python
import functools
import math

import jax
import jax.numpy as jnp
from jax import lax
from jax.experimental import pallas as pl
from jax.experimental.pallas import tpu as pltpu
from jax.sharding import PartitionSpec as P

HD = 128
FLOOR = -1e30
TILE = 768
STEP_COLS = 8
EXTRA = 1


def in_hbm(value):
    return pltpu.with_memory_space_constraint(value, pltpu.HBM)


def attention_body(seq_ref, q_ref, cka, ska, ckb, skb, cva, sva, cvb, svb, out_ref):
    rows = q_ref.shape[0]
    cache_rows = cka.shape[0]
    scale = HD ** (-0.5) * math.log2(math.e)
    q = q_ref[...].astype(jnp.float32) * scale
    q_hi = q.astype(jnp.bfloat16)
    q_lo = (q - q_hi.astype(jnp.float32)).astype(jnp.bfloat16)
    q_two = jnp.concatenate(
        [jnp.concatenate([q_hi[:, h * HD : (h + 1) * HD], q_lo[:, h * HD : (h + 1) * HD]], axis=1) for h in range(2)],
        axis=0,
    )
    whole = (cache_rows - 1) // TILE
    tiles = []
    for side, (ck, sk, cv, sv) in enumerate(((cka, ska, cva, sva), (ckb, skb, cvb, svb))):
        for t in range(whole):
            tiles.append((ck, cv, None, None, t * TILE, (t + 1) * TILE, None))
        tiles.append((ck, cv, sk, sv, whole * TILE, cache_rows, side))

    def take(main, fresh, lo, hi):
        return main[lo:hi, :] if fresh is None else jnp.concatenate([main[lo:hi, :], fresh[...]], axis=0)

    def score(tile):
        ck, _, sk, _, lo, hi, side = tile
        keys = take(ck, sk, lo, hi)
        scores = lax.dot_general(
            q_two,
            jnp.concatenate([keys, keys], axis=1),
            (((1,), (1,)), ((), ())),
            preferred_element_type=jnp.float32,
        )
        if side is None:
            return scores
        tail = scores[:, hi - lo :]
        if side == 0:
            token = lax.broadcasted_iota(jnp.int32, (rows, rows), 0)
            position = lax.broadcasted_iota(jnp.int32, (rows, rows), 1)
            seen = position <= token
            tail = jnp.where(jnp.concatenate([seen, seen], axis=0), tail, FLOOR)
        else:
            tail = jnp.where(seq_ref[0] > 0, tail, FLOOR)
        return jnp.concatenate([scores[:, : hi - lo], tail], axis=1)

    peak = acc = None
    upcoming = score(tiles[0])
    for i, tile in enumerate(tiles):
        scores = upcoming
        if i + 1 < len(tiles):
            upcoming = score(tiles[i + 1])
        tile_peak = jnp.max(scores, axis=1, keepdims=True)
        new_peak = tile_peak if peak is None else jnp.maximum(peak, tile_peak)
        expo = jnp.exp2(scores - new_peak).astype(jnp.bfloat16)
        values = take(tile[1], tile[3], tile[4], tile[5])
        added = jnp.dot(
            expo,
            jnp.concatenate([values, jnp.ones_like(values)], axis=1),
            preferred_element_type=jnp.float32,
        )
        acc = added if acc is None else acc * jnp.exp2(peak - new_peak) + added
        peak = new_peak
    result = acc[:, :HD] / acc[:, HD:]
    out_ref[:, :HD] = result[:rows].astype(out_ref.dtype)
    out_ref[:, HD:] = result[rows:].astype(out_ref.dtype)


def attention(my_seq, q, own, peer, first, count, earlier=None):
    rows, width = q.shape
    ck, sk, cv, sv = own
    pck, ps, pcv = peer
    cache_rows = ck.shape[0]
    qspec = pl.BlockSpec((rows, 2 * HD), lambda g, s: (0, g + first))
    cspec = pl.BlockSpec((cache_rows, HD), lambda g, s: (0, g + first))
    nspec = pl.BlockSpec((rows, HD), lambda g, s: (0, g + first))
    vspec = pl.BlockSpec((rows, HD), lambda g, s: (1, g + first))
    args = [q, ck, sk, pck, ps, cv, sv, pcv, ps]
    specs = [qspec, cspec, nspec, cspec, nspec, cspec, nspec, cspec, vspec]
    body = attention_body
    aliases = {}
    if earlier is not None:
        body = lambda *refs: attention_body(*refs[:10], *refs[11:])
        args.append(earlier)
        specs.append(pl.BlockSpec(memory_space=pltpu.HBM))
        aliases = {10: 0}
    return pl.pallas_call(
        body,
        out_shape=pltpu.HBM((rows, width), jnp.bfloat16),
        grid_spec=pltpu.PrefetchScalarGridSpec(
            num_scalar_prefetch=1,
            grid=(count,),
            in_specs=specs,
            out_specs=qspec,
        ),
        input_output_aliases=aliases,
        compiler_params=pltpu.CompilerParams(
            dimension_semantics=("arbitrary",), vmem_limit_bytes=20 << 20
        ),
        cost_estimate=pl.CostEstimate(flops=1, transcendentals=0, bytes_accessed=1),
        name="attention" if earlier is None else "late_attention",
    )(my_seq, *[in_hbm(a) for a in args])


def projection_body(sources, kept, has_acc, table_ref, rows_ref, x_ref, *refs):
    n_pieces = 1 + max(piece for row in sources for piece, _, _ in row)
    pieces = refs[:n_pieces]
    refs = refs[n_pieces:]
    if has_acc:
        acc_hbm, refs = refs[0], refs[1:]
    out_ref, held, sems, stage, out_sems = refs[:5]
    slots = len(sources[0]) * kept
    empty = len(sources) * slots
    row_ids = [rows_ref[i] for i in range(len(sources))]
    copies = []
    for i, row in enumerate(sources):
        for j, (piece, offset, by_row) in enumerate(row):
            start = offset + row_ids[i] * kept if by_row else offset
            copies.append(
                pltpu.make_async_copy(
                    pieces[piece].at[pl.ds(start, kept)],
                    held.at[pl.ds(i * slots + j * kept, kept)],
                    sems.at[i, j],
                )
            )
    for copy in copies:
        copy.start()
    n_steps = table_ref.shape[1] // STEP_COLS
    span = STEP_COLS * HD

    def fill(step):
        acc_ref, acc_sems = refs[5:]
        where = pl.ds(pl.multiple_of(step * span, span), span)
        return pltpu.make_async_copy(acc_hbm.at[:, where], acc_ref.at[step], acc_sems.at[step])

    if has_acc:
        for step in range(n_steps):
            fill(step).start()
    held[empty] = jnp.zeros(held.shape[1:], held.dtype)
    for copy in copies:
        copy.wait()
    x = jnp.concatenate([x_ref[:, pl.ds(pl.multiple_of(r * HD, HD), HD)] for r in row_ids], axis=1)

    def drain(slot, step):
        return pltpu.make_async_copy(
            stage.at[slot], out_ref.at[:, pl.ds(pl.multiple_of(step * span, span), span)], out_sems.at[slot]
        )

    def one_step(step, carry):
        slot = step % 2

        @pl.when(step >= 2)
        def _():
            drain(slot, step - 2).wait()

        if has_acc:
            fill(step).wait()
        for pair in range(STEP_COLS // 2):
            sides = []
            for side in range(2):
                col = step * STEP_COLS + 2 * pair + side
                sides.append(
                    jnp.concatenate(
                        [held[jnp.minimum(table_ref[r, col] + i * slots, empty)] for i, r in enumerate(row_ids)],
                        axis=0,
                    )
                )
            value = jnp.dot(x, jnp.concatenate(sides, axis=1), preferred_element_type=jnp.float32)
            where = slice(2 * pair * HD, 2 * (pair + 1) * HD)
            if has_acc:
                value = value + refs[5][step, :, where]
            stage[slot, :, where] = value.astype(out_ref.dtype)
        drain(slot, step).start()
        return carry

    lax.fori_loop(0, n_steps, one_step, 0)
    for step in range(max(0, n_steps - 2), n_steps):
        drain(step % 2, step).wait()


def projection(x, table, row_ids, sources, pieces, kept, acc, last):
    tokens, width = x.shape
    col_blocks = table.shape[1]
    n_rows = len(sources)
    slots = len(sources[0]) * kept
    shape = (tokens, col_blocks * HD)
    smem = pl.BlockSpec(memory_space=pltpu.SMEM)
    vmem = pl.BlockSpec(memory_space=pltpu.VMEM)
    hbm = pl.BlockSpec(memory_space=pl.ANY)
    scratch = [
        pltpu.VMEM((n_rows * slots + 1, HD, HD), jnp.bfloat16),
        pltpu.SemaphoreType.DMA((n_rows, len(sources[0]))),
    ]
    span = STEP_COLS * HD
    dtype = jnp.bfloat16 if last else jnp.float32
    scratch += [pltpu.VMEM((2, tokens, span), dtype), pltpu.SemaphoreType.DMA((2,))]
    if acc is not None:
        n_steps = col_blocks // STEP_COLS
        scratch += [pltpu.VMEM((n_steps, tokens, span), jnp.float32), pltpu.SemaphoreType.DMA((n_steps,))]
    return pl.pallas_call(
        functools.partial(projection_body, sources, kept, acc is not None),
        out_shape=pltpu.HBM(shape, dtype),
        in_specs=[smem, smem, vmem] + [hbm] * len(pieces) + ([hbm] if acc is not None else []),
        out_specs=hbm,
        scratch_shapes=scratch,
        compiler_params=pltpu.CompilerParams(vmem_limit_bytes=28 << 20),
        cost_estimate=pl.CostEstimate(flops=1, transcendentals=0, bytes_accessed=1),
        name="projection" if last else "early_projection",
    )(table, row_ids, x, in_hbm(pieces[0]), *pieces[1:], *(() if acc is None else (in_hbm(acc),)))


def swap(value, axis):
    return lax.ppermute(value, axis, [(0, 1), (1, 0)])


def after(value, *earlier):
    return lax.optimization_barrier((value,) + earlier)[0]


def peer_side(own):
    ck, sk, cv, sv = own
    return [swap(ck, "seq"), swap(jnp.concatenate([sk, sv], axis=0), "seq"), swap(cv, "seq")]


def column_table(all_columns, col_blocks):
    dp, _, kept = all_columns.shape
    slot = jnp.arange(dp, dtype=jnp.int32)[:, None] * kept + jnp.arange(kept, dtype=jnp.int32)[None, :]
    match = all_columns[..., None] == jnp.arange(col_blocks, dtype=jnp.int32)
    return jnp.min(jnp.where(match, slot[:, None, :, None], 1 << 20), axis=(0, 2))


def shards(mesh, queries, stretch_keys, stretch_values, cache_keys, cache_values, blocks, block_columns):
    width_dev = queries.shape[2]
    row_blocks, kept, block_size = blocks.shape[:3]
    col_blocks = mesh.shape["tensor"] * width_dev // block_size
    my_seq = lax.axis_index("seq")
    seq_one = my_seq.reshape(1)
    q = queries[0]
    own = [a[0] for a in (cache_keys, stretch_keys, cache_values, stretch_values)]
    flat = blocks.reshape(row_blocks * kept, block_size, block_size)

    if mesh.shape["dp"] == 2 and mesh.shape["groups"] == 2 and row_blocks % 16 == 0 and max(row_blocks, kept) <= block_size:
        unit = row_blocks // 16
        groups = lax.axis_index("groups")
        half = 8 * unit * my_seq
        relay = half + unit * (2 + 3 * groups)

        def piece(start, count, more=0):
            return lax.dynamic_slice_in_dim(flat, start * kept, count * kept + more, 0)

        heads = width_dev // (2 * HD)
        soon = max(heads // 4, 1)
        carried = jnp.pad(
            block_columns.astype(jnp.bfloat16), ((0, block_size - row_blocks), (0, block_size - kept))
        )
        near1 = swap(jnp.concatenate([piece(relay, unit), carried[None]], axis=0), "dp")
        near2 = swap(piece(relay + unit, 2 * unit), "dp")
        shared = swap(piece(half, 2 * unit, EXTRA), "dp")
        peer = peer_side(own)
        attended = attention(seq_one, q, own, peer, 0, soon)
        near1, attended = lax.optimization_barrier((near1, attended))
        peer_columns = near1[unit * kept, :row_blocks, :kept].astype(jnp.int32)
        table = column_table(jnp.stack([block_columns, peer_columns]), col_blocks)
        far1 = swap(near1[: unit * kept], "groups")
        near1_other = swap(near1[: unit * kept], "seq")
        attended = attention(seq_one, q, own, peer, soon, heads - soon, attended)
        near2, far1, attended = lax.optimization_barrier((near2, far1, attended))
        far2, far3 = [swap(near2[i * unit * kept : (i + 1) * unit * kept], "groups") for i in range(2)]
        near2_other = swap(near2, "seq")
        far1_other = swap(far1, "seq")
        other = 8 * unit * (1 - my_seq)

        def stage(plan, acc, last):
            row_list, sources, pieces = [], [], [flat]
            for start, count, value in plan:
                for i in range(count):
                    row_list.append(start + i)
                    sources.append(((0, 0, True), (len(pieces), i * kept, False)))
                pieces.append(value)
            return projection(attended, table, jnp.stack(row_list), tuple(sources), pieces, kept, acc, last)

        def relayed(base, group):
            return base + unit * (2 + 3 * group)

        early = stage(
            (
                (relayed(half, groups), unit, near1),
                (relayed(half, groups) + unit, 2 * unit, near2),
                (relayed(half, 1 - groups), unit, far1),
                (relayed(other, groups), unit, near1_other),
                (relayed(other, groups) + unit, 2 * unit, near2_other),
                (relayed(other, 1 - groups), unit, far1_other),
            ),
            None,
            False,
        )
        shared, far2, far3, early = lax.optimization_barrier((shared, far2, far3, early))
        shared_other = swap(shared[: 2 * unit * kept], "seq")
        far2_other = swap(far2, "seq")
        far3_other = swap(far3, "seq")
        partial_value = stage(
            (
                (half, 2 * unit, shared),
                (relayed(half, 1 - groups) + unit, unit, far2),
                (relayed(half, 1 - groups) + 2 * unit, unit, far3),
                (other, 2 * unit, shared_other),
                (relayed(other, 1 - groups) + unit, unit, far2_other),
                (relayed(other, 1 - groups) + 2 * unit, unit, far3_other),
            ),
            early,
            True,
        )
    else:
        dp = mesh.shape["dp"]
        gathered = lax.all_gather(flat, "dp", axis=0, tiled=True)
        table = column_table(lax.all_gather(block_columns, "dp", axis=0), col_blocks)
        peer = peer_side(own)
        attended = attention(seq_one, q, own, peer, 0, width_dev // (2 * HD))
        sources = tuple(tuple((0, d * row_blocks * kept, True) for d in range(dp)) for _ in range(row_blocks))
        partial_value = projection(
            attended, table, jnp.arange(row_blocks, dtype=jnp.int32), sources, [gathered], kept, None, True
        )
    owned = lax.psum_scatter(partial_value, "tensor", scatter_dimension=1, tiled=True)
    return owned[None]


def solution(mesh):
    token = P(("groups", "dp"), "seq", "tensor")
    placed = (token, token, token, token, token, P("tensor", "dp", None, None), P("tensor", "dp"))
    return jax.shard_map(
        functools.partial(shards, mesh),
        mesh=mesh,
        in_specs=placed,
        out_specs=token,
        check_vma=False,
    )
```

time: 492 us -> 182 us (0.37)
  local copies, waits for them, and re-layouts: 139 us -> 13.2 us
  waiting for transfers between devices: 206 us -> 92 us
  matrix products: 92.2 us -> 0 us
  Pallas kernels: 0 us -> 49 us
  other arithmetic: 34.1 us -> 4.11 us
  starting transfers between devices: 0.12 us -> 10 us
  blocking collectives: 5.77 us -> 0 us
    all_gather x3 -> x0, waiting for transfers between devices: 129 us -> none  [the longest x1 117 us: shards(): block_piece = lax.all_gather(blocks, 'dp', axis=1, tiled=True)]
    scatter x2 -> x0, local copies, waits for them, and re-layouts: 109 us -> none  [shards(): dense_panel = empty_panel.at[row_index, :, column_piece, :].set(block_piece)]
    dot_general x3 -> x0, matrix products: 92.2 us -> none  [the longest x1 36 us: shards(): jnp.einsum('stpgd,smpd->stpgm', query_heads, key_tiles, preferred_element...]
    pallas_call x0 -> x4, Pallas kernels: none -> 49 us  [the longest x2 25.2 us: attention(): pl.pallas_call(body, out_shape=pltpu.HBM((rows, width), jnp.bfloat16), gr...]
    reduce_sum x1 -> x0, other arithmetic: 21.7 us -> none  [shards(): run_total = jnp.sum(exp_terms, axis=-1)]
    ppermute x0 -> x15, waiting for transfers between devices: none -> 15.7 us  [swap(): return lax.ppermute(value, axis, [(0, 1), (1, 0)])]
    all_gather x1 -> x0, local copies, waits for them, and re-layouts: 11.7 us -> none  [shards(): value_piece = lax.all_gather(context_values, 'seq', axis=1, tiled=True)]
    broadcast_in_dim x1, local copies, waits for them, and re-layouts: 11.2 us -> 0.01 us  [shards(): carried[None]]
  transfers between devices with their start and end apart: 4 -> 16, of which waited for: 4 -> 7; matrix products, arithmetic and copies ran while one was open for 23% -> 7% of each run, Pallas kernels for 0% -> 20%
where the time goes in v2:
time: 182 us
  waiting for transfers between devices  92 us (51%)
  Pallas kernels  49 us (27%)
  between operations  13.5 us (7%)
  local copies, waits for them, and re-layouts  13.2 us (7%)
  starting transfers between devices  10 us (5%)
  other arithmetic  4.11 us (2%)
    reduce_scatter x1, waiting for transfers between devices, shards(): lax.psum_scatter(partial_value, 'tensor', scatter_dimension=1, tiled=True)  76.3 us
    pallas_call x2, Pallas kernels, attention(): pl.pallas_call(body, out_shape=pltpu.HBM((rows, width), jnp.bfloat16), gr...  25.2 us
    pallas_call x2, Pallas kernels, projection(): pl.pallas_call(functools.partial(projection_body, sources, kept, acc is n...  23.9 us
    ppermute x15, waiting for transfers between devices, swap(): return lax.ppermute(value, axis, [(0, 1), (1, 0)])  15.7 us
    ppermute x15, starting transfers between devices, swap(): return lax.ppermute(value, axis, [(0, 1), (1, 0)])  10 us
    dynamic_slice x3, local copies, waits for them, and re-layouts, piece(): return lax.dynamic_slice_in_dim(flat, start * kept, count * kept + more, 0)  5.9 us
    unnamed x16, local copies, waits for them, and re-layouts  4.13 us
  transfers between devices with their start and end apart: 16, of which 7 were waited for; matrix products, arithmetic and copies ran while one was open for 7% of the time, Pallas kernels for 20%

profile of v2, /device:TPU:0, one launch (start us, length us, event | category | flops | bytes accessed | tf_op | source)
XLA Modules:
  0.0 181.9 jit_solution(14309581315712454784)
XLA Ops:
  6.5 0.5 collective-permute-start.1
  7.0 2.2 %pad_maximum_fusion = bf16[512,1024]{1,0:T(8,128)(2,1)} fusion(bf16[256,1024]{1,0:T(8,128)(2,1)} %bitcast.41, bf16[256,1024]{1,0:T(8,128)(2,1)} %bitcast.38), kind=kLoop, calls=%fused_computation | loop fusion | flops 2097152 | bytes 2097152 | tf_op jit(solution)/shard_map/concatenate | solution.py:239
  9.3 0.5 collective-permute-start.2
  9.7 0.7 convert_element_type.9
  10.4 1.1 constant_dynamic-slice_fusion.2
  11.5 0.9 pad_maximum_fusion.1
  12.5 2.5 %collective-permute-start = (bf16[17,128,128]{2,1,0:T(8,128)(2,1)}, bf16[17,128,128]{2,1,0:T(8,128)(2,1)S(1)}, u32[]{:S(2)}, u32[]{:S(2)}) collective-permute-start(bf16[17,128,128]{2,1,0:T(8,128)(2,1)} %pad_maximum_fusion.1), channel_id=1, source_target_pairs={{0,1},{1,0},{2,3},{3,2},{4,5},{5,4},{6,7},{7,6},{8,9},{9,8},{10,11... | collective-permute-start | bytes 1671176 | tf_op jit(solution)/shard_map/ppermute | solution.py:230
  14.9 2.4 %constant_dynamic-slice_fusion.1 = bf16[32,128,128]{2,1,0:T(8,128)(2,1)} fusion(bf16[256,128,128]{2,1,0:T(8,128)(2,1)} %bitcast.28, s32[]{:T(128)S(6)} %select_n.15), kind=kLoop, calls=%fused_computation.9 | loop fusion | bytes 2097156 | tf_op jit(solution)/shard_map/dynamic_slice | solution.py:266
  17.4 2.8 %collective-permute-done.3.cvb.refs_8_ = bf16[1792,1024]{1,0:T(8,128)(2,1)} collective-permute-done((bf16[1792,1024]{1,0:T(8,128)(2,1)}, bf16[1792,1024]{1,0:T(8,128)(2,1)}, u32[]{:S(2)}, u32[]{:S(2)}) %collective-permute-start.3) | collective-permute-done | bytes 3670048 | tf_op jit(solution)/shard_map/ppermute | solution.py:230
  20.1 7.4 %attention.1.refs_10_ = bf16[256,2048]{1,0:T(8,128)(2,1)} custom-call(s32[1]{0:T(128)} %bitcast.3.seq_ref.refs_0_, bf16[256,2048]{1,0:T(8,128)(2,1)} %bitcast.44, bf16[1792,1024]{1,0:T(8,128)(2,1)} %bitcast.33, bf16[256,1024]{1,0:T(8,128)(2,1)} %bitcast.39, bf16[1792,1024]{1,0:T(8,128)(2,1)} %collective-permute-done.1.ckb.refs_4_, ...), custom_call_target="tpu_custom_call" | custom-call | flops 1 | bytes 1 | tf_op jit(solution)/shard_map/attention/pallas_call | solution.py:104
  27.5 1.1 collective-permute-done.refs_1_
  28.6 0.9 slice.17
  29.5 2.0 %collective-permute-start.5 = (bf16[16,128,128]{2,1,0:T(8,128)(2,1)}, bf16[16,128,128]{2,1,0:T(8,128)(2,1)}, u32[]{:S(2)}, u32[]{:S(2)}) collective-permute-start(bf16[16,128,128]{2,1,0:T(8,128)(2,1)} %slice.17), channel_id=1, source_target_pairs={{0,16},{16,0},{1,17},{17,1},{2,18},{18,2},{3,19},{19,3},{4,20},{20... | collective-permute-start | bytes 1572872 | tf_op jit(solution)/shard_map/ppermute | solution.py:230
  31.5 2.4 %constant_dynamic-slice_fusion = bf16[33,128,128]{2,1,0:T(8,128)(2,1)} fusion(bf16[256,128,128]{2,1,0:T(8,128)(2,1)} %bitcast.29, s32[]{:T(128)S(6)} %select_n.16), kind=kLoop, calls=%fused_computation.8 | loop fusion | bytes 2162692 | tf_op jit(solution)/shard_map/dynamic_slice | solution.py:266
  33.9 1.5 collective-permute-start.6
  35.4 17.8 %late_attention.1.x_ref = bf16[256,2048]{1,0:T(8,128)(2,1)} custom-call(s32[1]{0:T(128)} %bitcast.3.seq_ref.refs_0_, bf16[256,2048]{1,0:T(8,128)(2,1)} %bitcast.45, bf16[1792,1024]{1,0:T(8,128)(2,1)} %bitcast.34, bf16[256,1024]{1,0:T(8,128)(2,1)} %bitcast.40, bf16[1792,1024]{1,0:T(8,128)(2,1)} %collective-permute-done.1.ckb.refs_4_, ...), custom_call_target="tpu_custom_call", output_to_operand_aliasing={{}: (10, {})} | custom-call | flops 1 | bytes 1 | tf_op jit(solution)/shard_map/late_attention/pallas_call | solution.py:104
  53.8 1.1 fusion
  54.9 0.5 collective-permute-start.8
  55.4 0.8 copy-done.4
  56.2 1.5 collective-permute-start.7
  58.1 1.2 copy-done
  59.3 1.1 copy-done.3
  60.4 1.0 copy-done.5
  61.4 11.2 %early_projection.1.refs_7_ = f32[256,8192]{1,0:T(8,128)} custom-call(s32[16,64]{1,0:T(8,128)S(1)} %select_reduce_fusion.table_ref, s32[8]{0:T(128)S(1)} %stack.80.rows_ref, bf16[256,2048]{1,0:T(8,128)(2,1)S(1)} %copy-done, bf16[256,128,128]{2,1,0:T(8,128)(2,1)} %bitcast.30, bf16[17,128,128]{2,1,0:T(8,128)(2,1)S(1)} %copy-done.3, ...), custom_call_target="tpu_custom_call" | custom-call | flops 1 | bytes 1 | tf_op jit(solution)/shard_map/early_projection/pallas_call | solution.py:217
  72.6 1.5 collective-permute-done.6.refs_1_
  74.1 6.4 %collective-permute-done.7.refs_2_ = bf16[16,128,128]{2,1,0:T(8,128)(2,1)} collective-permute-done((bf16[16,128,128]{2,1,0:T(8,128)(2,1)}, bf16[16,128,128]{2,1,0:T(8,128)(2,1)}, u32[]{:S(2)}, u32[]{:S(2)}) %collective-permute-start.7) | collective-permute-done | bytes 524320 | tf_op jit(solution)/shard_map/ppermute | solution.py:230
  80.5 1.0 slice.20
  81.5 0.5 collective-permute-start.13
  82.1 2.8 %collective-permute-done.13.refs_5_ = bf16[16,128,128]{2,1,0:T(8,128)(2,1)} collective-permute-done((bf16[16,128,128]{2,1,0:T(8,128)(2,1)}, bf16[16,128,128]{2,1,0:T(8,128)(2,1)}, u32[]{:S(2)}, u32[]{:S(2)}) %collective-permute-start.13) | collective-permute-done | bytes 524320 | tf_op jit(solution)/shard_map/ppermute | solution.py:230
  84.9 1.1 collective-permute-done.14.refs_6_
  86.0 12.7 %projection.1 = bf16[256,8192]{1,0:T(8,128)(2,1)} custom-call(s32[16,64]{1,0:T(8,128)S(1)} %select_reduce_fusion.table_ref, s32[8]{0:T(128)S(1)} %stack.71.rows_ref, bf16[256,2048]{1,0:T(8,128)(2,1)S(1)} %copy-done.1, bf16[256,128,128]{2,1,0:T(8,128)(2,1)} %bitcast.31, bf16[33,128,128]{2,1,0:T(8,128)(2,1)S(1)} %collective-permute-done.6.refs_1_, ...), custom_call_target="tpu_custom_call" | custom-call | flops 1 | bytes 1 | tf_op jit(solution)/shard_map/projection/pallas_call | solution.py:217
  98.7 76.3 %reduce-scatter.2.cloned.1.call-done = bf16[256,2048]{1,0:T(8,128)(2,1)} async-done(((bf16[256,8192]{1,0:T(8,128)(2,1)}), bf16[256,2048]{1,0:T(8,128)(2,1)}) %reduce-scatter.2.cloned.1.call-update) | async-done | bytes 1048592 | tf_op jit(solution)/shard_map/reduce_scatter | solution.py:340
  (38 shorter events, 1.1 us)
Async XLA Ops:
  6.5 168.5 %reduce-scatter.2.cloned.1.call-start = ((), (), s32[]{:S(2)}) async-start(), calls=%async_computation.1 | async-start | bytes 5242880 | tf_op jit(solution)/shard_map/reduce_scatter | solution.py:340
  6.5 10.8 %collective-permute-start.1 = (bf16[1792,1024]{1,0:T(8,128)(2,1)}, bf16[1792,1024]{1,0:T(8,128)(2,1)}, u32[]{:S(2)}, u32[]{:S(2)}) collective-permute-start(bf16[1792,1024]{1,0:T(8,128)(2,1)} %bitcast.32), channel_id=1, source_target_pairs={{0,2},{2,0},{1,3},{3,1},{4,6},{6,4},{5,7},{7,5},{8,10},{10,8},{9,1... | collective-permute-start | bytes 11010056 | tf_op jit(solution)/shard_map/ppermute | solution.py:230
  7.0 13.1 %collective-permute-start.3 = (bf16[1792,1024]{1,0:T(8,128)(2,1)}, bf16[1792,1024]{1,0:T(8,128)(2,1)}, u32[]{:S(2)}, u32[]{:S(2)}) collective-permute-start(bf16[1792,1024]{1,0:T(8,128)(2,1)} %bitcast.35), channel_id=1, source_target_pairs={{0,2},{2,0},{1,3},{3,1},{4,6},{6,4},{5,7},{7,5},{8,10},{10,8},{9,1... | collective-permute-start | bytes 11010056 | tf_op jit(solution)/shard_map/ppermute | solution.py:230
  9.3 8.1 %collective-permute-start.2 = (bf16[512,1024]{1,0:T(8,128)(2,1)}, bf16[512,1024]{1,0:T(8,128)(2,1)S(1)}, u32[]{:S(2)}, u32[]{:S(2)}) collective-permute-start(bf16[512,1024]{1,0:T(8,128)(2,1)} %pad_maximum_fusion), channel_id=1, source_target_pairs={{0,2},{2,0},{1,3},{3,1},{4,6},{6,4},{5,7},{7,5},{8,10},{10,8},{9,1... | collective-permute-start | bytes 3145736 | tf_op jit(solution)/shard_map/ppermute | solution.py:230
  12.5 16.2 %collective-permute-start = (bf16[17,128,128]{2,1,0:T(8,128)(2,1)}, bf16[17,128,128]{2,1,0:T(8,128)(2,1)S(1)}, u32[]{:S(2)}, u32[]{:S(2)}) collective-permute-start(bf16[17,128,128]{2,1,0:T(8,128)(2,1)} %pad_maximum_fusion.1), channel_id=1, source_target_pairs={{0,1},{1,0},{2,3},{3,2},{4,5},{5,4},{6,7},{7,6},{8,9},{9,8},{10,11... | collective-permute-start | bytes 1671176 | tf_op jit(solution)/shard_map/ppermute | solution.py:230
  17.3 35.9 %collective-permute-start.4 = (bf16[32,128,128]{2,1,0:T(8,128)(2,1)}, bf16[32,128,128]{2,1,0:T(8,128)(2,1)S(1)}, u32[]{:S(2)}, u32[]{:S(2)}) collective-permute-start(bf16[32,128,128]{2,1,0:T(8,128)(2,1)} %constant_dynamic-slice_fusion.1), channel_id=1, source_target_pairs={{0,1},{1,0},{2,3},{3,2},{4,5},{5,4},{6,7},{7,6},{8,9},{9,8},{10,11... | collective-permute-start | bytes 3145736 | tf_op jit(solution)/shard_map/ppermute | solution.py:230
  17.3 2.8 %copy-start.6 = (bf16[512,1024]{1,0:T(8,128)(2,1)}, bf16[512,1024]{1,0:T(8,128)(2,1)S(1)}, u32[]{:S(2)}) copy-start(bf16[512,1024]{1,0:T(8,128)(2,1)S(1)} %collective-permute-done.2.skb.svb.refs_5_.refs_9_) | copy-start | bytes 3145732
  28.6 29.2 %copy-start.2 = (bf16[17,128,128]{2,1,0:T(8,128)(2,1)}, bf16[17,128,128]{2,1,0:T(8,128)(2,1)S(1)}, u32[]{:S(2)}) copy-start(bf16[17,128,128]{2,1,0:T(8,128)(2,1)S(1)} %collective-permute-done.refs_1_) | copy-start | bytes 1671172
  29.5 23.7 %collective-permute-start.5 = (bf16[16,128,128]{2,1,0:T(8,128)(2,1)}, bf16[16,128,128]{2,1,0:T(8,128)(2,1)}, u32[]{:S(2)}, u32[]{:S(2)}) collective-permute-start(bf16[16,128,128]{2,1,0:T(8,128)(2,1)} %slice.17), channel_id=1, source_target_pairs={{0,16},{16,0},{1,17},{17,1},{2,18},{18,2},{3,19},{19,3},{4,20},{20... | collective-permute-start | bytes 1572872 | tf_op jit(solution)/shard_map/ppermute | solution.py:230
  31.5 23.9 %collective-permute-start.9 = (bf16[16,128,128]{2,1,0:T(8,128)(2,1)}, bf16[16,128,128]{2,1,0:T(8,128)(2,1)S(1)}, u32[]{:S(2)}, u32[]{:S(2)}) collective-permute-start(bf16[16,128,128]{2,1,0:T(8,128)(2,1)} %slice.17), channel_id=1, source_target_pairs={{0,2},{2,0},{1,3},{3,1},{4,6},{6,4},{5,7},{7,5},{8,10},{10,8},{9,1... | collective-permute-start | bytes 1572872 | tf_op jit(solution)/shard_map/ppermute | solution.py:230
  33.9 23.9 %copy-start.7 = (s32[16,16]{1,0:T(8,128)S(1)}, s32[16,16]{1,0:T(8,128)}, u32[]{:S(2)}) copy-start(s32[16,16]{1,0:T(8,128)} %param.13) | copy-start | bytes 3076
  33.9 40.2 %collective-permute-start.6 = (bf16[33,128,128]{2,1,0:T(8,128)(2,1)}, bf16[33,128,128]{2,1,0:T(8,128)(2,1)S(1)}, u32[]{:S(2)}, u32[]{:S(2)}) collective-permute-start(bf16[33,128,128]{2,1,0:T(8,128)(2,1)} %constant_dynamic-slice_fusion), channel_id=1, source_target_pairs={{0,1},{1,0},{2,3},{3,2},{4,5},{5,4},{6,7},{7,6},{8,9},{9,8},{10,11... | collective-permute-start | bytes 3244040 | tf_op jit(solution)/shard_map/ppermute | solution.py:230
  53.2 4.9 %collective-permute-start.10 = (bf16[32,128,128]{2,1,0:T(8,128)(2,1)S(1)}, bf16[32,128,128]{2,1,0:T(8,128)(2,1)}, u32[]{:S(2)}, u32[]{:S(2)}) collective-permute-start(bf16[32,128,128]{2,1,0:T(8,128)(2,1)S(1)} %collective-permute-done.4.refs_2_), channel_id=1, source_target_pairs={{0,2},{2,0},{1,3},{3,1},{4,6},{6,4},{5,7},{7,5},{8,10},{10,8},{9,1... | collective-permute-start | bytes 3145736 | tf_op jit(solution)/shard_map/ppermute | solution.py:230
  53.5 4.5 %collective-permute-start.11 = (bf16[16,128,128]{2,1,0:T(8,128)(2,1)}, bf16[16,128,128]{2,1,0:T(8,128)(2,1)}, u32[]{:S(2)}, u32[]{:S(2)}) collective-permute-start(bf16[16,128,128]{2,1,0:T(8,128)(2,1)} %collective-permute-done.5.refs_3_), channel_id=1, source_target_pairs={{0,2},{2,0},{1,3},{3,1},{4,6},{6,4},{5,7},{7,5},{8,10},{10,8},{9,1... | collective-permute-start | bytes 1572872 | tf_op jit(solution)/shard_map/ppermute | solution.py:230
  54.9 19.2 %collective-permute-start.8 = (bf16[16,128,128]{2,1,0:T(8,128)(2,1)}, bf16[16,128,128]{2,1,0:T(8,128)(2,1)}, u32[]{:S(2)}, u32[]{:S(2)}) collective-permute-start(bf16[16,128,128]{2,1,0:T(8,128)(2,1)} %get-tuple-element.23), channel_id=1, source_target_pairs={{0,16},{16,0},{1,17},{17,1},{2,18},{18,2},{3,19},{19,3},{4,20},{20... | collective-permute-start | bytes 1572872 | tf_op jit(solution)/shard_map/ppermute | solution.py:230
  55.4 0.8 copy-start.4
  56.2 24.3 %collective-permute-start.7 = (bf16[16,128,128]{2,1,0:T(8,128)(2,1)}, bf16[16,128,128]{2,1,0:T(8,128)(2,1)}, u32[]{:S(2)}, u32[]{:S(2)}) collective-permute-start(bf16[16,128,128]{2,1,0:T(8,128)(2,1)} %get-tuple-element.24), channel_id=1, source_target_pairs={{0,16},{16,0},{1,17},{17,1},{2,18},{18,2},{3,19},{19,3},{4,20},{20... | collective-permute-start | bytes 1572872 | tf_op jit(solution)/shard_map/ppermute | solution.py:230
  58.1 1.2 copy-start
  59.3 1.1 copy-start.3
  60.4 1.0 copy-start.5
  61.4 24.6 %copy-start.1 = (bf16[256,2048]{1,0:T(8,128)(2,1)S(1)}, bf16[256,2048]{1,0:T(8,128)(2,1)}, u32[]{:S(2)}) copy-start(bf16[256,2048]{1,0:T(8,128)(2,1)} %late_attention.1.x_ref) | copy-start | bytes 3145732
  81.5 4.5 %collective-permute-start.12 = (bf16[32,128,128]{2,1,0:T(8,128)(2,1)}, bf16[32,128,128]{2,1,0:T(8,128)(2,1)S(1)}, u32[]{:S(2)}, u32[]{:S(2)}) collective-permute-start(bf16[32,128,128]{2,1,0:T(8,128)(2,1)} %slice.20), channel_id=1, source_target_pairs={{0,2},{2,0},{1,3},{3,1},{4,6},{6,4},{5,7},{7,5},{8,10},{10,8},{9,1... | collective-permute-start | bytes 3145736 | tf_op jit(solution)/shard_map/ppermute | solution.py:230
  81.5 3.4 %collective-permute-start.13 = (bf16[16,128,128]{2,1,0:T(8,128)(2,1)}, bf16[16,128,128]{2,1,0:T(8,128)(2,1)}, u32[]{:S(2)}, u32[]{:S(2)}) collective-permute-start(bf16[16,128,128]{2,1,0:T(8,128)(2,1)} %collective-permute-done.7.refs_2_), channel_id=1, source_target_pairs={{0,2},{2,0},{1,3},{3,1},{4,6},{6,4},{5,7},{7,5},{8,10},{10,8},{9,1... | collective-permute-start | bytes 1572872 | tf_op jit(solution)/shard_map/ppermute | solution.py:230
  82.0 4.0 %collective-permute-start.14 = (bf16[16,128,128]{2,1,0:T(8,128)(2,1)}, bf16[16,128,128]{2,1,0:T(8,128)(2,1)}, u32[]{:S(2)}, u32[]{:S(2)}) collective-permute-start(bf16[16,128,128]{2,1,0:T(8,128)(2,1)} %collective-permute-done.8.refs_3_), channel_id=1, source_target_pairs={{0,2},{2,0},{1,3},{3,1},{4,6},{6,4},{5,7},{7,5},{8,10},{10,8},{9,1... | collective-permute-start | bytes 1572872 | tf_op jit(solution)/shard_map/ppermute | solution.py:230
Sparse Core Ops, SparseCore 0:
  98.8 76.1 reduce-scatter.1

commit v3 on v2

--- a/solution.py
+++ b/solution.py
@@ -11,8 +11,8 @@
 HD = 128
 FLOOR = -1e30
 TILE = 768
-STEP_COLS = 8
-EXTRA = 1
+STEP_COLS = 16
+EXTRA = 3
 
 
 def in_hbm(value):
@@ -86,14 +86,13 @@
 def attention(my_seq, q, own, peer, first, count, earlier=None):
     rows, width = q.shape
     ck, sk, cv, sv = own
-    pck, ps, pcv = peer
+    pck, psk, pcv, psv = peer
     cache_rows = ck.shape[0]
     qspec = pl.BlockSpec((rows, 2 * HD), lambda g, s: (0, g + first))
     cspec = pl.BlockSpec((cache_rows, HD), lambda g, s: (0, g + first))
     nspec = pl.BlockSpec((rows, HD), lambda g, s: (0, g + first))
-    vspec = pl.BlockSpec((rows, HD), lambda g, s: (1, g + first))
-    args = [q, ck, sk, pck, ps, cv, sv, pcv, ps]
-    specs = [qspec, cspec, nspec, cspec, nspec, cspec, nspec, cspec, vspec]
+    args = [q, ck, sk, pck, psk, cv, sv, pcv, psv]
+    specs = [qspec, cspec, nspec, cspec, nspec, cspec, nspec, cspec, nspec]
     body = attention_body
     aliases = {}
     if earlier is not None:
@@ -119,13 +118,13 @@
     )(my_seq, *[in_hbm(a) for a in args])
 
 
-def projection_body(sources, kept, has_acc, table_ref, rows_ref, x_ref, *refs):
+def projection_body(sources, kept, has_acc, table_ref, rows_ref, x_hbm, *refs):
     n_pieces = 1 + max(piece for row in sources for piece, _, _ in row)
     pieces = refs[:n_pieces]
     refs = refs[n_pieces:]
     if has_acc:
         acc_hbm, refs = refs[0], refs[1:]
-    out_ref, held, sems, stage, out_sems = refs[:5]
+    out_ref, held, sems, stage, out_sems, x_ref, x_sem = refs[:7]
     slots = len(sources[0]) * kept
     empty = len(sources) * slots
     row_ids = [rows_ref[i] for i in range(len(sources))]
@@ -140,13 +139,15 @@
                     sems.at[i, j],
                 )
             )
+    x_copy = pltpu.make_async_copy(x_hbm, x_ref, x_sem)
+    x_copy.start()
     for copy in copies:
         copy.start()
     n_steps = table_ref.shape[1] // STEP_COLS
     span = STEP_COLS * HD
 
     def fill(step):
-        acc_ref, acc_sems = refs[5:]
+        acc_ref, acc_sems = refs[7:]
         where = pl.ds(pl.multiple_of(step * span, span), span)
         return pltpu.make_async_copy(acc_hbm.at[:, where], acc_ref.at[step], acc_sems.at[step])
 
@@ -154,6 +155,7 @@
         for step in range(n_steps):
             fill(step).start()
     held[empty] = jnp.zeros(held.shape[1:], held.dtype)
+    x_copy.wait()
     for copy in copies:
         copy.wait()
     x = jnp.concatenate([x_ref[:, pl.ds(pl.multiple_of(r * HD, HD), HD)] for r in row_ids], axis=1)
@@ -185,7 +187,7 @@
             value = jnp.dot(x, jnp.concatenate(sides, axis=1), preferred_element_type=jnp.float32)
             where = slice(2 * pair * HD, 2 * (pair + 1) * HD)
             if has_acc:
-                value = value + refs[5][step, :, where]
+                value = value + refs[7][step, :, where]
             stage[slot, :, where] = value.astype(out_ref.dtype)
         drain(slot, step).start()
         return carry
@@ -202,28 +204,28 @@
     slots = len(sources[0]) * kept
     shape = (tokens, col_blocks * HD)
     smem = pl.BlockSpec(memory_space=pltpu.SMEM)
-    vmem = pl.BlockSpec(memory_space=pltpu.VMEM)
     hbm = pl.BlockSpec(memory_space=pl.ANY)
     scratch = [
         pltpu.VMEM((n_rows * slots + 1, HD, HD), jnp.bfloat16),
         pltpu.SemaphoreType.DMA((n_rows, len(sources[0]))),
     ]
     span = STEP_COLS * HD
-    dtype = jnp.bfloat16 if last else jnp.float32
+    dtype = jnp.bfloat16
     scratch += [pltpu.VMEM((2, tokens, span), dtype), pltpu.SemaphoreType.DMA((2,))]
+    scratch += [pltpu.VMEM((tokens, width), x.dtype), pltpu.SemaphoreType.DMA(())]
     if acc is not None:
         n_steps = col_blocks // STEP_COLS
-        scratch += [pltpu.VMEM((n_steps, tokens, span), jnp.float32), pltpu.SemaphoreType.DMA((n_steps,))]
+        scratch += [pltpu.VMEM((n_steps, tokens, span), dtype), pltpu.SemaphoreType.DMA((n_steps,))]
     return pl.pallas_call(
         functools.partial(projection_body, sources, kept, acc is not None),
         out_shape=pltpu.HBM(shape, dtype),
-        in_specs=[smem, smem, vmem] + [hbm] * len(pieces) + ([hbm] if acc is not None else []),
+        in_specs=[smem, smem, hbm] + [hbm] * len(pieces) + ([hbm] if acc is not None else []),
         out_specs=hbm,
         scratch_shapes=scratch,
         compiler_params=pltpu.CompilerParams(vmem_limit_bytes=28 << 20),
         cost_estimate=pl.CostEstimate(flops=1, transcendentals=0, bytes_accessed=1),
         name="projection" if last else "early_projection",
-    )(table, row_ids, x, in_hbm(pieces[0]), *pieces[1:], *(() if acc is None else (in_hbm(acc),)))
+    )(table, row_ids, in_hbm(x), in_hbm(pieces[0]), *[p if last else in_hbm(p) for p in pieces[1:]], *(() if acc is None else (in_hbm(acc),)))
 
 
 def swap(value, axis):
@@ -236,7 +238,7 @@
 
 def peer_side(own):
     ck, sk, cv, sv = own
-    return [swap(ck, "seq"), swap(jnp.concatenate([sk, sv], axis=0), "seq"), swap(cv, "seq")]
+    return [swap(a, "seq") for a in (ck, sk, cv, sv)]
 
 
 def column_table(all_columns, col_blocks):
@@ -272,19 +274,21 @@
         )
         near1 = swap(jnp.concatenate([piece(relay, unit), carried[None]], axis=0), "dp")
         near2 = swap(piece(relay + unit, 2 * unit), "dp")
-        shared = swap(piece(half, 2 * unit, EXTRA), "dp")
         peer = peer_side(own)
+        shared, peer[0] = lax.optimization_barrier((piece(half, 2 * unit, EXTRA), peer[0]))
+        shared = swap(shared, "dp")
         attended = attention(seq_one, q, own, peer, 0, soon)
         near1, attended = lax.optimization_barrier((near1, attended))
         peer_columns = near1[unit * kept, :row_blocks, :kept].astype(jnp.int32)
         table = column_table(jnp.stack([block_columns, peer_columns]), col_blocks)
-        far1 = swap(near1[: unit * kept], "groups")
-        near1_other = swap(near1[: unit * kept], "seq")
-        attended = attention(seq_one, q, own, peer, soon, heads - soon, attended)
+        far1 = swap(near1, "groups")
+        near1_other = swap(near1, "seq")
+        attended = attention(seq_one, q, own, peer, soon, heads - 2 * soon, attended)
         near2, far1, attended = lax.optimization_barrier((near2, far1, attended))
         far2, far3 = [swap(near2[i * unit * kept : (i + 1) * unit * kept], "groups") for i in range(2)]
         near2_other = swap(near2, "seq")
         far1_other = swap(far1, "seq")
+        attended = attention(seq_one, q, own, peer, heads - soon, soon, attended)
         other = 8 * unit * (1 - my_seq)
 
         def stage(plan, acc, last):
@@ -312,7 +316,7 @@
             False,
         )
         shared, far2, far3, early = lax.optimization_barrier((shared, far2, far3, early))
-        shared_other = swap(shared[: 2 * unit * kept], "seq")
+        shared_other = swap(shared, "seq")
         far2_other = swap(far2, "seq")
         far3_other = swap(far3, "seq")
         partial_value = stage(

time: 182 us -> 177 us (0.973)
  local copies, waits for them, and re-layouts: 13.2 us -> 8.9 us
  starting transfers between devices: 10 us -> 13.3 us
  other arithmetic: 4.11 us -> 1.69 us
    ppermute x15 -> x16, waiting for transfers between devices: 15.7 us -> 12.1 us  [swap(): return lax.ppermute(value, axis, [(0, 1), (1, 0)])]
    ppermute x15 -> x16, starting transfers between devices: 10 us -> 13.3 us  [swap(): return lax.ppermute(value, axis, [(0, 1), (1, 0)])]
    unnamed x16 -> x8, local copies, waits for them, and re-layouts: 4.13 us -> 1.54 us
    pallas_call x2, Pallas kernels: 23.9 us -> 21.4 us  [projection(): pl.pallas_call(functools.partial(projection_body, sources, kept, acc is n...]
    concatenate x1 -> x0, other arithmetic: 2.24 us -> none  [peer_side(): jnp.concatenate([sk, sv], axis=0)]
    pallas_call x2 -> x3, Pallas kernels: 25.2 us -> 27.3 us  [attention(): pl.pallas_call(body, out_shape=pltpu.HBM((rows, width), jnp.bfloat16), gr...]
    reduce_scatter x1, waiting for transfers between devices: 76.3 us -> 78.4 us  [shards(): lax.psum_scatter(partial_value, 'tensor', scatter_dimension=1, tiled=True)]
    slice x2 -> x0, local copies, waits for them, and re-layouts: 1.94 us -> none  [the longest x1 1.04 us: shards(): shared_other = swap(shared[:2 * unit * kept], 'seq')]
  transfers between devices with their start and end apart: 16 -> 17, of which waited for: 7 -> 8; matrix products, arithmetic and copies ran while one was open for 7% -> 5% of each run, Pallas kernels for 20% -> 22%
where the time goes in v3:
time: 177 us
  waiting for transfers between devices  90.5 us (51%)
  Pallas kernels  48.7 us (28%)
  between operations  13.5 us (8%)
  starting transfers between devices  13.3 us (8%)
  local copies, waits for them, and re-layouts  8.9 us (5%)
    reduce_scatter x1, waiting for transfers between devices, shards(): lax.psum_scatter(partial_value, 'tensor', scatter_dimension=1, tiled=True)  78.4 us
    pallas_call x3, Pallas kernels, attention(): pl.pallas_call(body, out_shape=pltpu.HBM((rows, width), jnp.bfloat16), gr...  27.3 us
    pallas_call x2, Pallas kernels, projection(): pl.pallas_call(functools.partial(projection_body, sources, kept, acc is n...  21.4 us
    ppermute x16, starting transfers between devices, swap(): return lax.ppermute(value, axis, [(0, 1), (1, 0)])  13.3 us
    ppermute x16, waiting for transfers between devices, swap(): return lax.ppermute(value, axis, [(0, 1), (1, 0)])  12.1 us
    dynamic_slice x3, local copies, waits for them, and re-layouts, piece(): return lax.dynamic_slice_in_dim(flat, start * kept, count * kept + more, 0)  4.85 us
  transfers between devices with their start and end apart: 17, of which 8 were waited for; matrix products, arithmetic and copies ran while one was open for 5% of the time, Pallas kernels for 22%

profile of v3, /device:TPU:0, one launch (start us, length us, event | category | flops | bytes accessed | tf_op | source)
XLA Modules:
  0.0 176.6 jit_solution(15308806865863206233)
XLA Ops:
  6.5 0.5 collective-permute-start.1
  7.0 0.7 convert_element_type.9
  7.8 1.1 constant_dynamic-slice_fusion.2
  8.9 3.0 %collective-permute-start = (bf16[17,128,128]{2,1,0:T(8,128)(2,1)S(1)}, bf16[17,128,128]{2,1,0:T(8,128)(2,1)}, u32[]{:S(2)}, u32[]{:S(2)}) collective-permute-start(bf16[17,128,128]{2,1,0:T(8,128)(2,1)S(1)} %pad_maximum_fusion), channel_id=1, source_target_pairs={{0,1},{1,0},{2,3},{3,2},{4,5},{5,4},{6,7},{7,6},{8,9},{9,8},{10,11... | collective-permute-start | bytes 1671176 | tf_op jit(solution)/shard_map/ppermute | solution.py:232
  11.9 0.5 collective-permute-start.4
  12.4 1.3 constant_dynamic-slice_fusion
  13.7 2.5 %collective-permute-start.5 = (bf16[32,128,128]{2,1,0:T(8,128)(2,1)S(1)}, bf16[32,128,128]{2,1,0:T(8,128)(2,1)}, u32[]{:S(2)}, u32[]{:S(2)}) collective-permute-start(bf16[32,128,128]{2,1,0:T(8,128)(2,1)S(1)} %constant_dynamic-slice_fusion), channel_id=1, source_target_pairs={{0,1},{1,0},{2,3},{3,2},{4,5},{5,4},{6,7},{7,6},{8,9},{9,8},{10,11... | collective-permute-start | bytes 3145736 | tf_op jit(solution)/shard_map/ppermute | solution.py:232
  16.2 2.5 %constant_dynamic-slice_fusion.1 = bf16[35,128,128]{2,1,0:T(8,128)(2,1)} fusion(bf16[256,128,128]{2,1,0:T(8,128)(2,1)} %bitcast.29, s32[]{:T(128)S(6)} %select_n.14), kind=kLoop, calls=%fused_computation.8 | loop fusion | bytes 2293764 | tf_op jit(solution)/shard_map/dynamic_slice | solution.py:268
  18.7 0.5 collective-permute-done.2.skb.refs_5_
  19.2 0.7 collective-permute-done.4.svb.refs_9_
  19.9 0.2 collective-permute-done.3.cvb.refs_8_
  20.1 0.6 copy-done.1
  20.7 7.4 %attention.1.refs_10_ = bf16[256,2048]{1,0:T(8,128)(2,1)} custom-call(s32[1]{0:T(128)} %bitcast.3.seq_ref.refs_0_, bf16[256,2048]{1,0:T(8,128)(2,1)} %bitcast.40, bf16[1792,1024]{1,0:T(8,128)(2,1)} %bitcast.33, bf16[256,1024]{1,0:T(8,128)(2,1)} %bitcast.44, bf16[1792,1024]{1,0:T(8,128)(2,1)} %collective-permute-done.1.ckb.refs_4_, ...), custom_call_target="tpu_custom_call" | custom-call | flops 1 | bytes 1 | tf_op jit(solution)/shard_map/attention/pallas_call | solution.py:103
  28.1 2.4 %collective-permute-start.6 = (bf16[17,128,128]{2,1,0:T(8,128)(2,1)}, bf16[17,128,128]{2,1,0:T(8,128)(2,1)}, u32[]{:S(2)}, u32[]{:S(2)}) collective-permute-start(bf16[17,128,128]{2,1,0:T(8,128)(2,1)} %collective-permute-done.refs_1_), channel_id=1, source_target_pairs={{0,16},{16,0},{1,17},{17,1},{2,18},{18,2},{3,19},{19,3},{4,20},{20... | collective-permute-start | bytes 1671176 | tf_op jit(solution)/shard_map/ppermute | solution.py:232
  30.5 1.5 collective-permute-start.7
  31.9 12.6 %late_attention.2.refs_10_ = bf16[256,2048]{1,0:T(8,128)(2,1)} custom-call(s32[1]{0:T(128)} %bitcast.3.seq_ref.refs_0_, bf16[256,2048]{1,0:T(8,128)(2,1)} %bitcast.41, bf16[1792,1024]{1,0:T(8,128)(2,1)} %bitcast.34, bf16[256,1024]{1,0:T(8,128)(2,1)} %bitcast.45, ...), custom_call_target="tpu_custom_call", output_to_operand_aliasing={{}: (10, {})} | custom-call | flops 1 | bytes 1 | tf_op jit(solution)/shard_map/late_attention/pallas_call | solution.py:103
  44.5 3.4 %collective-permute-done.5.refs_2_ = bf16[32,128,128]{2,1,0:T(8,128)(2,1)} collective-permute-done((bf16[32,128,128]{2,1,0:T(8,128)(2,1)S(1)}, bf16[32,128,128]{2,1,0:T(8,128)(2,1)}, u32[]{:S(2)}, u32[]{:S(2)}) %collective-permute-start.5) | collective-permute-done | bytes 1048608 | tf_op jit(solution)/shard_map/ppermute | solution.py:232
  47.9 2.3 %fusion = (bf16[16,128,128]{2,1,0:T(8,128)(2,1)}, bf16[16,128,128]{2,1,0:T(8,128)(2,1)}) fusion(bf16[32,128,128]{2,1,0:T(8,128)(2,1)} %collective-permute-done.5.refs_2_), kind=kLoop, calls=%fused_computation.11 | loop fusion | bytes 2097152 | tf_op jit(solution)/shard_map/slice | solution.py:288
  50.3 2.1 %collective-permute-start.8 = (bf16[16,128,128]{2,1,0:T(8,128)(2,1)}, bf16[16,128,128]{2,1,0:T(8,128)(2,1)S(1)}, u32[]{:S(2)}, u32[]{:S(2)}) collective-permute-start(bf16[16,128,128]{2,1,0:T(8,128)(2,1)} %get-tuple-element.28), channel_id=1, source_target_pairs={{0,16},{16,0},{1,17},{17,1},{2,18},{18,2},{3,19},{19,3},{4,20},{20... | collective-permute-start | bytes 1572872 | tf_op jit(solution)/shard_map/ppermute | solution.py:232
  52.4 0.2 collective-permute-start.12
  52.7 0.1 stack.80.rows_ref
  52.8 0.7 slice_convert_fusion
  53.5 0.2 select_reduce_fusion.table_ref
  53.6 7.4 %late_attention.3.x_hbm = bf16[256,2048]{1,0:T(8,128)(2,1)} custom-call(s32[1]{0:T(128)} %bitcast.3.seq_ref.refs_0_, bf16[256,2048]{1,0:T(8,128)(2,1)} %bitcast.42, bf16[1792,1024]{1,0:T(8,128)(2,1)} %bitcast.35, bf16[256,1024]{1,0:T(8,128)(2,1)} %bitcast.46, bf16[1792,1024]{1,0:T(8,128)(2,1)} %collective-permute-done.1.ckb.refs_4_, ...), custom_call_target="tpu_custom_call", output_to_operand_aliasing={{}: (10, {})} | custom-call | flops 1 | bytes 1 | tf_op jit(solution)/shard_map/late_attention/pallas_call | solution.py:103
  61.1 1.0 copy-done.2
  62.0 10.8 %early_projection.1.refs_7_ = bf16[256,8192]{1,0:T(8,128)(2,1)} custom-call(s32[16,64]{1,0:T(8,128)S(1)} %select_reduce_fusion.table_ref, s32[8]{0:T(128)S(1)} %stack.80.rows_ref, bf16[256,2048]{1,0:T(8,128)(2,1)} %late_attention.3.x_hbm, bf16[256,128,128]{2,1,0:T(8,128)(2,1)} %bitcast.30, bf16[17,128,128]{2,1,0:T(8,128)(2,1)} %collective-permute-done.refs_1_, ...), custom_call_target="tpu_custom_call" | custom-call | flops 1 | bytes 1 | tf_op jit(solution)/shard_map/early_projection/pallas_call | solution.py:219
  72.9 3.5 %collective-permute-done.9.refs_3_ = bf16[16,128,128]{2,1,0:T(8,128)(2,1)S(1)} collective-permute-done((bf16[16,128,128]{2,1,0:T(8,128)(2,1)}, bf16[16,128,128]{2,1,0:T(8,128)(2,1)S(1)}, u32[]{:S(2)}, u32[]{:S(2)}) %collective-permute-start.9) | collective-permute-done | bytes 524320 | tf_op jit(solution)/shard_map/ppermute | solution.py:232
  76.4 0.5 collective-permute-start.14
  77.0 2.7 %collective-permute-done.14.refs_5_ = bf16[16,128,128]{2,1,0:T(8,128)(2,1)} collective-permute-done((bf16[16,128,128]{2,1,0:T(8,128)(2,1)S(1)}, bf16[16,128,128]{2,1,0:T(8,128)(2,1)}, u32[]{:S(2)}, u32[]{:S(2)}) %collective-permute-start.14) | collective-permute-done | bytes 524320 | tf_op jit(solution)/shard_map/ppermute | solution.py:232
  79.7 1.0 collective-permute-done.15.refs_6_
  80.7 10.6 %projection.1 = bf16[256,8192]{1,0:T(8,128)(2,1)} custom-call(s32[16,64]{1,0:T(8,128)S(1)} %select_reduce_fusion.table_ref, s32[8]{0:T(128)S(1)} %stack.71.rows_ref, bf16[256,2048]{1,0:T(8,128)(2,1)} %late_attention.3.x_hbm, bf16[256,128,128]{2,1,0:T(8,128)(2,1)} %bitcast.31, bf16[35,128,128]{2,1,0:T(8,128)(2,1)S(1)} %collective-permute-done.7.refs_1_, ...), custom_call_target="tpu_custom_call" | custom-call | flops 1 | bytes 1 | tf_op jit(solution)/shard_map/projection/pallas_call | solution.py:219
  91.3 78.4 %reduce-scatter.2.cloned.1.call-done = bf16[256,2048]{1,0:T(8,128)(2,1)} async-done(((bf16[256,8192]{1,0:T(8,128)(2,1)}), bf16[256,2048]{1,0:T(8,128)(2,1)}) %reduce-scatter.2.cloned.1.call-update) | async-done | bytes 1048592 | tf_op jit(solution)/shard_map/reduce_scatter | solution.py:344
  (30 shorter events, 0.4 us)
Async XLA Ops:
  6.5 163.2 %reduce-scatter.2.cloned.1.call-start = ((), (), s32[]{:S(2)}) async-start(), calls=%async_computation.1 | async-start | bytes 5242880 | tf_op jit(solution)/shard_map/reduce_scatter | solution.py:344
  6.5 7.2 %collective-permute-start.1 = (bf16[1792,1024]{1,0:T(8,128)(2,1)}, bf16[1792,1024]{1,0:T(8,128)(2,1)}, u32[]{:S(2)}, u32[]{:S(2)}) collective-permute-start(bf16[1792,1024]{1,0:T(8,128)(2,1)} %bitcast.32), channel_id=1, source_target_pairs={{0,2},{2,0},{1,3},{3,1},{4,6},{6,4},{5,7},{7,5},{8,10},{10,8},{9,1... | collective-permute-start | bytes 11010056 | tf_op jit(solution)/shard_map/ppermute | solution.py:232
  7.0 13.1 %collective-permute-start.3 = (bf16[1792,1024]{1,0:T(8,128)(2,1)}, bf16[1792,1024]{1,0:T(8,128)(2,1)}, u32[]{:S(2)}, u32[]{:S(2)}) collective-permute-start(bf16[1792,1024]{1,0:T(8,128)(2,1)} %bitcast.36), channel_id=1, source_target_pairs={{0,2},{2,0},{1,3},{3,1},{4,6},{6,4},{5,7},{7,5},{8,10},{10,8},{9,1... | collective-permute-start | bytes 11010056 | tf_op jit(solution)/shard_map/ppermute | solution.py:232
  8.9 19.1 %collective-permute-start = (bf16[17,128,128]{2,1,0:T(8,128)(2,1)S(1)}, bf16[17,128,128]{2,1,0:T(8,128)(2,1)}, u32[]{:S(2)}, u32[]{:S(2)}) collective-permute-start(bf16[17,128,128]{2,1,0:T(8,128)(2,1)S(1)} %pad_maximum_fusion), channel_id=1, source_target_pairs={{0,1},{1,0},{2,3},{3,2},{4,5},{5,4},{6,7},{7,6},{8,9},{9,8},{10,11... | collective-permute-start | bytes 1671176 | tf_op jit(solution)/shard_map/ppermute | solution.py:232
  11.9 7.2 %collective-permute-start.2 = (bf16[256,1024]{1,0:T(8,128)(2,1)}, bf16[256,1024]{1,0:T(8,128)(2,1)S(1)}, u32[]{:S(2)}, u32[]{:S(2)}) collective-permute-start(bf16[256,1024]{1,0:T(8,128)(2,1)} %bitcast.43), channel_id=1, source_target_pairs={{0,2},{2,0},{1,3},{3,1},{4,6},{6,4},{5,7},{7,5},{8,10},{10,8},{9,1... | collective-permute-start | bytes 1572872 | tf_op jit(solution)/shard_map/ppermute | solution.py:232
  11.9 8.0 %collective-permute-start.4 = (bf16[256,1024]{1,0:T(8,128)(2,1)}, bf16[256,1024]{1,0:T(8,128)(2,1)S(1)}, u32[]{:S(2)}, u32[]{:S(2)}) collective-permute-start(bf16[256,1024]{1,0:T(8,128)(2,1)} %bitcast.47), channel_id=1, source_target_pairs={{0,2},{2,0},{1,3},{3,1},{4,6},{6,4},{5,7},{7,5},{8,10},{10,8},{9,1... | collective-permute-start | bytes 1572872 | tf_op jit(solution)/shard_map/ppermute | solution.py:232
  13.7 34.2 %collective-permute-start.5 = (bf16[32,128,128]{2,1,0:T(8,128)(2,1)S(1)}, bf16[32,128,128]{2,1,0:T(8,128)(2,1)}, u32[]{:S(2)}, u32[]{:S(2)}) collective-permute-start(bf16[32,128,128]{2,1,0:T(8,128)(2,1)S(1)} %constant_dynamic-slice_fusion), channel_id=1, source_target_pairs={{0,1},{1,0},{2,3},{3,2},{4,5},{5,4},{6,7},{7,6},{8,9},{9,8},{10,11... | collective-permute-start | bytes 3145736 | tf_op jit(solution)/shard_map/ppermute | solution.py:232
  19.2 1.0 copy-start
  19.9 0.8 copy-start.1
  28.0 25.4 %copy-start.3 = (s32[16,16]{1,0:T(8,128)S(1)}, s32[16,16]{1,0:T(8,128)}, u32[]{:S(2)}) copy-start(s32[16,16]{1,0:T(8,128)} %param.13) | copy-start | bytes 3076
  28.1 19.9 %collective-permute-start.6 = (bf16[17,128,128]{2,1,0:T(8,128)(2,1)}, bf16[17,128,128]{2,1,0:T(8,128)(2,1)}, u32[]{:S(2)}, u32[]{:S(2)}) collective-permute-start(bf16[17,128,128]{2,1,0:T(8,128)(2,1)} %collective-permute-done.refs_1_), channel_id=1, source_target_pairs={{0,16},{16,0},{1,17},{17,1},{2,18},{18,2},{3,19},{19,3},{4,20},{20... | collective-permute-start | bytes 1671176 | tf_op jit(solution)/shard_map/ppermute | solution.py:232
  30.5 21.9 %collective-permute-start.10 = (bf16[17,128,128]{2,1,0:T(8,128)(2,1)}, bf16[17,128,128]{2,1,0:T(8,128)(2,1)}, u32[]{:S(2)}, u32[]{:S(2)}) collective-permute-start(bf16[17,128,128]{2,1,0:T(8,128)(2,1)} %collective-permute-done.refs_1_), channel_id=1, source_target_pairs={{0,2},{2,0},{1,3},{3,1},{4,6},{6,4},{5,7},{7,5},{8,10},{10,8},{9,1... | collective-permute-start | bytes 1671176 | tf_op jit(solution)/shard_map/ppermute | solution.py:232
  30.5 45.9 %collective-permute-start.7 = (bf16[35,128,128]{2,1,0:T(8,128)(2,1)}, bf16[35,128,128]{2,1,0:T(8,128)(2,1)S(1)}, u32[]{:S(2)}, u32[]{:S(2)}) collective-permute-start(bf16[35,128,128]{2,1,0:T(8,128)(2,1)} %constant_dynamic-slice_fusion.1), channel_id=1, source_target_pairs={{0,1},{1,0},{2,3},{3,2},{4,5},{5,4},{6,7},{7,6},{8,9},{9,8},{10,11... | collective-permute-start | bytes 3440648 | tf_op jit(solution)/shard_map/ppermute | solution.py:232
  47.9 13.1 %collective-permute-start.11 = (bf16[32,128,128]{2,1,0:T(8,128)(2,1)}, bf16[32,128,128]{2,1,0:T(8,128)(2,1)S(1)}, u32[]{:S(2)}, u32[]{:S(2)}) collective-permute-start(bf16[32,128,128]{2,1,0:T(8,128)(2,1)} %collective-permute-done.5.refs_2_), channel_id=1, source_target_pairs={{0,2},{2,0},{1,3},{3,1},{4,6},{6,4},{5,7},{7,5},{8,10},{10,8},{9,1... | collective-permute-start | bytes 3145736 | tf_op jit(solution)/shard_map/ppermute | solution.py:232
  50.3 22.6 %collective-permute-start.8 = (bf16[16,128,128]{2,1,0:T(8,128)(2,1)}, bf16[16,128,128]{2,1,0:T(8,128)(2,1)S(1)}, u32[]{:S(2)}, u32[]{:S(2)}) collective-permute-start(bf16[16,128,128]{2,1,0:T(8,128)(2,1)} %get-tuple-element.28), channel_id=1, source_target_pairs={{0,16},{16,0},{1,17},{17,1},{2,18},{18,2},{3,19},{19,3},{4,20},{20... | collective-permute-start | bytes 1572872 | tf_op jit(solution)/shard_map/ppermute | solution.py:232
  52.4 24.0 %collective-permute-start.9 = (bf16[16,128,128]{2,1,0:T(8,128)(2,1)}, bf16[16,128,128]{2,1,0:T(8,128)(2,1)S(1)}, u32[]{:S(2)}, u32[]{:S(2)}) collective-permute-start(bf16[16,128,128]{2,1,0:T(8,128)(2,1)} %get-tuple-element.27), channel_id=1, source_target_pairs={{0,16},{16,0},{1,17},{17,1},{2,18},{18,2},{3,19},{19,3},{4,20},{20... | collective-permute-start | bytes 1572872 | tf_op jit(solution)/shard_map/ppermute | solution.py:232
  52.4 8.7 %collective-permute-start.12 = (bf16[17,128,128]{2,1,0:T(8,128)(2,1)}, bf16[17,128,128]{2,1,0:T(8,128)(2,1)}, u32[]{:S(2)}, u32[]{:S(2)}) collective-permute-start(bf16[17,128,128]{2,1,0:T(8,128)(2,1)} %collective-permute-done.6.refs_3_), channel_id=1, source_target_pairs={{0,2},{2,0},{1,3},{3,1},{4,6},{6,4},{5,7},{7,5},{8,10},{10,8},{9,1... | collective-permute-start | bytes 1671176 | tf_op jit(solution)/shard_map/ppermute | solution.py:232
  61.1 1.0 copy-start.2
  76.4 4.3 %collective-permute-start.13 = (bf16[35,128,128]{2,1,0:T(8,128)(2,1)S(1)}, bf16[35,128,128]{2,1,0:T(8,128)(2,1)S(1)}, u32[]{:S(2)}, u32[]{:S(2)}) collective-permute-start(bf16[35,128,128]{2,1,0:T(8,128)(2,1)S(1)} %collective-permute-done.7.refs_1_), channel_id=1, source_target_pairs={{0,2},{2,0},{1,3},{3,1},{4,6},{6,4},{5,7},{7,5},{8,10},{10,8},{9,1... | collective-permute-start | bytes 3440648 | tf_op jit(solution)/shard_map/ppermute | solution.py:232
  76.4 3.3 %collective-permute-start.14 = (bf16[16,128,128]{2,1,0:T(8,128)(2,1)S(1)}, bf16[16,128,128]{2,1,0:T(8,128)(2,1)}, u32[]{:S(2)}, u32[]{:S(2)}) collective-permute-start(bf16[16,128,128]{2,1,0:T(8,128)(2,1)S(1)} %collective-permute-done.8.refs_2_), channel_id=1, source_target_pairs={{0,2},{2,0},{1,3},{3,1},{4,6},{6,4},{5,7},{7,5},{8,10},{10,8},{9,1... | collective-permute-start | bytes 1572872 | tf_op jit(solution)/shard_map/ppermute | solution.py:232
  76.9 3.8 %collective-permute-start.15 = (bf16[16,128,128]{2,1,0:T(8,128)(2,1)S(1)}, bf16[16,128,128]{2,1,0:T(8,128)(2,1)}, u32[]{:S(2)}, u32[]{:S(2)}) collective-permute-start(bf16[16,128,128]{2,1,0:T(8,128)(2,1)S(1)} %collective-permute-done.9.refs_3_), channel_id=1, source_target_pairs={{0,2},{2,0},{1,3},{3,1},{4,6},{6,4},{5,7},{7,5},{8,10},{10,8},{9,1... | collective-permute-start | bytes 1572872 | tf_op jit(solution)/shard_map/ppermute | solution.py:232
Sparse Core Ops, SparseCore 0:
  91.5 78.2 reduce-scatter.1

commit v4 on v3

--- a/solution.py
+++ b/solution.py
@@ -118,17 +118,21 @@
     )(my_seq, *[in_hbm(a) for a in args])
 
 
-def projection_body(sources, kept, has_acc, table_ref, rows_ref, x_hbm, *refs):
+def projection_body(sources, kept, has_acc, split, n_steps, table_ref, rows_ref, cols_ref, x_hbm, *refs):
     n_pieces = 1 + max(piece for row in sources for piece, _, _ in row)
-    pieces = refs[:n_pieces]
-    refs = refs[n_pieces:]
+    pieces, refs = refs[:n_pieces], refs[n_pieces:]
     if has_acc:
         acc_hbm, refs = refs[0], refs[1:]
-    out_ref, held, sems, stage, out_sems, x_ref, x_sem = refs[:7]
+    n_outs = 2 * n_steps if split else 1
+    outs, refs = refs[:n_outs], refs[n_outs:]
+    held, sems, stage, out_sems, x_ref, x_sem = refs[:6]
     slots = len(sources[0]) * kept
     empty = len(sources) * slots
     row_ids = [rows_ref[i] for i in range(len(sources))]
-    copies = []
+    step_cols = stage.shape[2] // HD
+    span = step_cols * HD
+    tokens = stage.shape[1]
+    copies = [pltpu.make_async_copy(x_hbm, x_ref, x_sem)]
     for i, row in enumerate(sources):
         for j, (piece, offset, by_row) in enumerate(row):
             start = offset + row_ids[i] * kept if by_row else offset
@@ -139,45 +143,43 @@
                     sems.at[i, j],
                 )
             )
-    x_copy = pltpu.make_async_copy(x_hbm, x_ref, x_sem)
-    x_copy.start()
     for copy in copies:
         copy.start()
-    n_steps = table_ref.shape[1] // STEP_COLS
-    span = STEP_COLS * HD
-
-    def fill(step):
-        acc_ref, acc_sems = refs[7:]
-        where = pl.ds(pl.multiple_of(step * span, span), span)
-        return pltpu.make_async_copy(acc_hbm.at[:, where], acc_ref.at[step], acc_sems.at[step])
-
+    where = [pl.ds(pl.multiple_of(cols_ref[step] * HD, span), span) for step in range(n_steps)]
+    fills = []
     if has_acc:
+        acc_ref, acc_sems = refs[6:]
         for step in range(n_steps):
-            fill(step).start()
+            fills.append(pltpu.make_async_copy(acc_hbm.at[:, where[step]], acc_ref.at[step], acc_sems.at[step]))
+            fills[step].start()
     held[empty] = jnp.zeros(held.shape[1:], held.dtype)
-    x_copy.wait()
     for copy in copies:
         copy.wait()
     x = jnp.concatenate([x_ref[:, pl.ds(pl.multiple_of(r * HD, HD), HD)] for r in row_ids], axis=1)
-
-    def drain(slot, step):
-        return pltpu.make_async_copy(
-            stage.at[slot], out_ref.at[:, pl.ds(pl.multiple_of(step * span, span), span)], out_sems.at[slot]
-        )
-
-    def one_step(step, carry):
+    drains = []
+    for step in range(n_steps):
         slot = step % 2
-
-        @pl.when(step >= 2)
-        def _():
-            drain(slot, step - 2).wait()
-
+        if split:
+            half = tokens // 2
+            drains.append(
+                [
+                    pltpu.make_async_copy(
+                        stage.at[slot, pl.ds(side * half, half)], outs[2 * step + side], out_sems.at[slot, side]
+                    )
+                    for side in range(2)
+                ]
+            )
+        else:
+            drains.append([pltpu.make_async_copy(stage.at[slot], outs[0].at[:, where[step]], out_sems.at[slot, 0])])
+        if step >= 2:
+            for copy in drains[step - 2]:
+                copy.wait()
         if has_acc:
-            fill(step).wait()
-        for pair in range(STEP_COLS // 2):
+            fills[step].wait()
+        for pair in range(step_cols // 2):
             sides = []
             for side in range(2):
-                col = step * STEP_COLS + 2 * pair + side
+                col = cols_ref[step] + 2 * pair + side
                 sides.append(
                     jnp.concatenate(
                         [held[jnp.minimum(table_ref[r, col] + i * slots, empty)] for i, r in enumerate(row_ids)],
@@ -185,47 +187,81 @@
                     )
                 )
             value = jnp.dot(x, jnp.concatenate(sides, axis=1), preferred_element_type=jnp.float32)
-            where = slice(2 * pair * HD, 2 * (pair + 1) * HD)
+            lanes = slice(2 * pair * HD, 2 * (pair + 1) * HD)
             if has_acc:
-                value = value + refs[7][step, :, where]
-            stage[slot, :, where] = value.astype(out_ref.dtype)
-        drain(slot, step).start()
-        return carry
-
-    lax.fori_loop(0, n_steps, one_step, 0)
+                value = value + acc_ref[step, :, lanes]
+            stage[slot, :, lanes] = value.astype(stage.dtype)
+        for copy in drains[step]:
+            copy.start()
     for step in range(max(0, n_steps - 2), n_steps):
-        drain(step % 2, step).wait()
-
-
-def projection(x, table, row_ids, sources, pieces, kept, acc, last):
+        for copy in drains[step]:
+            copy.wait()
+
+
+def projection(x, table, row_ids, sources, pieces, kept, acc=None, columns=None):
     tokens, width = x.shape
     col_blocks = table.shape[1]
     n_rows = len(sources)
     slots = len(sources[0]) * kept
-    shape = (tokens, col_blocks * HD)
+    split = columns is not None
+    if split:
+        step_cols, n_steps = width // HD, columns.shape[0]
+        out_shape = [pltpu.HBM((tokens // 2, width), x.dtype)] * (2 * n_steps)
+    else:
+        step_cols = min(STEP_COLS, col_blocks)
+        n_steps = col_blocks // step_cols
+        columns = jnp.arange(n_steps, dtype=jnp.int32) * step_cols
+        out_shape = [pltpu.HBM((tokens, col_blocks * HD), x.dtype)]
+    span = step_cols * HD
     smem = pl.BlockSpec(memory_space=pltpu.SMEM)
     hbm = pl.BlockSpec(memory_space=pl.ANY)
     scratch = [
-        pltpu.VMEM((n_rows * slots + 1, HD, HD), jnp.bfloat16),
+        pltpu.VMEM((n_rows * slots + 1, HD, HD), x.dtype),
         pltpu.SemaphoreType.DMA((n_rows, len(sources[0]))),
+        pltpu.VMEM((2, tokens, span), x.dtype),
+        pltpu.SemaphoreType.DMA((2, 2)),
+        pltpu.VMEM((tokens, width), x.dtype),
+        pltpu.SemaphoreType.DMA(()),
     ]
-    span = STEP_COLS * HD
-    dtype = jnp.bfloat16
-    scratch += [pltpu.VMEM((2, tokens, span), dtype), pltpu.SemaphoreType.DMA((2,))]
-    scratch += [pltpu.VMEM((tokens, width), x.dtype), pltpu.SemaphoreType.DMA(())]
     if acc is not None:
-        n_steps = col_blocks // STEP_COLS
-        scratch += [pltpu.VMEM((n_steps, tokens, span), dtype), pltpu.SemaphoreType.DMA((n_steps,))]
+        scratch += [pltpu.VMEM((n_steps, tokens, span), x.dtype), pltpu.SemaphoreType.DMA((n_steps,))]
     return pl.pallas_call(
-        functools.partial(projection_body, sources, kept, acc is not None),
-        out_shape=pltpu.HBM(shape, dtype),
-        in_specs=[smem, smem, hbm] + [hbm] * len(pieces) + ([hbm] if acc is not None else []),
-        out_specs=hbm,
+        functools.partial(projection_body, sources, kept, acc is not None, split, n_steps),
+        out_shape=out_shape,
+        in_specs=[smem, smem, smem, hbm] + [hbm] * len(pieces) + ([hbm] if acc is not None else []),
+        out_specs=[hbm] * len(out_shape),
         scratch_shapes=scratch,
         compiler_params=pltpu.CompilerParams(vmem_limit_bytes=28 << 20),
         cost_estimate=pl.CostEstimate(flops=1, transcendentals=0, bytes_accessed=1),
-        name="projection" if last else "early_projection",
-    )(table, row_ids, in_hbm(x), in_hbm(pieces[0]), *[p if last else in_hbm(p) for p in pieces[1:]], *(() if acc is None else (in_hbm(acc),)))
+        name="projection" if split else "early_projection",
+    )(
+        table,
+        row_ids,
+        columns,
+        in_hbm(x),
+        in_hbm(pieces[0]),
+        *[p if split else in_hbm(p) for p in pieces[1:]],
+        *(() if acc is None else (in_hbm(acc),)),
+    )
+
+
+def add(*values):
+    return sum(v.astype(jnp.float32) for v in values).astype(values[0].dtype)
+
+
+def line_scatter(parts, n):
+    arrived = [None, None]
+    for step in range(1, n):
+        for half in range(2):
+            up, down = parts(n - step)[half], parts(step)[half]
+            if arrived[half] is not None:
+                from_below, from_above = lax.optimization_barrier(arrived[half])
+                up, down = add(up, from_below), add(down, from_above)
+            arrived[half] = (
+                lax.ppermute(up, "tensor", [(i, i + 1) for i in range(step)]),
+                lax.ppermute(down, "tensor", [(i + 1, i) for i in range(n - 1 - step, n - 1)]),
+            )
+    return jnp.concatenate([add(parts(0)[half], *arrived[half]) for half in range(2)], axis=0)
 
 
 def swap(value, axis):
@@ -291,19 +327,19 @@
         attended = attention(seq_one, q, own, peer, heads - soon, soon, attended)
         other = 8 * unit * (1 - my_seq)
 
-        def stage(plan, acc, last):
+        def stage(plan, acc=None, columns=None):
             row_list, sources, pieces = [], [], [flat]
             for start, count, value in plan:
                 for i in range(count):
                     row_list.append(start + i)
                     sources.append(((0, 0, True), (len(pieces), i * kept, False)))
                 pieces.append(value)
-            return projection(attended, table, jnp.stack(row_list), tuple(sources), pieces, kept, acc, last)
+            return projection(attended, table, jnp.stack(row_list), tuple(sources), pieces, kept, acc, columns)
 
         def relayed(base, group):
             return base + unit * (2 + 3 * group)
 
-        early = stage(
+        (early,) = stage(
             (
                 (relayed(half, groups), unit, near1),
                 (relayed(half, groups) + unit, 2 * unit, near2),
@@ -312,25 +348,29 @@
                 (relayed(other, groups) + unit, 2 * unit, near2_other),
                 (relayed(other, 1 - groups), unit, far1_other),
             ),
-            None,
-            False,
         )
         shared, far2, far3, early = lax.optimization_barrier((shared, far2, far3, early))
         shared_other = swap(shared, "seq")
         far2_other = swap(far2, "seq")
         far3_other = swap(far3, "seq")
-        partial_value = stage(
-            (
-                (half, 2 * unit, shared),
-                (relayed(half, 1 - groups) + unit, unit, far2),
-                (relayed(half, 1 - groups) + 2 * unit, unit, far3),
-                (other, 2 * unit, shared_other),
-                (relayed(other, 1 - groups) + unit, unit, far2_other),
-                (relayed(other, 1 - groups) + 2 * unit, unit, far3_other),
-            ),
-            early,
-            True,
-        )
+        plan = (
+            (half, 2 * unit, shared),
+            (relayed(half, 1 - groups) + unit, unit, far2),
+            (relayed(half, 1 - groups) + 2 * unit, unit, far3),
+            (other, 2 * unit, shared_other),
+            (relayed(other, 1 - groups) + unit, unit, far2_other),
+            (relayed(other, 1 - groups) + 2 * unit, unit, far3_other),
+        )
+        n = mesh.shape["tensor"]
+        place = lax.axis_index("tensor")
+        sums = {}
+        for group in (sorted({n - 1, 1}), sorted(set(range(n)) - {n - 1, 1})):
+            if group:
+                columns = jnp.stack([(place + j) % n * row_blocks for j in group])
+                found = stage(plan, early, columns)
+                for i, j in enumerate(group):
+                    sums[j] = found[2 * i : 2 * i + 2]
+        return line_scatter(lambda j: sums[j], n)[None]
     else:
         dp = mesh.shape["dp"]
         gathered = lax.all_gather(flat, "dp", axis=0, tiled=True)
@@ -338,8 +378,8 @@
         peer = peer_side(own)
         attended = attention(seq_one, q, own, peer, 0, width_dev // (2 * HD))
         sources = tuple(tuple((0, d * row_blocks * kept, True) for d in range(dp)) for _ in range(row_blocks))
-        partial_value = projection(
-            attended, table, jnp.arange(row_blocks, dtype=jnp.int32), sources, [gathered], kept, None, True
+        (partial_value,) = projection(
+            attended, table, jnp.arange(row_blocks, dtype=jnp.int32), sources, [gathered], kept
         )
     owned = lax.psum_scatter(partial_value, "tensor", scatter_dimension=1, tiled=True)
     return owned[None]

time: 177 us -> 155 us (0.88)
  waiting for transfers between devices: 90.5 us -> 43.9 us
  starting transfers between devices: 13.3 us -> 42 us
  between operations: 13.5 us -> 0.36 us
  other arithmetic: 1.69 us -> 7.44 us
  Pallas kernels: 48.7 us -> 53 us
    reduce_scatter x1 -> x0, waiting for transfers between devices: 78.4 us -> none  [shards(): lax.psum_scatter(partial_value, 'tensor', scatter_dimension=1, tiled=True)]
    ppermute x0 -> x12, waiting for transfers between devices: none -> 30.8 us  [the longest x6 27 us: line_scatter(): lax.ppermute(up, 'tensor', [(i, i + 1) for i in range(step)])]
    ppermute x0 -> x12, starting transfers between devices: none -> 29.4 us  [the longest x6 23.9 us: line_scatter(): lax.ppermute(up, 'tensor', [(i, i + 1) for i in range(step)])]
    pallas_call x2 -> x3, Pallas kernels: 21.4 us -> 25.7 us  [projection(): pl.pallas_call(functools.partial(projection_body, sources, kept, acc is n...]
    convert_element_type x0 -> x8, other arithmetic: none -> 3.78 us  [add(): return sum((v.astype(jnp.float32) for v in values)).astype(values[0].dtype)]
  transfers between devices with their start and end apart: 17 -> 28, of which waited for: 8 -> 13; matrix products, arithmetic and copies ran while one was open for 5% -> 7% of each run, Pallas kernels for 22% -> 29%
where the time goes in v4:
time: 155 us
  Pallas kernels  53 us (34%)
  waiting for transfers between devices  43.9 us (28%)
  starting transfers between devices  42 us (27%)
  local copies, waits for them, and re-layouts  7.83 us (5%)
  other arithmetic  7.44 us (5%)
    pallas_call x3, Pallas kernels, attention(): pl.pallas_call(body, out_shape=pltpu.HBM((rows, width), jnp.bfloat16), gr...  27.3 us
    ppermute x6, waiting for transfers between devices, line_scatter(): lax.ppermute(up, 'tensor', [(i, i + 1) for i in range(step)])  27 us
    pallas_call x3, Pallas kernels, projection(): pl.pallas_call(functools.partial(projection_body, sources, kept, acc is n...  25.7 us
    ppermute x6, starting transfers between devices, line_scatter(): lax.ppermute(up, 'tensor', [(i, i + 1) for i in range(step)])  23.9 us
    ppermute x16, waiting for transfers between devices, swap(): return lax.ppermute(value, axis, [(0, 1), (1, 0)])  13.1 us
    ppermute x16, starting transfers between devices, swap(): return lax.ppermute(value, axis, [(0, 1), (1, 0)])  12.6 us
    ppermute x6, starting transfers between devices, line_scatter(): lax.ppermute(down, 'tensor', [(i + 1, i) for i in range(n - 1 - step, n -...  5.49 us
    ppermute x6, waiting for transfers between devices, line_scatter(): lax.ppermute(down, 'tensor', [(i + 1, i) for i in range(n - 1 - step, n -...  3.79 us
  transfers between devices with their start and end apart: 28, of which 13 were waited for; matrix products, arithmetic and copies ran while one was open for 7% of the time, Pallas kernels for 29%

profile of v4, /device:TPU:0, one launch (start us, length us, event | category | flops | bytes accessed | tf_op | source)
XLA Modules:
  0.0 154.5 jit_solution(2859831165112201010)
XLA Ops:
  3.2 2.9 %collective-permute-start = (bf16[17,128,128]{2,1,0:T(8,128)(2,1)}, bf16[17,128,128]{2,1,0:T(8,128)(2,1)}, u32[]{:S(2)}, u32[]{:S(2)}) collective-permute-start(bf16[17,128,128]{2,1,0:T(8,128)(2,1)} %pad_maximum_fusion), channel_id=1, source_target_pairs={{0,1},{1,0},{2,3},{3,2},{4,5},{5,4},{6,7},{7,6},{8,9},{9,8},{10,11... | collective-permute-start | bytes 1671176 | tf_op jit(solution)/shard_map/ppermute | solution.py:268
  7.9 1.8 %collective-permute-start.5 = (bf16[32,128,128]{2,1,0:T(8,128)(2,1)S(1)}, bf16[32,128,128]{2,1,0:T(8,128)(2,1)}, u32[]{:S(2)}, u32[]{:S(2)}) collective-permute-start(bf16[32,128,128]{2,1,0:T(8,128)(2,1)S(1)} %constant_dynamic-slice_fusion), channel_id=1, source_target_pairs={{0,1},{1,0},{2,3},{3,2},{4,5},{5,4},{6,7},{7,6},{8,9},{9,8},{10,11... | collective-permute-start | bytes 3145736 | tf_op jit(solution)/shard_map/ppermute | solution.py:268
  9.7 1.4 constant_dynamic-slice_fusion.1
  11.1 1.6 %collective-permute-done.2.skb.refs_5_ = bf16[256,1024]{1,0:T(8,128)(2,1)S(1)} collective-permute-done((bf16[256,1024]{1,0:T(8,128)(2,1)}, bf16[256,1024]{1,0:T(8,128)(2,1)S(1)}, u32[]{:S(2)}, u32[]{:S(2)}) %collective-permute-start.2) | collective-permute-done | bytes 524320 | tf_op jit(solution)/shard_map/ppermute | solution.py:268
  14.2 7.4 %attention.1.refs_10_ = bf16[256,2048]{1,0:T(8,128)(2,1)} custom-call(s32[1]{0:T(128)} %bitcast.3.seq_ref.refs_0_, bf16[256,2048]{1,0:T(8,128)(2,1)} %bitcast.46, bf16[1792,1024]{1,0:T(8,128)(2,1)} %bitcast.39, bf16[256,1024]{1,0:T(8,128)(2,1)} %bitcast.50, bf16[1792,1024]{1,0:T(8,128)(2,1)} %collective-permute-done.1.ckb.refs_4_, ...), custom_call_target="tpu_custom_call" | custom-call | flops 1 | bytes 1 | tf_op jit(solution)/shard_map/attention/pallas_call | solution.py:103
  21.6 2.3 %collective-permute-start.6 = (bf16[17,128,128]{2,1,0:T(8,128)(2,1)}, bf16[17,128,128]{2,1,0:T(8,128)(2,1)}, u32[]{:S(2)}, u32[]{:S(2)}) collective-permute-start(bf16[17,128,128]{2,1,0:T(8,128)(2,1)} %collective-permute-done.refs_1_), channel_id=1, source_target_pairs={{0,16},{16,0},{1,17},{17,1},{2,18},{18,2},{3,19},{19,3},{4,20},{20... | collective-permute-start | bytes 1671176 | tf_op jit(solution)/shard_map/ppermute | solution.py:268
  24.0 1.6 %collective-permute-start.7 = (bf16[35,128,128]{2,1,0:T(8,128)(2,1)S(1)}, bf16[35,128,128]{2,1,0:T(8,128)(2,1)S(1)}, u32[]{:S(2)}, u32[]{:S(2)}) collective-permute-start(bf16[35,128,128]{2,1,0:T(8,128)(2,1)S(1)} %constant_dynamic-slice_fusion.1), channel_id=1, source_target_pairs={{0,1},{1,0},{2,3},{3,2},{4,5},{5,4},{6,7},{7,6},{8,9},{9,8},{10,11... | collective-permute-start | bytes 3440648 | tf_op jit(solution)/shard_map/ppermute | solution.py:268
  25.6 12.6 %late_attention.2.refs_10_ = bf16[256,2048]{1,0:T(8,128)(2,1)} custom-call(s32[1]{0:T(128)} %bitcast.3.seq_ref.refs_0_, bf16[256,2048]{1,0:T(8,128)(2,1)} %bitcast.47, bf16[1792,1024]{1,0:T(8,128)(2,1)} %bitcast.40, bf16[256,1024]{1,0:T(8,128)(2,1)} %bitcast.51, ...), custom_call_target="tpu_custom_call", output_to_operand_aliasing={{}: (10, {})} | custom-call | flops 1 | bytes 1 | tf_op jit(solution)/shard_map/late_attention/pallas_call | solution.py:103
  38.1 4.2 %collective-permute-done.5.refs_2_ = bf16[32,128,128]{2,1,0:T(8,128)(2,1)} collective-permute-done((bf16[32,128,128]{2,1,0:T(8,128)(2,1)S(1)}, bf16[32,128,128]{2,1,0:T(8,128)(2,1)}, u32[]{:S(2)}, u32[]{:S(2)}) %collective-permute-start.5) | collective-permute-done | bytes 1048608 | tf_op jit(solution)/shard_map/ppermute | solution.py:268
  43.7 2.2 %collective-permute-start.8 = (bf16[16,128,128]{2,1,0:T(8,128)(2,1)S(1)}, bf16[16,128,128]{2,1,0:T(8,128)(2,1)S(1)}, u32[]{:S(2)}, u32[]{:S(2)}) collective-permute-start(bf16[16,128,128]{2,1,0:T(8,128)(2,1)S(1)} %get-tuple-element.60), channel_id=1, source_target_pairs={{0,16},{16,0},{1,17},{17,1},{2,18},{18,2},{3,19},{19,3},{4,20},{20... | collective-permute-start | bytes 1572872 | tf_op jit(solution)/shard_map/ppermute | solution.py:268
  47.1 7.4 %late_attention.3.x_hbm = bf16[256,2048]{1,0:T(8,128)(2,1)} custom-call(s32[1]{0:T(128)} %bitcast.3.seq_ref.refs_0_, bf16[256,2048]{1,0:T(8,128)(2,1)} %bitcast.48, bf16[1792,1024]{1,0:T(8,128)(2,1)} %bitcast.41, bf16[256,1024]{1,0:T(8,128)(2,1)} %bitcast.52, bf16[1792,1024]{1,0:T(8,128)(2,1)} %collective-permute-done.1.ckb.refs_4_, ...), custom_call_target="tpu_custom_call", output_to_operand_aliasing={{}: (10, {})} | custom-call | flops 1 | bytes 1 | tf_op jit(solution)/shard_map/late_attention/pallas_call | solution.py:103
  56.3 10.6 %early_projection.1.refs_7_ = bf16[256,8192]{1,0:T(8,128)(2,1)} custom-call(s32[16,64]{1,0:T(8,128)S(1)} %select_reduce_fusion.table_ref, s32[8]{0:T(128)S(1)} %stack.110.rows_ref, s32[4]{0:T(128)S(1)} %iota_multiply_fusion.cols_ref, bf16[256,2048]{1,0:T(8,128)(2,1)} %late_attention.3.x_hbm, bf16[256,128,128]{2,1,0:T(8,128)(2,1)} %bitcast.35, ...), custom_call_target="tpu_custom_call" | custom-call | flops 1 | bytes 1 | tf_op jit(solution)/shard_map/early_projection/pallas_call | solution.py:228
  66.9 2.8 %collective-permute-done.9.refs_3_ = bf16[16,128,128]{2,1,0:T(8,128)(2,1)S(1)} collective-permute-done((bf16[16,128,128]{2,1,0:T(8,128)(2,1)S(1)}, bf16[16,128,128]{2,1,0:T(8,128)(2,1)S(1)}, u32[]{:S(2)}, u32[]{:S(2)}) %collective-permute-start.9) | collective-permute-done | bytes 524320 | tf_op jit(solution)/shard_map/ppermute | solution.py:268
  70.4 2.6 %collective-permute-done.14.refs_5_ = bf16[16,128,128]{2,1,0:T(8,128)(2,1)} collective-permute-done((bf16[16,128,128]{2,1,0:T(8,128)(2,1)S(1)}, bf16[16,128,128]{2,1,0:T(8,128)(2,1)}, u32[]{:S(2)}, u32[]{:S(2)}) %collective-permute-start.14) | collective-permute-done | bytes 524320 | tf_op jit(solution)/shard_map/ppermute | solution.py:268
  74.0 7.6 %projection.3 = (bf16[128,2048]{1,0:T(8,128)(2,1)}, bf16[128,2048]{1,0:T(8,128)(2,1)}, bf16[128,2048]{1,0:T(8,128)(2,1)}, bf16[128,2048]{1,0:T(8,128)(2,1)}) custom-call(s32[16,64]{1,0:T(8,128)S(1)} %select_reduce_fusion.table_ref, s32[8]{0:T(128)S(1)} %stack.98.rows_ref, s32[2]{0:T(128)S(1)} %get-tuple-element.66.cols_ref, ...), custom_call_target="tpu_custom_call" | custom-call | flops 1 | bytes 1 | tf_op jit(solution)/shard_map/projection/pallas_call | solution.py:228
  81.6 3.7 %collective-permute-start.22 = (bf16[128,2048]{1,0:T(8,128)(2,1)}, bf16[128,2048]{1,0:T(8,128)(2,1)S(1)}, u32[]{:S(2)}, u32[]{:S(2)}) collective-permute-start(bf16[128,2048]{1,0:T(8,128)(2,1)} %get-tuple-element.54), channel_id=1, source_target_pairs={{0,4},{1,5},{2,6},{3,7},{16,20},{17,21},{18,22},{19,23}} | collective-permute-start | bytes 1572872 | tf_op jit(solution)/shard_map/ppermute | solution.py:261
  86.0 1.3 collective-permute-start.16
  88.1 7.6 %projection.2 = (bf16[128,2048]{1,0:T(8,128)(2,1)}, bf16[128,2048]{1,0:T(8,128)(2,1)}, bf16[128,2048]{1,0:T(8,128)(2,1)}, bf16[128,2048]{1,0:T(8,128)(2,1)}) custom-call(s32[16,64]{1,0:T(8,128)S(1)} %select_reduce_fusion.table_ref, s32[8]{0:T(128)S(1)} %stack.98.rows_ref, s32[2]{0:T(128)S(1)} %get-tuple-element.65.cols_ref, ...), custom_call_target="tpu_custom_call" | custom-call | flops 1 | bytes 1 | tf_op jit(solution)/shard_map/projection/pallas_call | solution.py:228
  95.7 2.2 %collective-permute-done.22 = bf16[128,2048]{1,0:T(8,128)(2,1)S(1)} collective-permute-done((bf16[128,2048]{1,0:T(8,128)(2,1)}, bf16[128,2048]{1,0:T(8,128)(2,1)S(1)}, u32[]{:S(2)}, u32[]{:S(2)}) %collective-permute-start.22) | collective-permute-done | bytes 524320 | tf_op jit(solution)/shard_map/ppermute | solution.py:261
  97.9 1.4 fusion.3
  99.3 4.3 %collective-permute-start.24 = (bf16[128,2048]{1,0:T(8,128)(2,1)S(1)}, bf16[128,2048]{1,0:T(8,128)(2,1)S(1)}, u32[]{:S(2)}, u32[]{:S(2)}) collective-permute-start(bf16[128,2048]{1,0:T(8,128)(2,1)S(1)} %get-tuple-element.64), channel_id=1, source_target_pairs={{0,4},{4,8},{1,5},{5,9},{2,6},{6,10},{3,7},{7,11},{16,20},{20,24},... | collective-permute-start | bytes 1572872 | tf_op jit(solution)/shard_map/ppermute | solution.py:261
  104.3 4.8 %collective-permute-done.16 = bf16[128,2048]{1,0:T(8,128)(2,1)S(1)} collective-permute-done((bf16[128,2048]{1,0:T(8,128)(2,1)}, bf16[128,2048]{1,0:T(8,128)(2,1)S(1)}, u32[]{:S(2)}, u32[]{:S(2)}) %collective-permute-start.16) | collective-permute-done | bytes 524320 | tf_op jit(solution)/shard_map/ppermute | solution.py:261
  109.1 1.4 fusion.1
  110.6 4.4 %collective-permute-start.18 = (bf16[128,2048]{1,0:T(8,128)(2,1)S(1)}, bf16[128,2048]{1,0:T(8,128)(2,1)S(1)}, u32[]{:S(2)}, u32[]{:S(2)}) collective-permute-start(bf16[128,2048]{1,0:T(8,128)(2,1)S(1)} %get-tuple-element.62), channel_id=1, source_target_pairs={{0,4},{4,8},{1,5},{5,9},{2,6},{6,10},{3,7},{7,11},{16,20},{20,24},... | collective-permute-start | bytes 1572872 | tf_op jit(solution)/shard_map/ppermute | solution.py:261
  115.7 4.5 %collective-permute-done.24 = bf16[128,2048]{1,0:T(8,128)(2,1)S(1)} collective-permute-done((bf16[128,2048]{1,0:T(8,128)(2,1)S(1)}, bf16[128,2048]{1,0:T(8,128)(2,1)S(1)}, u32[]{:S(2)}, u32[]{:S(2)}) %collective-permute-start.24) | collective-permute-done | bytes 524320 | tf_op jit(solution)/shard_map/ppermute | solution.py:261
  120.4 1.4 collective-permute-start.27
  122.0 5.0 %collective-permute-start.26 = (bf16[128,2048]{1,0:T(8,128)(2,1)S(1)}, bf16[128,2048]{1,0:T(8,128)(2,1)S(1)}, u32[]{:S(2)}, u32[]{:S(2)}) collective-permute-start(bf16[128,2048]{1,0:T(8,128)(2,1)S(1)} %add_convert_fusion.2), channel_id=1, source_target_pairs={{0,4},{4,8},{8,12},{1,5},{5,9},{9,13},{2,6},{6,10},{10,14},{3,7},{... | collective-permute-start | bytes 1572872 | tf_op jit(solution)/shard_map/ppermute | solution.py:261
  127.0 4.5 %collective-permute-done.18 = bf16[128,2048]{1,0:T(8,128)(2,1)S(1)} collective-permute-done((bf16[128,2048]{1,0:T(8,128)(2,1)S(1)}, bf16[128,2048]{1,0:T(8,128)(2,1)S(1)}, u32[]{:S(2)}, u32[]{:S(2)}) %collective-permute-start.18) | collective-permute-done | bytes 524320 | tf_op jit(solution)/shard_map/ppermute | solution.py:261
  133.1 5.1 %collective-permute-start.20 = (bf16[128,2048]{1,0:T(8,128)(2,1)S(1)}, bf16[128,2048]{1,0:T(8,128)(2,1)S(1)}, u32[]{:S(2)}, u32[]{:S(2)}) collective-permute-start(bf16[128,2048]{1,0:T(8,128)(2,1)S(1)} %add_convert_fusion.5), channel_id=1, source_target_pairs={{0,4},{4,8},{8,12},{1,5},{5,9},{9,13},{2,6},{6,10},{10,14},{3,7},{... | collective-permute-start | bytes 1572872 | tf_op jit(solution)/shard_map/ppermute | solution.py:261
  138.2 4.6 %collective-permute-done.26 = bf16[128,2048]{1,0:T(8,128)(2,1)S(1)} collective-permute-done((bf16[128,2048]{1,0:T(8,128)(2,1)S(1)}, bf16[128,2048]{1,0:T(8,128)(2,1)S(1)}, u32[]{:S(2)}, u32[]{:S(2)}) %collective-permute-start.26) | collective-permute-done | bytes 524320 | tf_op jit(solution)/shard_map/ppermute | solution.py:261
  143.0 3.8 %collective-permute-done.21 = bf16[128,2048]{1,0:T(8,128)(2,1)S(1)} collective-permute-done((bf16[128,2048]{1,0:T(8,128)(2,1)S(1)}, bf16[128,2048]{1,0:T(8,128)(2,1)S(1)}, u32[]{:S(2)}, u32[]{:S(2)}) %collective-permute-start.21) | collective-permute-done | bytes 524320 | tf_op jit(solution)/shard_map/ppermute | solution.py:262
  146.8 6.4 %collective-permute-done.20 = bf16[128,2048]{1,0:T(8,128)(2,1)S(1)} collective-permute-done((bf16[128,2048]{1,0:T(8,128)(2,1)S(1)}, bf16[128,2048]{1,0:T(8,128)(2,1)S(1)}, u32[]{:S(2)}, u32[]{:S(2)}) %collective-permute-start.20) | collective-permute-done | bytes 524320 | tf_op jit(solution)/shard_map/ppermute | solution.py:261
  (79 shorter events, 18.8 us)
Async XLA Ops:
  0.0 7.9 %collective-permute-start.1 = (bf16[1792,1024]{1,0:T(8,128)(2,1)}, bf16[1792,1024]{1,0:T(8,128)(2,1)}, u32[]{:S(2)}, u32[]{:S(2)}) collective-permute-start(bf16[1792,1024]{1,0:T(8,128)(2,1)} %bitcast.38), channel_id=1, source_target_pairs={{0,2},{2,0},{1,3},{3,1},{4,6},{6,4},{5,7},{7,5},{8,10},{10,8},{9,1... | collective-permute-start | bytes 11010056 | tf_op jit(solution)/shard_map/ppermute | solution.py:268
  0.5 13.0 %collective-permute-start.3 = (bf16[1792,1024]{1,0:T(8,128)(2,1)}, bf16[1792,1024]{1,0:T(8,128)(2,1)}, u32[]{:S(2)}, u32[]{:S(2)}) collective-permute-start(bf16[1792,1024]{1,0:T(8,128)(2,1)} %bitcast.42), channel_id=1, source_target_pairs={{0,2},{2,0},{1,3},{3,1},{4,6},{6,4},{5,7},{7,5},{8,10},{10,8},{9,1... | collective-permute-start | bytes 11010056 | tf_op jit(solution)/shard_map/ppermute | solution.py:268
  3.2 18.4 %collective-permute-start = (bf16[17,128,128]{2,1,0:T(8,128)(2,1)}, bf16[17,128,128]{2,1,0:T(8,128)(2,1)}, u32[]{:S(2)}, u32[]{:S(2)}) collective-permute-start(bf16[17,128,128]{2,1,0:T(8,128)(2,1)} %pad_maximum_fusion), channel_id=1, source_target_pairs={{0,1},{1,0},{2,3},{3,2},{4,5},{5,4},{6,7},{7,6},{8,9},{9,8},{10,11... | collective-permute-start | bytes 1671176 | tf_op jit(solution)/shard_map/ppermute | solution.py:268
  6.1 6.6 %collective-permute-start.2 = (bf16[256,1024]{1,0:T(8,128)(2,1)}, bf16[256,1024]{1,0:T(8,128)(2,1)S(1)}, u32[]{:S(2)}, u32[]{:S(2)}) collective-permute-start(bf16[256,1024]{1,0:T(8,128)(2,1)} %bitcast.49), channel_id=1, source_target_pairs={{0,2},{2,0},{1,3},{3,1},{4,6},{6,4},{5,7},{7,5},{8,10},{10,8},{9,1... | collective-permute-start | bytes 1572872 | tf_op jit(solution)/shard_map/ppermute | solution.py:268
  6.1 7.3 %collective-permute-start.4 = (bf16[256,1024]{1,0:T(8,128)(2,1)}, bf16[256,1024]{1,0:T(8,128)(2,1)S(1)}, u32[]{:S(2)}, u32[]{:S(2)}) collective-permute-start(bf16[256,1024]{1,0:T(8,128)(2,1)} %bitcast.53), channel_id=1, source_target_pairs={{0,2},{2,0},{1,3},{3,1},{4,6},{6,4},{5,7},{7,5},{8,10},{10,8},{9,1... | collective-permute-start | bytes 1572872 | tf_op jit(solution)/shard_map/ppermute | solution.py:268
  7.9 34.4 %collective-permute-start.5 = (bf16[32,128,128]{2,1,0:T(8,128)(2,1)S(1)}, bf16[32,128,128]{2,1,0:T(8,128)(2,1)}, u32[]{:S(2)}, u32[]{:S(2)}) collective-permute-start(bf16[32,128,128]{2,1,0:T(8,128)(2,1)S(1)} %constant_dynamic-slice_fusion), channel_id=1, source_target_pairs={{0,1},{1,0},{2,3},{3,2},{4,5},{5,4},{6,7},{7,6},{8,9},{9,8},{10,11... | collective-permute-start | bytes 3145736 | tf_op jit(solution)/shard_map/ppermute | solution.py:268
  21.6 20.7 %collective-permute-start.6 = (bf16[17,128,128]{2,1,0:T(8,128)(2,1)}, bf16[17,128,128]{2,1,0:T(8,128)(2,1)}, u32[]{:S(2)}, u32[]{:S(2)}) collective-permute-start(bf16[17,128,128]{2,1,0:T(8,128)(2,1)} %collective-permute-done.refs_1_), channel_id=1, source_target_pairs={{0,16},{16,0},{1,17},{17,1},{2,18},{18,2},{3,19},{19,3},{4,20},{20... | collective-permute-start | bytes 1671176 | tf_op jit(solution)/shard_map/ppermute | solution.py:268
  24.0 22.0 %collective-permute-start.10 = (bf16[17,128,128]{2,1,0:T(8,128)(2,1)}, bf16[17,128,128]{2,1,0:T(8,128)(2,1)S(1)}, u32[]{:S(2)}, u32[]{:S(2)}) collective-permute-start(bf16[17,128,128]{2,1,0:T(8,128)(2,1)} %collective-permute-done.refs_1_), channel_id=1, source_target_pairs={{0,2},{2,0},{1,3},{3,1},{4,6},{6,4},{5,7},{7,5},{8,10},{10,8},{9,1... | collective-permute-start | bytes 1671176 | tf_op jit(solution)/shard_map/ppermute | solution.py:268
  24.0 45.7 %collective-permute-start.7 = (bf16[35,128,128]{2,1,0:T(8,128)(2,1)S(1)}, bf16[35,128,128]{2,1,0:T(8,128)(2,1)S(1)}, u32[]{:S(2)}, u32[]{:S(2)}) collective-permute-start(bf16[35,128,128]{2,1,0:T(8,128)(2,1)S(1)} %constant_dynamic-slice_fusion.1), channel_id=1, source_target_pairs={{0,1},{1,0},{2,3},{3,2},{4,5},{5,4},{6,7},{7,6},{8,9},{9,8},{10,11... | collective-permute-start | bytes 3440648 | tf_op jit(solution)/shard_map/ppermute | solution.py:268
  42.3 12.2 %collective-permute-start.11 = (bf16[32,128,128]{2,1,0:T(8,128)(2,1)}, bf16[32,128,128]{2,1,0:T(8,128)(2,1)S(1)}, u32[]{:S(2)}, u32[]{:S(2)}) collective-permute-start(bf16[32,128,128]{2,1,0:T(8,128)(2,1)} %collective-permute-done.5.refs_2_), channel_id=1, source_target_pairs={{0,2},{2,0},{1,3},{3,1},{4,6},{6,4},{5,7},{7,5},{8,10},{10,8},{9,1... | collective-permute-start | bytes 3145736 | tf_op jit(solution)/shard_map/ppermute | solution.py:268
  43.7 23.1 %collective-permute-start.8 = (bf16[16,128,128]{2,1,0:T(8,128)(2,1)S(1)}, bf16[16,128,128]{2,1,0:T(8,128)(2,1)S(1)}, u32[]{:S(2)}, u32[]{:S(2)}) collective-permute-start(bf16[16,128,128]{2,1,0:T(8,128)(2,1)S(1)} %get-tuple-element.60), channel_id=1, source_target_pairs={{0,16},{16,0},{1,17},{17,1},{2,18},{18,2},{3,19},{19,3},{4,20},{20... | collective-permute-start | bytes 1572872 | tf_op jit(solution)/shard_map/ppermute | solution.py:268
  45.9 23.8 %collective-permute-start.9 = (bf16[16,128,128]{2,1,0:T(8,128)(2,1)S(1)}, bf16[16,128,128]{2,1,0:T(8,128)(2,1)S(1)}, u32[]{:S(2)}, u32[]{:S(2)}) collective-permute-start(bf16[16,128,128]{2,1,0:T(8,128)(2,1)S(1)} %get-tuple-element.59), channel_id=1, source_target_pairs={{0,16},{16,0},{1,17},{17,1},{2,18},{18,2},{3,19},{19,3},{4,20},{20... | collective-permute-start | bytes 1572872 | tf_op jit(solution)/shard_map/ppermute | solution.py:268
  46.0 8.5 %collective-permute-start.12 = (bf16[17,128,128]{2,1,0:T(8,128)(2,1)}, bf16[17,128,128]{2,1,0:T(8,128)(2,1)S(1)}, u32[]{:S(2)}, u32[]{:S(2)}) collective-permute-start(bf16[17,128,128]{2,1,0:T(8,128)(2,1)} %collective-permute-done.6.refs_3_), channel_id=1, source_target_pairs={{0,2},{2,0},{1,3},{3,1},{4,6},{6,4},{5,7},{7,5},{8,10},{10,8},{9,1... | collective-permute-start | bytes 1671176 | tf_op jit(solution)/shard_map/ppermute | solution.py:268
  69.7 4.3 %collective-permute-start.13 = (bf16[35,128,128]{2,1,0:T(8,128)(2,1)S(1)}, bf16[35,128,128]{2,1,0:T(8,128)(2,1)S(1)}, u32[]{:S(2)}, u32[]{:S(2)}) collective-permute-start(bf16[35,128,128]{2,1,0:T(8,128)(2,1)S(1)} %collective-permute-done.7.refs_1_), channel_id=1, source_target_pairs={{0,2},{2,0},{1,3},{3,1},{4,6},{6,4},{5,7},{7,5},{8,10},{10,8},{9,1... | collective-permute-start | bytes 3440648 | tf_op jit(solution)/shard_map/ppermute | solution.py:268
  69.7 3.3 %collective-permute-start.14 = (bf16[16,128,128]{2,1,0:T(8,128)(2,1)S(1)}, bf16[16,128,128]{2,1,0:T(8,128)(2,1)}, u32[]{:S(2)}, u32[]{:S(2)}) collective-permute-start(bf16[16,128,128]{2,1,0:T(8,128)(2,1)S(1)} %collective-permute-done.8.refs_2_), channel_id=1, source_target_pairs={{0,2},{2,0},{1,3},{3,1},{4,6},{6,4},{5,7},{7,5},{8,10},{10,8},{9,1... | collective-permute-start | bytes 1572872 | tf_op jit(solution)/shard_map/ppermute | solution.py:268
  70.2 3.8 %collective-permute-start.15 = (bf16[16,128,128]{2,1,0:T(8,128)(2,1)S(1)}, bf16[16,128,128]{2,1,0:T(8,128)(2,1)}, u32[]{:S(2)}, u32[]{:S(2)}) collective-permute-start(bf16[16,128,128]{2,1,0:T(8,128)(2,1)S(1)} %collective-permute-done.9.refs_3_), channel_id=1, source_target_pairs={{0,2},{2,0},{1,3},{3,1},{4,6},{6,4},{5,7},{7,5},{8,10},{10,8},{9,1... | collective-permute-start | bytes 1572872 | tf_op jit(solution)/shard_map/ppermute | solution.py:268
  81.6 16.3 %collective-permute-start.22 = (bf16[128,2048]{1,0:T(8,128)(2,1)}, bf16[128,2048]{1,0:T(8,128)(2,1)S(1)}, u32[]{:S(2)}, u32[]{:S(2)}) collective-permute-start(bf16[128,2048]{1,0:T(8,128)(2,1)} %get-tuple-element.54), channel_id=1, source_target_pairs={{0,4},{1,5},{2,6},{3,7},{16,20},{17,21},{18,22},{19,23}} | collective-permute-start | bytes 1572872 | tf_op jit(solution)/shard_map/ppermute | solution.py:261
  85.3 12.6 %collective-permute-start.23 = (bf16[128,2048]{1,0:T(8,128)(2,1)}, bf16[128,2048]{1,0:T(8,128)(2,1)S(1)}, u32[]{:S(2)}, u32[]{:S(2)}) collective-permute-start(bf16[128,2048]{1,0:T(8,128)(2,1)} %get-tuple-element.52), channel_id=1, source_target_pairs={{12,8},{13,9},{14,10},{15,11},{28,24},{29,25},{30,26},{31,27}} | collective-permute-start | bytes 1572872 | tf_op jit(solution)/shard_map/ppermute | solution.py:262
  86.0 23.1 %collective-permute-start.16 = (bf16[128,2048]{1,0:T(8,128)(2,1)}, bf16[128,2048]{1,0:T(8,128)(2,1)S(1)}, u32[]{:S(2)}, u32[]{:S(2)}) collective-permute-start(bf16[128,2048]{1,0:T(8,128)(2,1)} %get-tuple-element.46), channel_id=1, source_target_pairs={{0,4},{1,5},{2,6},{3,7},{16,20},{17,21},{18,22},{19,23}} | collective-permute-start | bytes 1572872 | tf_op jit(solution)/shard_map/ppermute | solution.py:261
  87.4 21.8 %collective-permute-start.17 = (bf16[128,2048]{1,0:T(8,128)(2,1)}, bf16[128,2048]{1,0:T(8,128)(2,1)S(1)}, u32[]{:S(2)}, u32[]{:S(2)}) collective-permute-start(bf16[128,2048]{1,0:T(8,128)(2,1)} %get-tuple-element.44), channel_id=1, source_target_pairs={{12,8},{13,9},{14,10},{15,11},{28,24},{29,25},{30,26},{31,27}} | collective-permute-start | bytes 1572872 | tf_op jit(solution)/shard_map/ppermute | solution.py:262
  95.7 26.2 %copy-start.7 = (bf16[128,2048]{1,0:T(8,128)(2,1)S(1)}, bf16[128,2048]{1,0:T(8,128)(2,1)}, u32[]{:S(2)}) copy-start(bf16[128,2048]{1,0:T(8,128)(2,1)} %get-tuple-element.52) | copy-start | bytes 1572868
  97.9 33.6 %copy-start.6 = (bf16[128,2048]{1,0:T(8,128)(2,1)S(1)}, bf16[128,2048]{1,0:T(8,128)(2,1)}, u32[]{:S(2)}) copy-start(bf16[128,2048]{1,0:T(8,128)(2,1)} %get-tuple-element.46) | copy-start | bytes 1572868
  99.3 20.9 %collective-permute-start.24 = (bf16[128,2048]{1,0:T(8,128)(2,1)S(1)}, bf16[128,2048]{1,0:T(8,128)(2,1)S(1)}, u32[]{:S(2)}, u32[]{:S(2)}) collective-permute-start(bf16[128,2048]{1,0:T(8,128)(2,1)S(1)} %get-tuple-element.64), channel_id=1, source_target_pairs={{0,4},{4,8},{1,5},{5,9},{2,6},{6,10},{3,7},{7,11},{16,20},{20,24},... | collective-permute-start | bytes 1572872 | tf_op jit(solution)/shard_map/ppermute | solution.py:261
  103.6 16.6 %collective-permute-start.25 = (bf16[128,2048]{1,0:T(8,128)(2,1)S(1)}, bf16[128,2048]{1,0:T(8,128)(2,1)S(1)}, u32[]{:S(2)}, u32[]{:S(2)}) collective-permute-start(bf16[128,2048]{1,0:T(8,128)(2,1)S(1)} %get-tuple-element.63), channel_id=1, source_target_pairs={{8,4},{12,8},{9,5},{13,9},{10,6},{14,10},{11,7},{15,11},{24,20},{2... | collective-permute-start | bytes 1572872 | tf_op jit(solution)/shard_map/ppermute | solution.py:262
  110.6 32.2 %copy-start.10 = (bf16[128,2048]{1,0:T(8,128)(2,1)S(1)}, bf16[128,2048]{1,0:T(8,128)(2,1)}, u32[]{:S(2)}) copy-start(bf16[128,2048]{1,0:T(8,128)(2,1)} %get-tuple-element.51) | copy-start | bytes 1572868
  110.6 20.9 %collective-permute-start.18 = (bf16[128,2048]{1,0:T(8,128)(2,1)S(1)}, bf16[128,2048]{1,0:T(8,128)(2,1)S(1)}, u32[]{:S(2)}, u32[]{:S(2)}) collective-permute-start(bf16[128,2048]{1,0:T(8,128)(2,1)S(1)} %get-tuple-element.62), channel_id=1, source_target_pairs={{0,4},{4,8},{1,5},{5,9},{2,6},{6,10},{3,7},{7,11},{16,20},{20,24},... | collective-permute-start | bytes 1572872 | tf_op jit(solution)/shard_map/ppermute | solution.py:261
  115.0 16.5 %collective-permute-start.19 = (bf16[128,2048]{1,0:T(8,128)(2,1)S(1)}, bf16[128,2048]{1,0:T(8,128)(2,1)S(1)}, u32[]{:S(2)}, u32[]{:S(2)}) collective-permute-start(bf16[128,2048]{1,0:T(8,128)(2,1)S(1)} %get-tuple-element.61), channel_id=1, source_target_pairs={{8,4},{12,8},{9,5},{13,9},{10,6},{14,10},{11,7},{15,11},{24,20},{2... | collective-permute-start | bytes 1572872 | tf_op jit(solution)/shard_map/ppermute | solution.py:262
  120.4 32.8 %copy-start.9 = (bf16[128,2048]{1,0:T(8,128)(2,1)S(1)}, bf16[128,2048]{1,0:T(8,128)(2,1)}, u32[]{:S(2)}) copy-start(bf16[128,2048]{1,0:T(8,128)(2,1)} %get-tuple-element.43) | copy-start | bytes 1572868
  120.4 17.8 %collective-permute-start.27 = (bf16[128,2048]{1,0:T(8,128)(2,1)S(1)}, bf16[128,2048]{1,0:T(8,128)(2,1)S(1)}, u32[]{:S(2)}, u32[]{:S(2)}) collective-permute-start(bf16[128,2048]{1,0:T(8,128)(2,1)S(1)} %add_convert_fusion.1), channel_id=1, source_target_pairs={{4,0},{8,4},{12,8},{5,1},{9,5},{13,9},{6,2},{10,6},{14,10},{7,3},{... | collective-permute-start | bytes 1572872 | tf_op jit(solution)/shard_map/ppermute | solution.py:262
  122.0 20.7 %collective-permute-start.26 = (bf16[128,2048]{1,0:T(8,128)(2,1)S(1)}, bf16[128,2048]{1,0:T(8,128)(2,1)S(1)}, u32[]{:S(2)}, u32[]{:S(2)}) collective-permute-start(bf16[128,2048]{1,0:T(8,128)(2,1)S(1)} %add_convert_fusion.2), channel_id=1, source_target_pairs={{0,4},{4,8},{8,12},{1,5},{5,9},{9,13},{2,6},{6,10},{10,14},{3,7},{... | collective-permute-start | bytes 1572872 | tf_op jit(solution)/shard_map/ppermute | solution.py:261
  131.6 15.1 %collective-permute-start.21 = (bf16[128,2048]{1,0:T(8,128)(2,1)S(1)}, bf16[128,2048]{1,0:T(8,128)(2,1)S(1)}, u32[]{:S(2)}, u32[]{:S(2)}) collective-permute-start(bf16[128,2048]{1,0:T(8,128)(2,1)S(1)} %add_convert_fusion.4), channel_id=1, source_target_pairs={{4,0},{8,4},{12,8},{5,1},{9,5},{13,9},{6,2},{10,6},{14,10},{7,3},{... | collective-permute-start | bytes 1572872 | tf_op jit(solution)/shard_map/ppermute | solution.py:262
  133.1 20.1 %collective-permute-start.20 = (bf16[128,2048]{1,0:T(8,128)(2,1)S(1)}, bf16[128,2048]{1,0:T(8,128)(2,1)S(1)}, u32[]{:S(2)}, u32[]{:S(2)}) collective-permute-start(bf16[128,2048]{1,0:T(8,128)(2,1)S(1)} %add_convert_fusion.5), channel_id=1, source_target_pairs={{0,4},{4,8},{8,12},{1,5},{5,9},{9,13},{2,6},{6,10},{10,14},{3,7},{... | collective-permute-start | bytes 1572872 | tf_op jit(solution)/shard_map/ppermute | solution.py:261
  (8 other events, 81.7 us)

commit v5 on v4

--- a/solution.py
+++ b/solution.py
@@ -294,7 +294,7 @@
     own = [a[0] for a in (cache_keys, stretch_keys, cache_values, stretch_values)]
     flat = blocks.reshape(row_blocks * kept, block_size, block_size)
 
-    if mesh.shape["dp"] == 2 and mesh.shape["groups"] == 2 and row_blocks % 16 == 0 and max(row_blocks, kept) <= block_size:
+    if mesh.shape["dp"] == 2 and mesh.shape["groups"] == 2 and row_blocks % 16 == 0 and width_dev >= 16 * HD and max(row_blocks, kept) <= block_size:
         unit = row_blocks // 16
         groups = lax.axis_index("groups")
         half = 8 * unit * my_seq
@@ -304,7 +304,7 @@
             return lax.dynamic_slice_in_dim(flat, start * kept, count * kept + more, 0)
 
         heads = width_dev // (2 * HD)
-        soon = max(heads // 4, 1)
+        soon, last = heads // 4, heads // 8
         carried = jnp.pad(
             block_columns.astype(jnp.bfloat16), ((0, block_size - row_blocks), (0, block_size - kept))
         )
@@ -319,12 +319,12 @@
         table = column_table(jnp.stack([block_columns, peer_columns]), col_blocks)
         far1 = swap(near1, "groups")
         near1_other = swap(near1, "seq")
-        attended = attention(seq_one, q, own, peer, soon, heads - 2 * soon, attended)
+        attended = attention(seq_one, q, own, peer, soon, heads - soon - last, attended)
         near2, far1, attended = lax.optimization_barrier((near2, far1, attended))
-        far2, far3 = [swap(near2[i * unit * kept : (i + 1) * unit * kept], "groups") for i in range(2)]
+        far2 = swap(near2, "groups")
         near2_other = swap(near2, "seq")
         far1_other = swap(far1, "seq")
-        attended = attention(seq_one, q, own, peer, heads - soon, soon, attended)
+        attended = attention(seq_one, q, own, peer, heads - last, last, attended)
         other = 8 * unit * (1 - my_seq)
 
         def stage(plan, acc=None, columns=None):
@@ -349,17 +349,15 @@
                 (relayed(other, 1 - groups), unit, far1_other),
             ),
         )
-        shared, far2, far3, early = lax.optimization_barrier((shared, far2, far3, early))
+        shared, early = lax.optimization_barrier((shared, early))
         shared_other = swap(shared, "seq")
+        far2, early = lax.optimization_barrier((far2, early))
         far2_other = swap(far2, "seq")
-        far3_other = swap(far3, "seq")
         plan = (
             (half, 2 * unit, shared),
-            (relayed(half, 1 - groups) + unit, unit, far2),
-            (relayed(half, 1 - groups) + 2 * unit, unit, far3),
+            (relayed(half, 1 - groups) + unit, 2 * unit, far2),
             (other, 2 * unit, shared_other),
-            (relayed(other, 1 - groups) + unit, unit, far2_other),
-            (relayed(other, 1 - groups) + 2 * unit, unit, far3_other),
+            (relayed(other, 1 - groups) + unit, 2 * unit, far2_other),
         )
         n = mesh.shape["tensor"]
         place = lax.axis_index("tensor")

time: 155 us -> 152 us (0.981)
  waiting for transfers between devices: 43.9 us -> 40.7 us
  local copies, waits for them, and re-layouts: 7.83 us -> 9.51 us
    ppermute x16 -> x14, waiting for transfers between devices: 13.1 us -> 10 us  [swap(): return lax.ppermute(value, axis, [(0, 1), (1, 0)])]
    dynamic_slice x3, local copies, waits for them, and re-layouts: 3.74 us -> 5.88 us  [piece(): return lax.dynamic_slice_in_dim(flat, start * kept, count * kept + more, 0)]
    unnamed x24 -> x28, local copies, waits for them, and re-layouts: 2.61 us -> 3.46 us
    ppermute x16 -> x14, starting transfers between devices: 12.6 us -> 12 us  [swap(): return lax.ppermute(value, axis, [(0, 1), (1, 0)])]
  transfers between devices with their start and end apart: 28 -> 26, of which waited for: 13 -> 14; matrix products, arithmetic and copies ran while one was open for 7% -> 7% of each run, Pallas kernels for 29% -> 30%
where the time goes in v5:
time: 152 us
  Pallas kernels  53 us (35%)
  starting transfers between devices  41.4 us (27%)
  waiting for transfers between devices  40.7 us (27%)
  local copies, waits for them, and re-layouts  9.51 us (6%)
  other arithmetic  6.63 us (4%)
    pallas_call x3, Pallas kernels, attention(): pl.pallas_call(body, out_shape=pltpu.HBM((rows, width), jnp.bfloat16), gr...  27.3 us
    ppermute x6, waiting for transfers between devices, line_scatter(): lax.ppermute(up, 'tensor', [(i, i + 1) for i in range(step)])  26.9 us
    pallas_call x3, Pallas kernels, projection(): pl.pallas_call(functools.partial(projection_body, sources, kept, acc is n...  25.7 us
    ppermute x6, starting transfers between devices, line_scatter(): lax.ppermute(up, 'tensor', [(i, i + 1) for i in range(step)])  23.9 us
    ppermute x14, starting transfers between devices, swap(): return lax.ppermute(value, axis, [(0, 1), (1, 0)])  12 us
    ppermute x14, waiting for transfers between devices, swap(): return lax.ppermute(value, axis, [(0, 1), (1, 0)])  10 us
    dynamic_slice x3, local copies, waits for them, and re-layouts, piece(): return lax.dynamic_slice_in_dim(flat, start * kept, count * kept + more, 0)  5.88 us
    ppermute x6, starting transfers between devices, line_scatter(): lax.ppermute(down, 'tensor', [(i + 1, i) for i in range(n - 1 - step, n -...  5.49 us
  transfers between devices with their start and end apart: 26, of which 14 were waited for; matrix products, arithmetic and copies ran while one was open for 7% of the time, Pallas kernels for 30%

profile of v5, /device:TPU:0, one launch (start us, length us, event | category | flops | bytes accessed | tf_op | source)
XLA Modules:
  0.0 151.6 jit_solution(8570908079504563943)
XLA Ops:
  2.4 3.0 %collective-permute-start = (bf16[17,128,128]{2,1,0:T(8,128)(2,1)S(1)}, bf16[17,128,128]{2,1,0:T(8,128)(2,1)S(1)}, u32[]{:S(2)}, u32[]{:S(2)}) collective-permute-start(bf16[17,128,128]{2,1,0:T(8,128)(2,1)S(1)} %pad_maximum_fusion), channel_id=1, source_target_pairs={{0,1},{1,0},{2,3},{3,2},{4,5},{5,4},{6,7},{7,6},{8,9},{9,8},{10,11... | collective-permute-start | bytes 1671176 | tf_op jit(solution)/shard_map/ppermute | solution.py:268
  5.9 2.3 %constant_dynamic-slice_fusion = bf16[32,128,128]{2,1,0:T(8,128)(2,1)} fusion(bf16[256,128,128]{2,1,0:T(8,128)(2,1)} %bitcast.33, s32[]{:T(128)S(6)} %select_n.37), kind=kLoop, calls=%fused_computation.22 | loop fusion | bytes 2097156 | tf_op jit(solution)/shard_map/dynamic_slice | solution.py:304
  8.2 1.5 collective-permute-start.5
  9.7 2.5 %constant_dynamic-slice_fusion.1 = bf16[35,128,128]{2,1,0:T(8,128)(2,1)} fusion(bf16[256,128,128]{2,1,0:T(8,128)(2,1)} %bitcast.34, s32[]{:T(128)S(6)} %select_n.33), kind=kLoop, calls=%fused_computation.23 | loop fusion | bytes 2293764 | tf_op jit(solution)/shard_map/dynamic_slice | solution.py:304
  14.2 7.4 %attention.1.refs_10_ = bf16[256,2048]{1,0:T(8,128)(2,1)} custom-call(s32[1]{0:T(128)} %bitcast.3.seq_ref.refs_0_, bf16[256,2048]{1,0:T(8,128)(2,1)} %bitcast.46, bf16[1792,1024]{1,0:T(8,128)(2,1)} %bitcast.39, bf16[256,1024]{1,0:T(8,128)(2,1)} %bitcast.50, bf16[1792,1024]{1,0:T(8,128)(2,1)} %collective-permute-done.1.ckb.refs_4_, ...), custom_call_target="tpu_custom_call" | custom-call | flops 1 | bytes 1 | tf_op jit(solution)/shard_map/attention/pallas_call | solution.py:103
  21.6 2.4 %collective-permute-start.6 = (bf16[17,128,128]{2,1,0:T(8,128)(2,1)S(1)}, bf16[17,128,128]{2,1,0:T(8,128)(2,1)S(1)}, u32[]{:S(2)}, u32[]{:S(2)}) collective-permute-start(bf16[17,128,128]{2,1,0:T(8,128)(2,1)S(1)} %collective-permute-done.refs_1_), channel_id=1, source_target_pairs={{0,16},{16,0},{1,17},{17,1},{2,18},{18,2},{3,19},{19,3},{4,20},{20... | collective-permute-start | bytes 1671176 | tf_op jit(solution)/shard_map/ppermute | solution.py:268
  23.9 1.5 collective-permute-start.7
  25.4 15.2 %late_attention.2.refs_10_ = bf16[256,2048]{1,0:T(8,128)(2,1)} custom-call(s32[1]{0:T(128)} %bitcast.3.seq_ref.refs_0_, bf16[256,2048]{1,0:T(8,128)(2,1)} %bitcast.47, bf16[1792,1024]{1,0:T(8,128)(2,1)} %bitcast.40, bf16[256,1024]{1,0:T(8,128)(2,1)} %bitcast.51, ...), custom_call_target="tpu_custom_call", output_to_operand_aliasing={{}: (10, {})} | custom-call | flops 1 | bytes 1 | tf_op jit(solution)/shard_map/late_attention/pallas_call | solution.py:103
  42.2 2.1 %collective-permute-start.11 = (bf16[32,128,128]{2,1,0:T(8,128)(2,1)}, bf16[32,128,128]{2,1,0:T(8,128)(2,1)S(1)}, u32[]{:S(2)}, u32[]{:S(2)}) collective-permute-start(bf16[32,128,128]{2,1,0:T(8,128)(2,1)} %collective-permute-done.5.refs_2_), channel_id=1, source_target_pairs={{0,16},{16,0},{1,17},{17,1},{2,18},{18,2},{3,19},{19,3},{4,20},{20... | collective-permute-start | bytes 3145736 | tf_op jit(solution)/shard_map/ppermute | solution.py:268
  45.9 4.8 %late_attention.3.x_hbm = bf16[256,2048]{1,0:T(8,128)(2,1)} custom-call(s32[1]{0:T(128)} %bitcast.3.seq_ref.refs_0_, bf16[256,2048]{1,0:T(8,128)(2,1)} %bitcast.48, bf16[1792,1024]{1,0:T(8,128)(2,1)} %bitcast.41, bf16[256,1024]{1,0:T(8,128)(2,1)} %bitcast.52, bf16[1792,1024]{1,0:T(8,128)(2,1)} %collective-permute-done.1.ckb.refs_4_, ...), custom_call_target="tpu_custom_call", output_to_operand_aliasing={{}: (10, {})} | custom-call | flops 1 | bytes 1 | tf_op jit(solution)/shard_map/late_attention/pallas_call | solution.py:103
  52.7 10.5 %early_projection.1.refs_5_ = bf16[256,8192]{1,0:T(8,128)(2,1)} custom-call(s32[16,64]{1,0:T(8,128)S(1)} %select_reduce_fusion.table_ref, s32[8]{0:T(128)S(1)} %stack.110.rows_ref, s32[4]{0:T(128)S(1)} %iota_multiply_fusion.cols_ref, bf16[256,2048]{1,0:T(8,128)(2,1)} %late_attention.3.x_hbm, bf16[256,128,128]{2,1,0:T(8,128)(2,1)} %bitcast.35, ...), custom_call_target="tpu_custom_call" | custom-call | flops 1 | bytes 1 | tf_op jit(solution)/shard_map/early_projection/pallas_call | solution.py:228
  63.2 2.0 %collective-permute-done.7.refs_1_ = bf16[35,128,128]{2,1,0:T(8,128)(2,1)S(1)} collective-permute-done((bf16[35,128,128]{2,1,0:T(8,128)(2,1)}, bf16[35,128,128]{2,1,0:T(8,128)(2,1)S(1)}, u32[]{:S(2)}, u32[]{:S(2)}) %collective-permute-start.7) | collective-permute-done | bytes 1146912 | tf_op jit(solution)/shard_map/ppermute | solution.py:268
  65.2 3.1 %collective-permute-done.11.refs_2_ = bf16[32,128,128]{2,1,0:T(8,128)(2,1)S(1)} collective-permute-done((bf16[32,128,128]{2,1,0:T(8,128)(2,1)}, bf16[32,128,128]{2,1,0:T(8,128)(2,1)S(1)}, u32[]{:S(2)}, u32[]{:S(2)}) %collective-permute-start.11) | collective-permute-done | bytes 1048608 | tf_op jit(solution)/shard_map/ppermute | solution.py:268
  68.5 2.6 %collective-permute-done.13.refs_4_ = bf16[32,128,128]{2,1,0:T(8,128)(2,1)} collective-permute-done((bf16[32,128,128]{2,1,0:T(8,128)(2,1)S(1)}, bf16[32,128,128]{2,1,0:T(8,128)(2,1)}, u32[]{:S(2)}, u32[]{:S(2)}) %collective-permute-start.13) | collective-permute-done | bytes 1048608 | tf_op jit(solution)/shard_map/ppermute | solution.py:268
  71.1 7.6 %projection.3 = (bf16[128,2048]{1,0:T(8,128)(2,1)}, bf16[128,2048]{1,0:T(8,128)(2,1)}, bf16[128,2048]{1,0:T(8,128)(2,1)}, bf16[128,2048]{1,0:T(8,128)(2,1)}) custom-call(s32[16,64]{1,0:T(8,128)S(1)} %select_reduce_fusion.table_ref, s32[8]{0:T(128)S(1)} %stack.98.rows_ref, s32[2]{0:T(128)S(1)} %get-tuple-element.64.cols_ref, ...), custom_call_target="tpu_custom_call" | custom-call | flops 1 | bytes 1 | tf_op jit(solution)/shard_map/projection/pallas_call | solution.py:228
  78.7 3.7 %collective-permute-start.20 = (bf16[128,2048]{1,0:T(8,128)(2,1)}, bf16[128,2048]{1,0:T(8,128)(2,1)S(1)}, u32[]{:S(2)}, u32[]{:S(2)}) collective-permute-start(bf16[128,2048]{1,0:T(8,128)(2,1)} %get-tuple-element.54), channel_id=1, source_target_pairs={{0,4},{1,5},{2,6},{3,7},{16,20},{17,21},{18,22},{19,23}} | collective-permute-start | bytes 1572872 | tf_op jit(solution)/shard_map/ppermute | solution.py:261
  83.2 1.3 collective-permute-start.14
  85.2 7.6 %projection.2 = (bf16[128,2048]{1,0:T(8,128)(2,1)}, bf16[128,2048]{1,0:T(8,128)(2,1)}, bf16[128,2048]{1,0:T(8,128)(2,1)}, bf16[128,2048]{1,0:T(8,128)(2,1)}) custom-call(s32[16,64]{1,0:T(8,128)S(1)} %select_reduce_fusion.table_ref, s32[8]{0:T(128)S(1)} %stack.98.rows_ref, s32[2]{0:T(128)S(1)} %get-tuple-element.63.cols_ref, ...), custom_call_target="tpu_custom_call" | custom-call | flops 1 | bytes 1 | tf_op jit(solution)/shard_map/projection/pallas_call | solution.py:228
  92.8 2.2 %collective-permute-done.20 = bf16[128,2048]{1,0:T(8,128)(2,1)S(1)} collective-permute-done((bf16[128,2048]{1,0:T(8,128)(2,1)}, bf16[128,2048]{1,0:T(8,128)(2,1)S(1)}, u32[]{:S(2)}, u32[]{:S(2)}) %collective-permute-start.20) | collective-permute-done | bytes 524320 | tf_op jit(solution)/shard_map/ppermute | solution.py:261
  95.0 1.4 fusion.3
  96.4 4.3 %collective-permute-start.22 = (bf16[128,2048]{1,0:T(8,128)(2,1)S(1)}, bf16[128,2048]{1,0:T(8,128)(2,1)S(1)}, u32[]{:S(2)}, u32[]{:S(2)}) collective-permute-start(bf16[128,2048]{1,0:T(8,128)(2,1)S(1)} %get-tuple-element.62), channel_id=1, source_target_pairs={{0,4},{4,8},{1,5},{5,9},{2,6},{6,10},{3,7},{7,11},{16,20},{20,24},... | collective-permute-start | bytes 1572872 | tf_op jit(solution)/shard_map/ppermute | solution.py:261
  101.4 4.8 %collective-permute-done.14 = bf16[128,2048]{1,0:T(8,128)(2,1)S(1)} collective-permute-done((bf16[128,2048]{1,0:T(8,128)(2,1)}, bf16[128,2048]{1,0:T(8,128)(2,1)S(1)}, u32[]{:S(2)}, u32[]{:S(2)}) %collective-permute-start.14) | collective-permute-done | bytes 524320 | tf_op jit(solution)/shard_map/ppermute | solution.py:261
  106.2 1.4 fusion.1
  107.7 4.4 %collective-permute-start.16 = (bf16[128,2048]{1,0:T(8,128)(2,1)S(1)}, bf16[128,2048]{1,0:T(8,128)(2,1)S(1)}, u32[]{:S(2)}, u32[]{:S(2)}) collective-permute-start(bf16[128,2048]{1,0:T(8,128)(2,1)S(1)} %get-tuple-element.60), channel_id=1, source_target_pairs={{0,4},{4,8},{1,5},{5,9},{2,6},{6,10},{3,7},{7,11},{16,20},{20,24},... | collective-permute-start | bytes 1572872 | tf_op jit(solution)/shard_map/ppermute | solution.py:261
  112.8 4.5 %collective-permute-done.22 = bf16[128,2048]{1,0:T(8,128)(2,1)S(1)} collective-permute-done((bf16[128,2048]{1,0:T(8,128)(2,1)S(1)}, bf16[128,2048]{1,0:T(8,128)(2,1)S(1)}, u32[]{:S(2)}, u32[]{:S(2)}) %collective-permute-start.22) | collective-permute-done | bytes 524320 | tf_op jit(solution)/shard_map/ppermute | solution.py:261
  117.5 1.4 collective-permute-start.25
  119.1 5.0 %collective-permute-start.24 = (bf16[128,2048]{1,0:T(8,128)(2,1)S(1)}, bf16[128,2048]{1,0:T(8,128)(2,1)S(1)}, u32[]{:S(2)}, u32[]{:S(2)}) collective-permute-start(bf16[128,2048]{1,0:T(8,128)(2,1)S(1)} %add_convert_fusion.2), channel_id=1, source_target_pairs={{0,4},{4,8},{8,12},{1,5},{5,9},{9,13},{2,6},{6,10},{10,14},{3,7},{... | collective-permute-start | bytes 1572872 | tf_op jit(solution)/shard_map/ppermute | solution.py:261
  124.1 4.5 %collective-permute-done.16 = bf16[128,2048]{1,0:T(8,128)(2,1)S(1)} collective-permute-done((bf16[128,2048]{1,0:T(8,128)(2,1)S(1)}, bf16[128,2048]{1,0:T(8,128)(2,1)S(1)}, u32[]{:S(2)}, u32[]{:S(2)}) %collective-permute-start.16) | collective-permute-done | bytes 524320 | tf_op jit(solution)/shard_map/ppermute | solution.py:261
  130.2 5.1 %collective-permute-start.18 = (bf16[128,2048]{1,0:T(8,128)(2,1)S(1)}, bf16[128,2048]{1,0:T(8,128)(2,1)S(1)}, u32[]{:S(2)}, u32[]{:S(2)}) collective-permute-start(bf16[128,2048]{1,0:T(8,128)(2,1)S(1)} %add_convert_fusion.5), channel_id=1, source_target_pairs={{0,4},{4,8},{8,12},{1,5},{5,9},{9,13},{2,6},{6,10},{10,14},{3,7},{... | collective-permute-start | bytes 1572872 | tf_op jit(solution)/shard_map/ppermute | solution.py:261
  135.3 4.6 %collective-permute-done.24 = bf16[128,2048]{1,0:T(8,128)(2,1)S(1)} collective-permute-done((bf16[128,2048]{1,0:T(8,128)(2,1)S(1)}, bf16[128,2048]{1,0:T(8,128)(2,1)S(1)}, u32[]{:S(2)}, u32[]{:S(2)}) %collective-permute-start.24) | collective-permute-done | bytes 524320 | tf_op jit(solution)/shard_map/ppermute | solution.py:261
  140.1 3.8 %collective-permute-done.19 = bf16[128,2048]{1,0:T(8,128)(2,1)S(1)} collective-permute-done((bf16[128,2048]{1,0:T(8,128)(2,1)S(1)}, bf16[128,2048]{1,0:T(8,128)(2,1)S(1)}, u32[]{:S(2)}, u32[]{:S(2)}) %collective-permute-start.19) | collective-permute-done | bytes 524320 | tf_op jit(solution)/shard_map/ppermute | solution.py:262
  143.9 6.4 %collective-permute-done.18 = bf16[128,2048]{1,0:T(8,128)(2,1)S(1)} collective-permute-done((bf16[128,2048]{1,0:T(8,128)(2,1)S(1)}, bf16[128,2048]{1,0:T(8,128)(2,1)S(1)}, u32[]{:S(2)}, u32[]{:S(2)}) %collective-permute-start.18) | collective-permute-done | bytes 524320 | tf_op jit(solution)/shard_map/ppermute | solution.py:261
  (78 shorter events, 16.4 us)
Async XLA Ops:
  0.0 8.2 %collective-permute-start.1 = (bf16[1792,1024]{1,0:T(8,128)(2,1)}, bf16[1792,1024]{1,0:T(8,128)(2,1)}, u32[]{:S(2)}, u32[]{:S(2)}) collective-permute-start(bf16[1792,1024]{1,0:T(8,128)(2,1)} %bitcast.38), channel_id=1, source_target_pairs={{0,2},{2,0},{1,3},{3,1},{4,6},{6,4},{5,7},{7,5},{8,10},{10,8},{9,1... | collective-permute-start | bytes 11010056 | tf_op jit(solution)/shard_map/ppermute | solution.py:268
  0.5 13.1 %collective-permute-start.3 = (bf16[1792,1024]{1,0:T(8,128)(2,1)}, bf16[1792,1024]{1,0:T(8,128)(2,1)}, u32[]{:S(2)}, u32[]{:S(2)}) collective-permute-start(bf16[1792,1024]{1,0:T(8,128)(2,1)} %bitcast.42), channel_id=1, source_target_pairs={{0,2},{2,0},{1,3},{3,1},{4,6},{6,4},{5,7},{7,5},{8,10},{10,8},{9,1... | collective-permute-start | bytes 11010056 | tf_op jit(solution)/shard_map/ppermute | solution.py:268
  2.4 19.2 %collective-permute-start = (bf16[17,128,128]{2,1,0:T(8,128)(2,1)S(1)}, bf16[17,128,128]{2,1,0:T(8,128)(2,1)S(1)}, u32[]{:S(2)}, u32[]{:S(2)}) collective-permute-start(bf16[17,128,128]{2,1,0:T(8,128)(2,1)S(1)} %pad_maximum_fusion), channel_id=1, source_target_pairs={{0,1},{1,0},{2,3},{3,2},{4,5},{5,4},{6,7},{7,6},{8,9},{9,8},{10,11... | collective-permute-start | bytes 1671176 | tf_op jit(solution)/shard_map/ppermute | solution.py:268
  5.4 7.2 %collective-permute-start.2 = (bf16[256,1024]{1,0:T(8,128)(2,1)}, bf16[256,1024]{1,0:T(8,128)(2,1)S(1)}, u32[]{:S(2)}, u32[]{:S(2)}) collective-permute-start(bf16[256,1024]{1,0:T(8,128)(2,1)} %bitcast.49), channel_id=1, source_target_pairs={{0,2},{2,0},{1,3},{3,1},{4,6},{6,4},{5,7},{7,5},{8,10},{10,8},{9,1... | collective-permute-start | bytes 1572872 | tf_op jit(solution)/shard_map/ppermute | solution.py:268
  5.4 8.0 %collective-permute-start.4 = (bf16[256,1024]{1,0:T(8,128)(2,1)}, bf16[256,1024]{1,0:T(8,128)(2,1)S(1)}, u32[]{:S(2)}, u32[]{:S(2)}) collective-permute-start(bf16[256,1024]{1,0:T(8,128)(2,1)} %bitcast.53), channel_id=1, source_target_pairs={{0,2},{2,0},{1,3},{3,1},{4,6},{6,4},{5,7},{7,5},{8,10},{10,8},{9,1... | collective-permute-start | bytes 1572872 | tf_op jit(solution)/shard_map/ppermute | solution.py:268
  8.2 33.2 %collective-permute-start.5 = (bf16[32,128,128]{2,1,0:T(8,128)(2,1)}, bf16[32,128,128]{2,1,0:T(8,128)(2,1)}, u32[]{:S(2)}, u32[]{:S(2)}) collective-permute-start(bf16[32,128,128]{2,1,0:T(8,128)(2,1)} %constant_dynamic-slice_fusion), channel_id=1, source_target_pairs={{0,1},{1,0},{2,3},{3,2},{4,5},{5,4},{6,7},{7,6},{8,9},{9,8},{10,11... | collective-permute-start | bytes 3145736 | tf_op jit(solution)/shard_map/ppermute | solution.py:268
  21.5 24.1 %copy-start.13 = (s32[16,16]{1,0:T(8,128)S(1)}, s32[16,16]{1,0:T(8,128)}, u32[]{:S(2)}) copy-start(s32[16,16]{1,0:T(8,128)} %param.13) | copy-start | bytes 3076
  21.6 19.8 %collective-permute-start.6 = (bf16[17,128,128]{2,1,0:T(8,128)(2,1)S(1)}, bf16[17,128,128]{2,1,0:T(8,128)(2,1)S(1)}, u32[]{:S(2)}, u32[]{:S(2)}) collective-permute-start(bf16[17,128,128]{2,1,0:T(8,128)(2,1)S(1)} %collective-permute-done.refs_1_), channel_id=1, source_target_pairs={{0,16},{16,0},{1,17},{17,1},{2,18},{18,2},{3,19},{19,3},{4,20},{20... | collective-permute-start | bytes 1671176 | tf_op jit(solution)/shard_map/ppermute | solution.py:268
  23.9 41.3 %collective-permute-start.7 = (bf16[35,128,128]{2,1,0:T(8,128)(2,1)}, bf16[35,128,128]{2,1,0:T(8,128)(2,1)S(1)}, u32[]{:S(2)}, u32[]{:S(2)}) collective-permute-start(bf16[35,128,128]{2,1,0:T(8,128)(2,1)} %constant_dynamic-slice_fusion.1), channel_id=1, source_target_pairs={{0,1},{1,0},{2,3},{3,2},{4,5},{5,4},{6,7},{7,6},{8,9},{9,8},{10,11... | collective-permute-start | bytes 3440648 | tf_op jit(solution)/shard_map/ppermute | solution.py:268
  42.2 8.4 %collective-permute-start.9 = (bf16[32,128,128]{2,1,0:T(8,128)(2,1)}, bf16[32,128,128]{2,1,0:T(8,128)(2,1)S(1)}, u32[]{:S(2)}, u32[]{:S(2)}) collective-permute-start(bf16[32,128,128]{2,1,0:T(8,128)(2,1)} %collective-permute-done.5.refs_2_), channel_id=1, source_target_pairs={{0,2},{2,0},{1,3},{3,1},{4,6},{6,4},{5,7},{7,5},{8,10},{10,8},{9,1... | collective-permute-start | bytes 3145736 | tf_op jit(solution)/shard_map/ppermute | solution.py:268
  42.2 26.1 %collective-permute-start.11 = (bf16[32,128,128]{2,1,0:T(8,128)(2,1)}, bf16[32,128,128]{2,1,0:T(8,128)(2,1)S(1)}, u32[]{:S(2)}, u32[]{:S(2)}) collective-permute-start(bf16[32,128,128]{2,1,0:T(8,128)(2,1)} %collective-permute-done.5.refs_2_), channel_id=1, source_target_pairs={{0,16},{16,0},{1,17},{17,1},{2,18},{18,2},{3,19},{19,3},{4,20},{20... | collective-permute-start | bytes 3145736 | tf_op jit(solution)/shard_map/ppermute | solution.py:268
  44.5 6.2 %collective-permute-start.8 = (bf16[17,128,128]{2,1,0:T(8,128)(2,1)}, bf16[17,128,128]{2,1,0:T(8,128)(2,1)S(1)}, u32[]{:S(2)}, u32[]{:S(2)}) collective-permute-start(bf16[17,128,128]{2,1,0:T(8,128)(2,1)} %copy-done.3), channel_id=1, source_target_pairs={{0,2},{2,0},{1,3},{3,1},{4,6},{6,4},{5,7},{7,5},{8,10},{10,8},{9,1... | collective-permute-start | bytes 1671176 | tf_op jit(solution)/shard_map/ppermute | solution.py:268
  44.7 5.9 %collective-permute-start.10 = (bf16[17,128,128]{2,1,0:T(8,128)(2,1)}, bf16[17,128,128]{2,1,0:T(8,128)(2,1)S(1)}, u32[]{:S(2)}, u32[]{:S(2)}) collective-permute-start(bf16[17,128,128]{2,1,0:T(8,128)(2,1)} %copy-done.4), channel_id=1, source_target_pairs={{0,2},{2,0},{1,3},{3,1},{4,6},{6,4},{5,7},{7,5},{8,10},{10,8},{9,1... | collective-permute-start | bytes 1671176 | tf_op jit(solution)/shard_map/ppermute | solution.py:268
  65.2 5.9 %collective-permute-start.12 = (bf16[35,128,128]{2,1,0:T(8,128)(2,1)S(1)}, bf16[35,128,128]{2,1,0:T(8,128)(2,1)S(1)}, u32[]{:S(2)}, u32[]{:S(2)}) collective-permute-start(bf16[35,128,128]{2,1,0:T(8,128)(2,1)S(1)} %collective-permute-done.7.refs_1_), channel_id=1, source_target_pairs={{0,2},{2,0},{1,3},{3,1},{4,6},{6,4},{5,7},{7,5},{8,10},{10,8},{9,1... | collective-permute-start | bytes 3440648 | tf_op jit(solution)/shard_map/ppermute | solution.py:268
  68.3 2.8 %collective-permute-start.13 = (bf16[32,128,128]{2,1,0:T(8,128)(2,1)S(1)}, bf16[32,128,128]{2,1,0:T(8,128)(2,1)}, u32[]{:S(2)}, u32[]{:S(2)}) collective-permute-start(bf16[32,128,128]{2,1,0:T(8,128)(2,1)S(1)} %collective-permute-done.11.refs_2_), channel_id=1, source_target_pairs={{0,2},{2,0},{1,3},{3,1},{4,6},{6,4},{5,7},{7,5},{8,10},{10,8},{9,1... | collective-permute-start | bytes 3145736 | tf_op jit(solution)/shard_map/ppermute | solution.py:268
  78.7 16.3 %collective-permute-start.20 = (bf16[128,2048]{1,0:T(8,128)(2,1)}, bf16[128,2048]{1,0:T(8,128)(2,1)S(1)}, u32[]{:S(2)}, u32[]{:S(2)}) collective-permute-start(bf16[128,2048]{1,0:T(8,128)(2,1)} %get-tuple-element.54), channel_id=1, source_target_pairs={{0,4},{1,5},{2,6},{3,7},{16,20},{17,21},{18,22},{19,23}} | collective-permute-start | bytes 1572872 | tf_op jit(solution)/shard_map/ppermute | solution.py:261
  82.5 12.6 %collective-permute-start.21 = (bf16[128,2048]{1,0:T(8,128)(2,1)}, bf16[128,2048]{1,0:T(8,128)(2,1)S(1)}, u32[]{:S(2)}, u32[]{:S(2)}) collective-permute-start(bf16[128,2048]{1,0:T(8,128)(2,1)} %get-tuple-element.52), channel_id=1, source_target_pairs={{12,8},{13,9},{14,10},{15,11},{28,24},{29,25},{30,26},{31,27}} | collective-permute-start | bytes 1572872 | tf_op jit(solution)/shard_map/ppermute | solution.py:262
  83.2 23.1 %collective-permute-start.14 = (bf16[128,2048]{1,0:T(8,128)(2,1)}, bf16[128,2048]{1,0:T(8,128)(2,1)S(1)}, u32[]{:S(2)}, u32[]{:S(2)}) collective-permute-start(bf16[128,2048]{1,0:T(8,128)(2,1)} %get-tuple-element.46), channel_id=1, source_target_pairs={{0,4},{1,5},{2,6},{3,7},{16,20},{17,21},{18,22},{19,23}} | collective-permute-start | bytes 1572872 | tf_op jit(solution)/shard_map/ppermute | solution.py:261
  84.5 21.8 %collective-permute-start.15 = (bf16[128,2048]{1,0:T(8,128)(2,1)}, bf16[128,2048]{1,0:T(8,128)(2,1)S(1)}, u32[]{:S(2)}, u32[]{:S(2)}) collective-permute-start(bf16[128,2048]{1,0:T(8,128)(2,1)} %get-tuple-element.44), channel_id=1, source_target_pairs={{12,8},{13,9},{14,10},{15,11},{28,24},{29,25},{30,26},{31,27}} | collective-permute-start | bytes 1572872 | tf_op jit(solution)/shard_map/ppermute | solution.py:262
  92.8 24.6 %copy-start.10 = (bf16[128,2048]{1,0:T(8,128)(2,1)S(1)}, bf16[128,2048]{1,0:T(8,128)(2,1)}, u32[]{:S(2)}) copy-start(bf16[128,2048]{1,0:T(8,128)(2,1)} %get-tuple-element.54) | copy-start | bytes 1572868
  92.8 26.1 %copy-start.9 = (bf16[128,2048]{1,0:T(8,128)(2,1)S(1)}, bf16[128,2048]{1,0:T(8,128)(2,1)}, u32[]{:S(2)}) copy-start(bf16[128,2048]{1,0:T(8,128)(2,1)} %get-tuple-element.52) | copy-start | bytes 1572868
  95.0 33.6 %copy-start.8 = (bf16[128,2048]{1,0:T(8,128)(2,1)S(1)}, bf16[128,2048]{1,0:T(8,128)(2,1)}, u32[]{:S(2)}) copy-start(bf16[128,2048]{1,0:T(8,128)(2,1)} %get-tuple-element.46) | copy-start | bytes 1572868
  96.4 20.9 %collective-permute-start.22 = (bf16[128,2048]{1,0:T(8,128)(2,1)S(1)}, bf16[128,2048]{1,0:T(8,128)(2,1)S(1)}, u32[]{:S(2)}, u32[]{:S(2)}) collective-permute-start(bf16[128,2048]{1,0:T(8,128)(2,1)S(1)} %get-tuple-element.62), channel_id=1, source_target_pairs={{0,4},{4,8},{1,5},{5,9},{2,6},{6,10},{3,7},{7,11},{16,20},{20,24},... | collective-permute-start | bytes 1572872 | tf_op jit(solution)/shard_map/ppermute | solution.py:261
  100.7 16.6 %collective-permute-start.23 = (bf16[128,2048]{1,0:T(8,128)(2,1)S(1)}, bf16[128,2048]{1,0:T(8,128)(2,1)S(1)}, u32[]{:S(2)}, u32[]{:S(2)}) collective-permute-start(bf16[128,2048]{1,0:T(8,128)(2,1)S(1)} %get-tuple-element.61), channel_id=1, source_target_pairs={{8,4},{12,8},{9,5},{13,9},{10,6},{14,10},{11,7},{15,11},{24,20},{2... | collective-permute-start | bytes 1572872 | tf_op jit(solution)/shard_map/ppermute | solution.py:262
  107.7 32.2 %copy-start.12 = (bf16[128,2048]{1,0:T(8,128)(2,1)S(1)}, bf16[128,2048]{1,0:T(8,128)(2,1)}, u32[]{:S(2)}) copy-start(bf16[128,2048]{1,0:T(8,128)(2,1)} %get-tuple-element.51) | copy-start | bytes 1572868
  107.7 20.9 %collective-permute-start.16 = (bf16[128,2048]{1,0:T(8,128)(2,1)S(1)}, bf16[128,2048]{1,0:T(8,128)(2,1)S(1)}, u32[]{:S(2)}, u32[]{:S(2)}) collective-permute-start(bf16[128,2048]{1,0:T(8,128)(2,1)S(1)} %get-tuple-element.60), channel_id=1, source_target_pairs={{0,4},{4,8},{1,5},{5,9},{2,6},{6,10},{3,7},{7,11},{16,20},{20,24},... | collective-permute-start | bytes 1572872 | tf_op jit(solution)/shard_map/ppermute | solution.py:261
  112.1 16.5 %collective-permute-start.17 = (bf16[128,2048]{1,0:T(8,128)(2,1)S(1)}, bf16[128,2048]{1,0:T(8,128)(2,1)S(1)}, u32[]{:S(2)}, u32[]{:S(2)}) collective-permute-start(bf16[128,2048]{1,0:T(8,128)(2,1)S(1)} %get-tuple-element.59), channel_id=1, source_target_pairs={{8,4},{12,8},{9,5},{13,9},{10,6},{14,10},{11,7},{15,11},{24,20},{2... | collective-permute-start | bytes 1572872 | tf_op jit(solution)/shard_map/ppermute | solution.py:262
  117.5 32.8 %copy-start.11 = (bf16[128,2048]{1,0:T(8,128)(2,1)S(1)}, bf16[128,2048]{1,0:T(8,128)(2,1)}, u32[]{:S(2)}) copy-start(bf16[128,2048]{1,0:T(8,128)(2,1)} %get-tuple-element.43) | copy-start | bytes 1572868
  117.5 17.8 %collective-permute-start.25 = (bf16[128,2048]{1,0:T(8,128)(2,1)S(1)}, bf16[128,2048]{1,0:T(8,128)(2,1)S(1)}, u32[]{:S(2)}, u32[]{:S(2)}) collective-permute-start(bf16[128,2048]{1,0:T(8,128)(2,1)S(1)} %add_convert_fusion.1), channel_id=1, source_target_pairs={{4,0},{8,4},{12,8},{5,1},{9,5},{13,9},{6,2},{10,6},{14,10},{7,3},{... | collective-permute-start | bytes 1572872 | tf_op jit(solution)/shard_map/ppermute | solution.py:262
  119.1 20.7 %collective-permute-start.24 = (bf16[128,2048]{1,0:T(8,128)(2,1)S(1)}, bf16[128,2048]{1,0:T(8,128)(2,1)S(1)}, u32[]{:S(2)}, u32[]{:S(2)}) collective-permute-start(bf16[128,2048]{1,0:T(8,128)(2,1)S(1)} %add_convert_fusion.2), channel_id=1, source_target_pairs={{0,4},{4,8},{8,12},{1,5},{5,9},{9,13},{2,6},{6,10},{10,14},{3,7},{... | collective-permute-start | bytes 1572872 | tf_op jit(solution)/shard_map/ppermute | solution.py:261
  128.7 15.1 %collective-permute-start.19 = (bf16[128,2048]{1,0:T(8,128)(2,1)S(1)}, bf16[128,2048]{1,0:T(8,128)(2,1)S(1)}, u32[]{:S(2)}, u32[]{:S(2)}) collective-permute-start(bf16[128,2048]{1,0:T(8,128)(2,1)S(1)} %add_convert_fusion.4), channel_id=1, source_target_pairs={{4,0},{8,4},{12,8},{5,1},{9,5},{13,9},{6,2},{10,6},{14,10},{7,3},{... | collective-permute-start | bytes 1572872 | tf_op jit(solution)/shard_map/ppermute | solution.py:262
  130.2 20.1 %collective-permute-start.18 = (bf16[128,2048]{1,0:T(8,128)(2,1)S(1)}, bf16[128,2048]{1,0:T(8,128)(2,1)S(1)}, u32[]{:S(2)}, u32[]{:S(2)}) collective-permute-start(bf16[128,2048]{1,0:T(8,128)(2,1)S(1)} %add_convert_fusion.5), channel_id=1, source_target_pairs={{0,4},{4,8},{8,12},{1,5},{5,9},{9,13},{2,6},{6,10},{10,14},{3,7},{... | collective-permute-start | bytes 1572872 | tf_op jit(solution)/shard_map/ppermute | solution.py:261
  (8 other events, 48.2 us)

commit v6 on v5

--- a/solution.py
+++ b/solution.py
@@ -240,7 +240,7 @@
         columns,
         in_hbm(x),
         in_hbm(pieces[0]),
-        *[p if split else in_hbm(p) for p in pieces[1:]],
+        *pieces[1:],
         *(() if acc is None else (in_hbm(acc),)),
     )
 
@@ -249,19 +249,21 @@
     return sum(v.astype(jnp.float32) for v in values).astype(values[0].dtype)
 
 
-def line_scatter(parts, n):
+def line_scatter(sent_first, parts, n):
     arrived = [None, None]
     for step in range(1, n):
         for half in range(2):
-            up, down = parts(n - step)[half], parts(step)[half]
-            if arrived[half] is not None:
+            up, down = parts[n - step][half], parts[step][half]
+            if step == 1:
+                up = down = sent_first[half]
+            else:
                 from_below, from_above = lax.optimization_barrier(arrived[half])
                 up, down = add(up, from_below), add(down, from_above)
             arrived[half] = (
                 lax.ppermute(up, "tensor", [(i, i + 1) for i in range(step)]),
                 lax.ppermute(down, "tensor", [(i + 1, i) for i in range(n - 1 - step, n - 1)]),
             )
-    return jnp.concatenate([add(parts(0)[half], *arrived[half]) for half in range(2)], axis=0)
+    return jnp.concatenate([add(parts[0][half], *arrived[half]) for half in range(2)], axis=0)
 
 
 def swap(value, axis):
@@ -361,14 +363,10 @@
         )
         n = mesh.shape["tensor"]
         place = lax.axis_index("tensor")
-        sums = {}
-        for group in (sorted({n - 1, 1}), sorted(set(range(n)) - {n - 1, 1})):
-            if group:
-                columns = jnp.stack([(place + j) % n * row_blocks for j in group])
-                found = stage(plan, early, columns)
-                for i, j in enumerate(group):
-                    sums[j] = found[2 * i : 2 * i + 2]
-        return line_scatter(lambda j: sums[j], n)[None]
+        ends = jnp.where(place == 0, (n - 1) * row_blocks, 0).astype(jnp.int32)
+        sent_first = stage(plan, early, ends.reshape(1))
+        found = stage(plan, early, jnp.stack([(place + j) % n * row_blocks for j in range(n)]))
+        return line_scatter(sent_first, [found[2 * j : 2 * j + 2] for j in range(n)], n)[None]
     else:
         dp = mesh.shape["dp"]
         gathered = lax.all_gather(flat, "dp", axis=0, tiled=True)

time: 152 us -> 153 us (level)
  starting transfers between devices: 41.4 us -> 44.3 us
  local copies, waits for them, and re-layouts: 9.51 us -> 6.93 us
    ppermute x6, waiting for transfers between devices: 26.9 us -> 23.2 us  [line_scatter(): lax.ppermute(up, 'tensor', [(i, i + 1) for i in range(step)])]
    ppermute x14, waiting for transfers between devices: 10 us -> 13.2 us  [swap(): return lax.ppermute(value, axis, [(0, 1), (1, 0)])]
    unnamed x28 -> x26, local copies, waits for them, and re-layouts: 3.46 us -> 0.88 us
  transfers between devices with their start and end apart: 26 -> 26, of which waited for: 14 -> 11; matrix products, arithmetic and copies ran while one was open for 7% -> 8% of each run, Pallas kernels for 30% -> 31%
where the time goes in v6:
time: 153 us; the launch traced here: 152 us
  Pallas kernels  53.6 us (35%)
  starting transfers between devices  44.3 us (29%)
  waiting for transfers between devices  40.1 us (26%)
  other arithmetic  6.99 us (5%)
  local copies, waits for them, and re-layouts  6.93 us (5%)
    pallas_call x3, Pallas kernels, attention(): pl.pallas_call(body, out_shape=pltpu.HBM((rows, width), jnp.bfloat16), gr...  27.4 us
    pallas_call x3, Pallas kernels, projection(): pl.pallas_call(functools.partial(projection_body, sources, kept, acc is n...  26.2 us
    ppermute x6, starting transfers between devices, line_scatter(): lax.ppermute(up, 'tensor', [(i, i + 1) for i in range(step)])  25.2 us
    ppermute x6, waiting for transfers between devices, line_scatter(): lax.ppermute(up, 'tensor', [(i, i + 1) for i in range(step)])  23.2 us
    ppermute x14, waiting for transfers between devices, swap(): return lax.ppermute(value, axis, [(0, 1), (1, 0)])  13.2 us
    ppermute x14, starting transfers between devices, swap(): return lax.ppermute(value, axis, [(0, 1), (1, 0)])  12.7 us
    ppermute x6, starting transfers between devices, line_scatter(): lax.ppermute(down, 'tensor', [(i + 1, i) for i in range(n - 1 - step, n -...  6.39 us
    dynamic_slice x3, local copies, waits for them, and re-layouts, piece(): return lax.dynamic_slice_in_dim(flat, start * kept, count * kept + more, 0)  5.87 us
  transfers between devices with their start and end apart: 26, of which 11 were waited for; matrix products, arithmetic and copies ran while one was open for 8% of the time, Pallas kernels for 31%

profile of v6, /device:TPU:0, one launch (start us, length us, event | category | flops | bytes accessed | tf_op | source)
XLA Modules:
  0.0 152.3 jit_solution(146285653674241644)
XLA Ops:
  2.9 3.0 %collective-permute-start = (bf16[17,128,128]{2,1,0:T(8,128)(2,1)S(1)}, bf16[17,128,128]{2,1,0:T(8,128)(2,1)S(1)}, u32[]{:S(2)}, u32[]{:S(2)}) collective-permute-start(bf16[17,128,128]{2,1,0:T(8,128)(2,1)S(1)} %pad_maximum_fusion), channel_id=1, source_target_pairs={{0,1},{1,0},{2,3},{3,2},{4,5},{5,4},{6,7},{7,6},{8,9},{9,8},{10,11... | collective-permute-start | bytes 1671176 | tf_op jit(solution)/shard_map/ppermute | solution.py:270
  5.9 2.3 %constant_dynamic-slice_fusion = bf16[32,128,128]{2,1,0:T(8,128)(2,1)} fusion(bf16[256,128,128]{2,1,0:T(8,128)(2,1)} %bitcast.34, s32[]{:T(128)S(6)} %select_n.43), kind=kLoop, calls=%fused_computation.22 | loop fusion | bytes 2097156 | tf_op jit(solution)/shard_map/dynamic_slice | solution.py:306
  8.2 1.6 %collective-permute-start.5 = (bf16[32,128,128]{2,1,0:T(8,128)(2,1)}, bf16[32,128,128]{2,1,0:T(8,128)(2,1)}, u32[]{:S(2)}, u32[]{:S(2)}) collective-permute-start(bf16[32,128,128]{2,1,0:T(8,128)(2,1)} %constant_dynamic-slice_fusion), channel_id=1, source_target_pairs={{0,1},{1,0},{2,3},{3,2},{4,5},{5,4},{6,7},{7,6},{8,9},{9,8},{10,11... | collective-permute-start | bytes 3145736 | tf_op jit(solution)/shard_map/ppermute | solution.py:270
  9.8 2.5 %constant_dynamic-slice_fusion.1 = bf16[35,128,128]{2,1,0:T(8,128)(2,1)} fusion(bf16[256,128,128]{2,1,0:T(8,128)(2,1)} %bitcast.35, s32[]{:T(128)S(6)} %select_n.37), kind=kLoop, calls=%fused_computation.23 | loop fusion | bytes 2293764 | tf_op jit(solution)/shard_map/dynamic_slice | solution.py:306
  13.6 7.4 %attention.1.refs_10_ = bf16[256,2048]{1,0:T(8,128)(2,1)} custom-call(s32[1]{0:T(128)} %bitcast.3.seq_ref.refs_0_, bf16[256,2048]{1,0:T(8,128)(2,1)} %bitcast.47, bf16[1792,1024]{1,0:T(8,128)(2,1)} %bitcast.40, bf16[256,1024]{1,0:T(8,128)(2,1)} %bitcast.51, bf16[1792,1024]{1,0:T(8,128)(2,1)} %collective-permute-done.1.ckb.refs_4_, ...), custom_call_target="tpu_custom_call" | custom-call | flops 1 | bytes 1 | tf_op jit(solution)/shard_map/attention/pallas_call | solution.py:103
  21.0 3.0 %collective-permute-start.6 = (bf16[17,128,128]{2,1,0:T(8,128)(2,1)S(1)}, bf16[17,128,128]{2,1,0:T(8,128)(2,1)S(1)}, u32[]{:S(2)}, u32[]{:S(2)}) collective-permute-start(bf16[17,128,128]{2,1,0:T(8,128)(2,1)S(1)} %collective-permute-done.refs_1_), channel_id=1, source_target_pairs={{0,16},{16,0},{1,17},{17,1},{2,18},{18,2},{3,19},{19,3},{4,20},{20... | collective-permute-start | bytes 1671176 | tf_op jit(solution)/shard_map/ppermute | solution.py:270
  23.9 1.5 collective-permute-start.7
  25.4 15.1 %late_attention.2.refs_10_ = bf16[256,2048]{1,0:T(8,128)(2,1)} custom-call(s32[1]{0:T(128)} %bitcast.3.seq_ref.refs_0_, bf16[256,2048]{1,0:T(8,128)(2,1)} %bitcast.48, bf16[1792,1024]{1,0:T(8,128)(2,1)} %bitcast.41, bf16[256,1024]{1,0:T(8,128)(2,1)} %bitcast.52, ...), custom_call_target="tpu_custom_call", output_to_operand_aliasing={{}: (10, {})} | custom-call | flops 1 | bytes 1 | tf_op jit(solution)/shard_map/late_attention/pallas_call | solution.py:103
  40.6 1.3 collective-permute-done.5.refs_2_
  42.7 2.1 %collective-permute-start.11 = (bf16[32,128,128]{2,1,0:T(8,128)(2,1)}, bf16[32,128,128]{2,1,0:T(8,128)(2,1)S(1)}, u32[]{:S(2)}, u32[]{:S(2)}) collective-permute-start(bf16[32,128,128]{2,1,0:T(8,128)(2,1)} %collective-permute-done.5.refs_2_), channel_id=1, source_target_pairs={{0,16},{16,0},{1,17},{17,1},{2,18},{18,2},{3,19},{19,3},{4,20},{20... | collective-permute-start | bytes 3145736 | tf_op jit(solution)/shard_map/ppermute | solution.py:270
  46.4 4.8 %late_attention.3.x_hbm = bf16[256,2048]{1,0:T(8,128)(2,1)} custom-call(s32[1]{0:T(128)} %bitcast.3.seq_ref.refs_0_, bf16[256,2048]{1,0:T(8,128)(2,1)} %bitcast.49, bf16[1792,1024]{1,0:T(8,128)(2,1)} %bitcast.42, bf16[256,1024]{1,0:T(8,128)(2,1)} %bitcast.53, bf16[1792,1024]{1,0:T(8,128)(2,1)} %collective-permute-done.1.ckb.refs_4_, ...), custom_call_target="tpu_custom_call", output_to_operand_aliasing={{}: (10, {})} | custom-call | flops 1 | bytes 1 | tf_op jit(solution)/shard_map/late_attention/pallas_call | solution.py:103
  51.3 9.7 %early_projection.1.refs_5_ = bf16[256,8192]{1,0:T(8,128)(2,1)} custom-call(s32[16,64]{1,0:T(8,128)S(1)} %select_reduce_fusion.table_ref, s32[8]{0:T(128)S(1)} %stack.109.rows_ref, s32[4]{0:T(128)S(1)} %iota_multiply_fusion.cols_ref, bf16[256,2048]{1,0:T(8,128)(2,1)} %late_attention.3.x_hbm, bf16[256,128,128]{2,1,0:T(8,128)(2,1)} %bitcast.36, ...), custom_call_target="tpu_custom_call" | custom-call | flops 1 | bytes 1 | tf_op jit(solution)/shard_map/early_projection/pallas_call | solution.py:228
  61.0 4.7 %collective-permute-done.7.refs_1_ = bf16[35,128,128]{2,1,0:T(8,128)(2,1)S(1)} collective-permute-done((bf16[35,128,128]{2,1,0:T(8,128)(2,1)}, bf16[35,128,128]{2,1,0:T(8,128)(2,1)S(1)}, u32[]{:S(2)}, u32[]{:S(2)}) %collective-permute-start.7) | collective-permute-done | bytes 1146912 | tf_op jit(solution)/shard_map/ppermute | solution.py:270
  65.7 3.1 %collective-permute-done.11.refs_2_ = bf16[32,128,128]{2,1,0:T(8,128)(2,1)S(1)} collective-permute-done((bf16[32,128,128]{2,1,0:T(8,128)(2,1)}, bf16[32,128,128]{2,1,0:T(8,128)(2,1)S(1)}, u32[]{:S(2)}, u32[]{:S(2)}) %collective-permute-start.11) | collective-permute-done | bytes 1048608 | tf_op jit(solution)/shard_map/ppermute | solution.py:270
  69.0 2.7 %collective-permute-done.13.refs_4_ = bf16[32,128,128]{2,1,0:T(8,128)(2,1)} collective-permute-done((bf16[32,128,128]{2,1,0:T(8,128)(2,1)S(1)}, bf16[32,128,128]{2,1,0:T(8,128)(2,1)}, u32[]{:S(2)}, u32[]{:S(2)}) %collective-permute-start.13) | collective-permute-done | bytes 1048608 | tf_op jit(solution)/shard_map/ppermute | solution.py:270
  71.7 6.3 %projection.3 = (bf16[128,2048]{1,0:T(8,128)(2,1)}, bf16[128,2048]{1,0:T(8,128)(2,1)}) custom-call(s32[16,64]{1,0:T(8,128)S(1)} %select_reduce_fusion.table_ref, s32[8]{0:T(128)S(1)} %stack.95.rows_ref, s32[1]{0:T(128)} %bitcast.29.cols_ref, bf16[256,2048]{1,0:T(8,128)(2,1)} %late_attention.3.x_hbm, bf16[256,128,128]{2,1,0:T(8,128)(2,1)} %bitcast.37, ...), custom_call_target="tpu_custom_call" | custom-call | flops 1 | bytes 1 | tf_op jit(solution)/shard_map/projection/pallas_call | solution.py:228
  77.9 1.5 collective-permute-start.15
  79.4 4.5 %collective-permute-start.14 = (bf16[128,2048]{1,0:T(8,128)(2,1)}, bf16[128,2048]{1,0:T(8,128)(2,1)}, u32[]{:S(2)}, u32[]{:S(2)}) collective-permute-start(bf16[128,2048]{1,0:T(8,128)(2,1)} %get-tuple-element.48), channel_id=1, source_target_pairs={{0,4},{1,5},{2,6},{3,7},{16,20},{17,21},{18,22},{19,23}} | collective-permute-start | bytes 1572872 | tf_op jit(solution)/shard_map/ppermute | solution.py:263
  86.0 10.2 %projection.2 = (bf16[128,2048]{1,0:T(8,128)(2,1)}, bf16[128,2048]{1,0:T(8,128)(2,1)}, bf16[128,2048]{1,0:T(8,128)(2,1)}, bf16[128,2048]{1,0:T(8,128)(2,1)}, bf1...) custom-call(s32[16,64]{1,0:T(8,128)S(1)} %select_reduce_fusion.table_, ...), custom_call_target="tpu_custom_call" | custom-call | flops 1 | bytes 1 | tf_op jit(solution)/shard_map/projection/pallas_call | solution.py:228
  96.3 1.8 %fusion.1 = (bf16[128,2048]{1,0:T(8,128)(2,1)S(1)}, bf16[128,2048]{1,0:T(8,128)(2,1)S(1)}) fusion(bf16[128,2048]{1,0:T(8,128)(2,1)} %get-tuple-element.47, bf16[128,2048]{1,0:T(8,128)(2,1)} %collective-permute-done.15, bf16[128,2048]{1,0:T(8,128)(2,1)} %collective-permute-done.14), kind=kLoop, calls=%fused_computation.5 | loop fusion | flops 1835008 | bytes 2621440 | tf_op jit(solution)/shard_map/convert_element_type | solution.py:249
  98.8 4.4 %collective-permute-start.16 = (bf16[128,2048]{1,0:T(8,128)(2,1)S(1)}, bf16[128,2048]{1,0:T(8,128)(2,1)S(1)}, u32[]{:S(2)}, u32[]{:S(2)}) collective-permute-start(bf16[128,2048]{1,0:T(8,128)(2,1)S(1)} %get-tuple-element.64), channel_id=1, source_target_pairs={{0,4},{4,8},{1,5},{5,9},{2,6},{6,10},{3,7},{7,11},{16,20},{20,24},... | collective-permute-start | bytes 1572872 | tf_op jit(solution)/shard_map/ppermute | solution.py:263
  103.2 3.8 %collective-permute-done.20 = bf16[128,2048]{1,0:T(8,128)(2,1)S(1)} collective-permute-done((bf16[128,2048]{1,0:T(8,128)(2,1)}, bf16[128,2048]{1,0:T(8,128)(2,1)S(1)}, u32[]{:S(2)}, u32[]{:S(2)}) %collective-permute-start.20) | collective-permute-done | bytes 524320 | tf_op jit(solution)/shard_map/ppermute | solution.py:263
  106.9 1.4 fusion.3
  109.2 4.9 %collective-permute-start.22 = (bf16[128,2048]{1,0:T(8,128)(2,1)S(1)}, bf16[128,2048]{1,0:T(8,128)(2,1)S(1)}, u32[]{:S(2)}, u32[]{:S(2)}) collective-permute-start(bf16[128,2048]{1,0:T(8,128)(2,1)S(1)} %get-tuple-element.66), channel_id=1, source_target_pairs={{0,4},{4,8},{1,5},{5,9},{2,6},{6,10},{3,7},{7,11},{16,20},{20,24},... | collective-permute-start | bytes 1572872 | tf_op jit(solution)/shard_map/ppermute | solution.py:263
  114.1 3.9 %collective-permute-done.16 = bf16[128,2048]{1,0:T(8,128)(2,1)S(1)} collective-permute-done((bf16[128,2048]{1,0:T(8,128)(2,1)S(1)}, bf16[128,2048]{1,0:T(8,128)(2,1)S(1)}, u32[]{:S(2)}, u32[]{:S(2)}) %collective-permute-start.16) | collective-permute-done | bytes 524320 | tf_op jit(solution)/shard_map/ppermute | solution.py:263
  118.2 1.4 collective-permute-start.19
  119.8 5.0 %collective-permute-start.18 = (bf16[128,2048]{1,0:T(8,128)(2,1)S(1)}, bf16[128,2048]{1,0:T(8,128)(2,1)S(1)}, u32[]{:S(2)}, u32[]{:S(2)}) collective-permute-start(bf16[128,2048]{1,0:T(8,128)(2,1)S(1)} %add_convert_fusion.5), channel_id=1, source_target_pairs={{0,4},{4,8},{8,12},{1,5},{5,9},{9,13},{2,6},{6,10},{10,14},{3,7},{... | collective-permute-start | bytes 1572872 | tf_op jit(solution)/shard_map/ppermute | solution.py:263
  124.9 4.4 %collective-permute-done.22 = bf16[128,2048]{1,0:T(8,128)(2,1)S(1)} collective-permute-done((bf16[128,2048]{1,0:T(8,128)(2,1)S(1)}, bf16[128,2048]{1,0:T(8,128)(2,1)S(1)}, u32[]{:S(2)}, u32[]{:S(2)}) %collective-permute-start.22) | collective-permute-done | bytes 524320 | tf_op jit(solution)/shard_map/ppermute | solution.py:263
  130.9 5.0 %collective-permute-start.24 = (bf16[128,2048]{1,0:T(8,128)(2,1)S(1)}, bf16[128,2048]{1,0:T(8,128)(2,1)S(1)}, u32[]{:S(2)}, u32[]{:S(2)}) collective-permute-start(bf16[128,2048]{1,0:T(8,128)(2,1)S(1)} %add_convert_fusion.2), channel_id=1, source_target_pairs={{0,4},{4,8},{8,12},{1,5},{5,9},{9,13},{2,6},{6,10},{10,14},{3,7},{... | collective-permute-start | bytes 1572872 | tf_op jit(solution)/shard_map/ppermute | solution.py:263
  136.0 4.6 %collective-permute-done.18 = bf16[128,2048]{1,0:T(8,128)(2,1)S(1)} collective-permute-done((bf16[128,2048]{1,0:T(8,128)(2,1)S(1)}, bf16[128,2048]{1,0:T(8,128)(2,1)S(1)}, u32[]{:S(2)}, u32[]{:S(2)}) %collective-permute-start.18) | collective-permute-done | bytes 524320 | tf_op jit(solution)/shard_map/ppermute | solution.py:263
  140.8 3.7 %collective-permute-done.25 = bf16[128,2048]{1,0:T(8,128)(2,1)S(1)} collective-permute-done((bf16[128,2048]{1,0:T(8,128)(2,1)S(1)}, bf16[128,2048]{1,0:T(8,128)(2,1)S(1)}, u32[]{:S(2)}, u32[]{:S(2)}) %collective-permute-start.25) | collective-permute-done | bytes 524320 | tf_op jit(solution)/shard_map/ppermute | solution.py:264
  144.5 6.4 %collective-permute-done.24 = bf16[128,2048]{1,0:T(8,128)(2,1)S(1)} collective-permute-done((bf16[128,2048]{1,0:T(8,128)(2,1)S(1)}, bf16[128,2048]{1,0:T(8,128)(2,1)S(1)}, u32[]{:S(2)}, u32[]{:S(2)}) %collective-permute-start.24) | collective-permute-done | bytes 524320 | tf_op jit(solution)/shard_map/ppermute | solution.py:263
  (76 shorter events, 13.6 us)
Async XLA Ops:
  0.0 8.2 %collective-permute-start.1 = (bf16[1792,1024]{1,0:T(8,128)(2,1)}, bf16[1792,1024]{1,0:T(8,128)(2,1)}, u32[]{:S(2)}, u32[]{:S(2)}) collective-permute-start(bf16[1792,1024]{1,0:T(8,128)(2,1)} %bitcast.39), channel_id=1, source_target_pairs={{0,2},{2,0},{1,3},{3,1},{4,6},{6,4},{5,7},{7,5},{8,10},{10,8},{9,1... | collective-permute-start | bytes 11010056 | tf_op jit(solution)/shard_map/ppermute | solution.py:270
  0.5 13.1 %collective-permute-start.3 = (bf16[1792,1024]{1,0:T(8,128)(2,1)}, bf16[1792,1024]{1,0:T(8,128)(2,1)}, u32[]{:S(2)}, u32[]{:S(2)}) collective-permute-start(bf16[1792,1024]{1,0:T(8,128)(2,1)} %bitcast.43), channel_id=1, source_target_pairs={{0,2},{2,0},{1,3},{3,1},{4,6},{6,4},{5,7},{7,5},{8,10},{10,8},{9,1... | collective-permute-start | bytes 11010056 | tf_op jit(solution)/shard_map/ppermute | solution.py:270
  0.5 11.8 %collective-permute-start.2 = (bf16[256,1024]{1,0:T(8,128)(2,1)}, bf16[256,1024]{1,0:T(8,128)(2,1)S(1)}, u32[]{:S(2)}, u32[]{:S(2)}) collective-permute-start(bf16[256,1024]{1,0:T(8,128)(2,1)} %bitcast.50), channel_id=1, source_target_pairs={{0,2},{2,0},{1,3},{3,1},{4,6},{6,4},{5,7},{7,5},{8,10},{10,8},{9,1... | collective-permute-start | bytes 1572872 | tf_op jit(solution)/shard_map/ppermute | solution.py:270
  1.0 11.4 %collective-permute-start.4 = (bf16[256,1024]{1,0:T(8,128)(2,1)}, bf16[256,1024]{1,0:T(8,128)(2,1)S(1)}, u32[]{:S(2)}, u32[]{:S(2)}) collective-permute-start(bf16[256,1024]{1,0:T(8,128)(2,1)} %bitcast.54), channel_id=1, source_target_pairs={{0,2},{2,0},{1,3},{3,1},{4,6},{6,4},{5,7},{7,5},{8,10},{10,8},{9,1... | collective-permute-start | bytes 1572872 | tf_op jit(solution)/shard_map/ppermute | solution.py:270
  2.9 18.1 %collective-permute-start = (bf16[17,128,128]{2,1,0:T(8,128)(2,1)S(1)}, bf16[17,128,128]{2,1,0:T(8,128)(2,1)S(1)}, u32[]{:S(2)}, u32[]{:S(2)}) collective-permute-start(bf16[17,128,128]{2,1,0:T(8,128)(2,1)S(1)} %pad_maximum_fusion), channel_id=1, source_target_pairs={{0,1},{1,0},{2,3},{3,2},{4,5},{5,4},{6,7},{7,6},{8,9},{9,8},{10,11... | collective-permute-start | bytes 1671176 | tf_op jit(solution)/shard_map/ppermute | solution.py:270
  8.2 33.7 %collective-permute-start.5 = (bf16[32,128,128]{2,1,0:T(8,128)(2,1)}, bf16[32,128,128]{2,1,0:T(8,128)(2,1)}, u32[]{:S(2)}, u32[]{:S(2)}) collective-permute-start(bf16[32,128,128]{2,1,0:T(8,128)(2,1)} %constant_dynamic-slice_fusion), channel_id=1, source_target_pairs={{0,1},{1,0},{2,3},{3,2},{4,5},{5,4},{6,7},{7,6},{8,9},{9,8},{10,11... | collective-permute-start | bytes 3145736 | tf_op jit(solution)/shard_map/ppermute | solution.py:270
  21.0 25.2 %copy-start.12 = (s32[16,16]{1,0:T(8,128)S(1)}, s32[16,16]{1,0:T(8,128)}, u32[]{:S(2)}) copy-start(s32[16,16]{1,0:T(8,128)} %param.13) | copy-start | bytes 3076
  21.0 20.9 %collective-permute-start.6 = (bf16[17,128,128]{2,1,0:T(8,128)(2,1)S(1)}, bf16[17,128,128]{2,1,0:T(8,128)(2,1)S(1)}, u32[]{:S(2)}, u32[]{:S(2)}) collective-permute-start(bf16[17,128,128]{2,1,0:T(8,128)(2,1)S(1)} %collective-permute-done.refs_1_), channel_id=1, source_target_pairs={{0,16},{16,0},{1,17},{17,1},{2,18},{18,2},{3,19},{19,3},{4,20},{20... | collective-permute-start | bytes 1671176 | tf_op jit(solution)/shard_map/ppermute | solution.py:270
  23.9 41.8 %collective-permute-start.7 = (bf16[35,128,128]{2,1,0:T(8,128)(2,1)}, bf16[35,128,128]{2,1,0:T(8,128)(2,1)S(1)}, u32[]{:S(2)}, u32[]{:S(2)}) collective-permute-start(bf16[35,128,128]{2,1,0:T(8,128)(2,1)} %constant_dynamic-slice_fusion.1), channel_id=1, source_target_pairs={{0,1},{1,0},{2,3},{3,2},{4,5},{5,4},{6,7},{7,6},{8,9},{9,8},{10,11... | collective-permute-start | bytes 3440648 | tf_op jit(solution)/shard_map/ppermute | solution.py:270
  42.7 8.5 %collective-permute-start.9 = (bf16[32,128,128]{2,1,0:T(8,128)(2,1)}, bf16[32,128,128]{2,1,0:T(8,128)(2,1)S(1)}, u32[]{:S(2)}, u32[]{:S(2)}) collective-permute-start(bf16[32,128,128]{2,1,0:T(8,128)(2,1)} %collective-permute-done.5.refs_2_), channel_id=1, source_target_pairs={{0,2},{2,0},{1,3},{3,1},{4,6},{6,4},{5,7},{7,5},{8,10},{10,8},{9,1... | collective-permute-start | bytes 3145736 | tf_op jit(solution)/shard_map/ppermute | solution.py:270
  42.7 26.1 %collective-permute-start.11 = (bf16[32,128,128]{2,1,0:T(8,128)(2,1)}, bf16[32,128,128]{2,1,0:T(8,128)(2,1)S(1)}, u32[]{:S(2)}, u32[]{:S(2)}) collective-permute-start(bf16[32,128,128]{2,1,0:T(8,128)(2,1)} %collective-permute-done.5.refs_2_), channel_id=1, source_target_pairs={{0,16},{16,0},{1,17},{17,1},{2,18},{18,2},{3,19},{19,3},{4,20},{20... | collective-permute-start | bytes 3145736 | tf_op jit(solution)/shard_map/ppermute | solution.py:270
  45.0 6.3 %collective-permute-start.8 = (bf16[17,128,128]{2,1,0:T(8,128)(2,1)}, bf16[17,128,128]{2,1,0:T(8,128)(2,1)S(1)}, u32[]{:S(2)}, u32[]{:S(2)}) collective-permute-start(bf16[17,128,128]{2,1,0:T(8,128)(2,1)} %copy-done), channel_id=1, source_target_pairs={{0,2},{2,0},{1,3},{3,1},{4,6},{6,4},{5,7},{7,5},{8,10},{10,8},{9,1... | collective-permute-start | bytes 1671176 | tf_op jit(solution)/shard_map/ppermute | solution.py:270
  45.2 6.0 %collective-permute-start.10 = (bf16[17,128,128]{2,1,0:T(8,128)(2,1)}, bf16[17,128,128]{2,1,0:T(8,128)(2,1)S(1)}, u32[]{:S(2)}, u32[]{:S(2)}) collective-permute-start(bf16[17,128,128]{2,1,0:T(8,128)(2,1)} %copy-done.2), channel_id=1, source_target_pairs={{0,2},{2,0},{1,3},{3,1},{4,6},{6,4},{5,7},{7,5},{8,10},{10,8},{9,1... | collective-permute-start | bytes 1671176 | tf_op jit(solution)/shard_map/ppermute | solution.py:270
  65.7 5.9 %collective-permute-start.12 = (bf16[35,128,128]{2,1,0:T(8,128)(2,1)S(1)}, bf16[35,128,128]{2,1,0:T(8,128)(2,1)S(1)}, u32[]{:S(2)}, u32[]{:S(2)}) collective-permute-start(bf16[35,128,128]{2,1,0:T(8,128)(2,1)S(1)} %collective-permute-done.7.refs_1_), channel_id=1, source_target_pairs={{0,2},{2,0},{1,3},{3,1},{4,6},{6,4},{5,7},{7,5},{8,10},{10,8},{9,1... | collective-permute-start | bytes 3440648 | tf_op jit(solution)/shard_map/ppermute | solution.py:270
  68.9 2.8 %collective-permute-start.13 = (bf16[32,128,128]{2,1,0:T(8,128)(2,1)S(1)}, bf16[32,128,128]{2,1,0:T(8,128)(2,1)}, u32[]{:S(2)}, u32[]{:S(2)}) collective-permute-start(bf16[32,128,128]{2,1,0:T(8,128)(2,1)S(1)} %collective-permute-done.11.refs_2_), channel_id=1, source_target_pairs={{0,2},{2,0},{1,3},{3,1},{4,6},{6,4},{5,7},{7,5},{8,10},{10,8},{9,1... | collective-permute-start | bytes 3145736 | tf_op jit(solution)/shard_map/ppermute | solution.py:270
  77.9 18.3 %collective-permute-start.15 = (bf16[128,2048]{1,0:T(8,128)(2,1)}, bf16[128,2048]{1,0:T(8,128)(2,1)}, u32[]{:S(2)}, u32[]{:S(2)}) collective-permute-start(bf16[128,2048]{1,0:T(8,128)(2,1)} %get-tuple-element.48), channel_id=1, source_target_pairs={{12,8},{13,9},{14,10},{15,11},{28,24},{29,25},{30,26},{31,27}} | collective-permute-start | bytes 1572872 | tf_op jit(solution)/shard_map/ppermute | solution.py:264
  79.4 16.9 %collective-permute-start.14 = (bf16[128,2048]{1,0:T(8,128)(2,1)}, bf16[128,2048]{1,0:T(8,128)(2,1)}, u32[]{:S(2)}, u32[]{:S(2)}) collective-permute-start(bf16[128,2048]{1,0:T(8,128)(2,1)} %get-tuple-element.48), channel_id=1, source_target_pairs={{0,4},{1,5},{2,6},{3,7},{16,20},{17,21},{18,22},{19,23}} | collective-permute-start | bytes 1572872 | tf_op jit(solution)/shard_map/ppermute | solution.py:263
  84.0 19.2 %collective-permute-start.21 = (bf16[128,2048]{1,0:T(8,128)(2,1)}, bf16[128,2048]{1,0:T(8,128)(2,1)S(1)}, u32[]{:S(2)}, u32[]{:S(2)}) collective-permute-start(bf16[128,2048]{1,0:T(8,128)(2,1)} %get-tuple-element.57), channel_id=1, source_target_pairs={{12,8},{13,9},{14,10},{15,11},{28,24},{29,25},{30,26},{31,27}} | collective-permute-start | bytes 1572872 | tf_op jit(solution)/shard_map/ppermute | solution.py:264
  84.7 22.3 %collective-permute-start.20 = (bf16[128,2048]{1,0:T(8,128)(2,1)}, bf16[128,2048]{1,0:T(8,128)(2,1)S(1)}, u32[]{:S(2)}, u32[]{:S(2)}) collective-permute-start(bf16[128,2048]{1,0:T(8,128)(2,1)} %get-tuple-element.57), channel_id=1, source_target_pairs={{0,4},{1,5},{2,6},{3,7},{16,20},{17,21},{18,22},{19,23}} | collective-permute-start | bytes 1572872 | tf_op jit(solution)/shard_map/ppermute | solution.py:263
  96.3 23.4 %copy-start.8 = (bf16[128,2048]{1,0:T(8,128)(2,1)S(1)}, bf16[128,2048]{1,0:T(8,128)(2,1)}, u32[]{:S(2)}) copy-start(bf16[128,2048]{1,0:T(8,128)(2,1)} %get-tuple-element.46) | copy-start | bytes 1572868
  96.3 33.0 %copy-start.7 = (bf16[128,2048]{1,0:T(8,128)(2,1)S(1)}, bf16[128,2048]{1,0:T(8,128)(2,1)}, u32[]{:S(2)}) copy-start(bf16[128,2048]{1,0:T(8,128)(2,1)} %get-tuple-element.61) | copy-start | bytes 1572868
  98.1 16.0 %collective-permute-start.17 = (bf16[128,2048]{1,0:T(8,128)(2,1)S(1)}, bf16[128,2048]{1,0:T(8,128)(2,1)S(1)}, u32[]{:S(2)}, u32[]{:S(2)}) collective-permute-start(bf16[128,2048]{1,0:T(8,128)(2,1)S(1)} %get-tuple-element.63), channel_id=1, source_target_pairs={{8,4},{12,8},{9,5},{13,9},{10,6},{14,10},{11,7},{15,11},{24,20},{2... | collective-permute-start | bytes 1572872 | tf_op jit(solution)/shard_map/ppermute | solution.py:264
  98.8 19.3 %collective-permute-start.16 = (bf16[128,2048]{1,0:T(8,128)(2,1)S(1)}, bf16[128,2048]{1,0:T(8,128)(2,1)S(1)}, u32[]{:S(2)}, u32[]{:S(2)}) collective-permute-start(bf16[128,2048]{1,0:T(8,128)(2,1)S(1)} %get-tuple-element.64), channel_id=1, source_target_pairs={{0,4},{4,8},{1,5},{5,9},{2,6},{6,10},{3,7},{7,11},{16,20},{20,24},... | collective-permute-start | bytes 1572872 | tf_op jit(solution)/shard_map/ppermute | solution.py:263
  106.9 23.8 %copy-start.6 = (bf16[128,2048]{1,0:T(8,128)(2,1)S(1)}, bf16[128,2048]{1,0:T(8,128)(2,1)}, u32[]{:S(2)}) copy-start(bf16[128,2048]{1,0:T(8,128)(2,1)} %get-tuple-element.55) | copy-start | bytes 1572868
  108.4 32.2 %copy-start.11 = (bf16[128,2048]{1,0:T(8,128)(2,1)S(1)}, bf16[128,2048]{1,0:T(8,128)(2,1)}, u32[]{:S(2)}) copy-start(bf16[128,2048]{1,0:T(8,128)(2,1)} %get-tuple-element.45) | copy-start | bytes 1572868
  108.4 16.5 %collective-permute-start.23 = (bf16[128,2048]{1,0:T(8,128)(2,1)S(1)}, bf16[128,2048]{1,0:T(8,128)(2,1)S(1)}, u32[]{:S(2)}, u32[]{:S(2)}) collective-permute-start(bf16[128,2048]{1,0:T(8,128)(2,1)S(1)} %get-tuple-element.65), channel_id=1, source_target_pairs={{8,4},{12,8},{9,5},{13,9},{10,6},{14,10},{11,7},{15,11},{24,20},{2... | collective-permute-start | bytes 1572872 | tf_op jit(solution)/shard_map/ppermute | solution.py:264
  109.2 20.1 %collective-permute-start.22 = (bf16[128,2048]{1,0:T(8,128)(2,1)S(1)}, bf16[128,2048]{1,0:T(8,128)(2,1)S(1)}, u32[]{:S(2)}, u32[]{:S(2)}) collective-permute-start(bf16[128,2048]{1,0:T(8,128)(2,1)S(1)} %get-tuple-element.66), channel_id=1, source_target_pairs={{0,4},{4,8},{1,5},{5,9},{2,6},{6,10},{3,7},{7,11},{16,20},{20,24},... | collective-permute-start | bytes 1572872 | tf_op jit(solution)/shard_map/ppermute | solution.py:263
  118.2 32.8 %copy-start.10 = (bf16[128,2048]{1,0:T(8,128)(2,1)S(1)}, bf16[128,2048]{1,0:T(8,128)(2,1)}, u32[]{:S(2)}) copy-start(bf16[128,2048]{1,0:T(8,128)(2,1)} %get-tuple-element.54) | copy-start | bytes 1572868
  118.2 17.7 %collective-permute-start.19 = (bf16[128,2048]{1,0:T(8,128)(2,1)S(1)}, bf16[128,2048]{1,0:T(8,128)(2,1)S(1)}, u32[]{:S(2)}, u32[]{:S(2)}) collective-permute-start(bf16[128,2048]{1,0:T(8,128)(2,1)S(1)} %add_convert_fusion.4), channel_id=1, source_target_pairs={{4,0},{8,4},{12,8},{5,1},{9,5},{13,9},{6,2},{10,6},{14,10},{7,3},{... | collective-permute-start | bytes 1572872 | tf_op jit(solution)/shard_map/ppermute | solution.py:264
  119.8 20.8 %collective-permute-start.18 = (bf16[128,2048]{1,0:T(8,128)(2,1)S(1)}, bf16[128,2048]{1,0:T(8,128)(2,1)S(1)}, u32[]{:S(2)}, u32[]{:S(2)}) collective-permute-start(bf16[128,2048]{1,0:T(8,128)(2,1)S(1)} %add_convert_fusion.5), channel_id=1, source_target_pairs={{0,4},{4,8},{8,12},{1,5},{5,9},{9,13},{2,6},{6,10},{10,14},{3,7},{... | collective-permute-start | bytes 1572872 | tf_op jit(solution)/shard_map/ppermute | solution.py:263
  129.4 15.1 %collective-permute-start.25 = (bf16[128,2048]{1,0:T(8,128)(2,1)S(1)}, bf16[128,2048]{1,0:T(8,128)(2,1)S(1)}, u32[]{:S(2)}, u32[]{:S(2)}) collective-permute-start(bf16[128,2048]{1,0:T(8,128)(2,1)S(1)} %add_convert_fusion.1), channel_id=1, source_target_pairs={{4,0},{8,4},{12,8},{5,1},{9,5},{13,9},{6,2},{10,6},{14,10},{7,3},{... | collective-permute-start | bytes 1572872 | tf_op jit(solution)/shard_map/ppermute | solution.py:264
  130.9 20.1 %collective-permute-start.24 = (bf16[128,2048]{1,0:T(8,128)(2,1)S(1)}, bf16[128,2048]{1,0:T(8,128)(2,1)S(1)}, u32[]{:S(2)}, u32[]{:S(2)}) collective-permute-start(bf16[128,2048]{1,0:T(8,128)(2,1)S(1)} %add_convert_fusion.2), channel_id=1, source_target_pairs={{0,4},{4,8},{8,12},{1,5},{5,9},{9,13},{2,6},{6,10},{10,14},{3,7},{... | collective-permute-start | bytes 1572872 | tf_op jit(solution)/shard_map/ppermute | solution.py:263
  (7 other events, 54.6 us)
